TPU v7x, 128 devices: a whole 4x4x4 slice. The times are simulated.
128 devices in a mesh: loop: 8 (over x_lo, y), grp: 16 (over z, x_hi, core).
Axes of the slice: x: 4 (x_hi: 2, x_lo: 2; x = x_hi * 2 + x_lo), y: 4, z: 4, core: 2. Of those that a mesh axis runs over, the one named last changes fastest.
Arguments:
- queries: bfloat16 [16384, 4096], P(('loop', 'grp')), as said below
- passages: bfloat16 [8192, 4096], P(('loop', 'grp')), as said below
- pool: bfloat16 [32768, 4096], P(('loop', 'grp')), as said below
- query_count: int32 [8, 16], P('loop', 'grp'), may hold values from 32 to 128, as said below
- positive: int32 [16384], P(('loop', 'grp')), may hold values from 0 to 511
- neg_owner: int32 [16384, 7], P(('loop', 'grp')), may hold values from 0 to 15, as said below
- neg_row: int32 [16384, 7], P(('loop', 'grp')), may hold values from 0 to 255
Outputs:
- loss: float32 [16384], P(('loop', 'grp'))
- grad_query: float32 [16384, 4096], P(('loop', 'grp'))
- grad_passage: float32 [8192, 4096], P(('loop', 'grp'))
- grad_pool: float32 [32768, 4096], P(('loop', 'grp'))
Inputs may be any that keep to these rules, and one draw needn't show every extreme that they name: `queries`: every entry lies in -0.25 to 0.25. `passages`: every entry lies in -0.25 to 0.25. `pool`: every entry lies in -0.25 to 0.25. `query_count`: some device has all 128 slots live. `neg_owner`: among the 896 entries of one device, at most 70 name one owner; for every loop index one owner is named exactly 70 times by every device of that loop index. Entries of slots that are not live are present too.
All inputs are finite; a program needn't handle non-finite values.
Results may differ from a plain program's by a relative error of at most 0.02.
Values may be sent and summed in bfloat16 or wider, within the bound.
No kernel may reach another device: no remote copies, remote signals or barrier semaphores. Data moves between devices by JAX's collectives and lax.ppermute only.
A program may use at most 192 MiB of HBM per device.

v0:
```python
import jax
import jax.numpy as jnp
from jax import lax
from jax.sharding import PartitionSpec as P

inv_temp = 50.0
eps = 1e-06


def passed_along(shard, axis, by):
    peers = lax.axis_size(axis)
    return lax.ppermute(shard, axis, [(i, (i + by) % peers) for i in range(peers)])


def unit_rows(rows):
    scale = lax.rsqrt(jnp.sum(rows * rows, axis=-1, keepdims=True) + eps)
    return (rows * scale, scale)


def unit_back(grad, unit, scale):
    return (grad - unit * jnp.sum(unit * grad, axis=-1, keepdims=True)) * scale


def cross(left, right):
    return lax.dot_general(
        left, right, (((1,), (1,)), ((), ())), preferred_element_type=jnp.float32
    )


def gather_back(coef, rows):
    return lax.dot_general(coef, rows, (((0,), (0,)), ((), ())), preferred_element_type=jnp.float32)


def local(queries, passages, pool, query_count, positive, neg_owner, neg_row):
    n_query, width = queries.shape
    n_pass = passages.shape[0]
    hard_count = neg_owner.shape[1]
    groups = lax.axis_size("grp")
    loops = lax.axis_size("loop")
    blocks_total = loops * n_pass
    cap = 5 * n_query * hard_count // (4 * groups)
    q_unit, q_scale = unit_rows(queries.astype(jnp.float32))
    p_unit, p_scale = unit_rows(passages.astype(jnp.float32))
    n_unit, n_scale = unit_rows(pool.astype(jnp.float32))
    q_hat = q_unit.astype(jnp.bfloat16)
    p_hat = p_unit.astype(jnp.bfloat16)
    n_hat = n_unit.astype(jnp.bfloat16)
    valid = (lax.iota(jnp.int32, n_query) < query_count.reshape(())).astype(jnp.float32)[:, None]
    owners = neg_owner.reshape(-1)
    wanted_rows = neg_row.reshape(-1)
    owner_hits = (owners[:, None] == lax.iota(jnp.int32, groups)[None, :]).astype(jnp.int32)
    rank = jnp.sum((jnp.cumsum(owner_hits, axis=0) - owner_hits) * owner_hits, axis=1)
    place = owners * cap + rank
    send_ids = jnp.zeros((groups * cap,), jnp.int32).at[place].set(wanted_rows).reshape(groups, cap)
    requested = lax.all_to_all(send_ids, "grp", split_axis=0, concat_axis=0, tiled=True)
    picked = n_hat[requested]
    reply = lax.all_to_all(picked, "grp", split_axis=0, concat_axis=0, tiled=True)
    negs = reply.reshape(groups * cap, width)[place].reshape(n_query, hard_count, width)
    hard = jnp.einsum("qd,qkd->qk", q_hat, negs, preferred_element_type=jnp.float32) * inv_temp
    scores = cross(q_hat, lax.all_gather(p_hat, "loop", axis=0, tiled=True)) * inv_temp
    weights_in = jnp.exp(scores - inv_temp)
    weights_hard = jnp.exp(hard - inv_temp)
    total = jnp.sum(weights_in, axis=1) + jnp.sum(weights_hard, axis=1)
    chosen = jnp.take_along_axis(scores, positive[:, None], axis=1)[:, 0]
    loss = valid[:, 0] * (jnp.log(total) + inv_temp - chosen)
    target = (positive[:, None] == lax.iota(jnp.int32, blocks_total)[None, :]).astype(jnp.float32)
    coef_in = (valid * (weights_in / total[:, None] - target)).astype(jnp.bfloat16)
    coef_hard = (valid * weights_hard / total[:, None]).astype(jnp.bfloat16)
    hard_part = jnp.einsum("qk,qkd->qd", coef_hard, negs, preferred_element_type=jnp.float32)
    neg_grad = (
        inv_temp * coef_hard.astype(jnp.float32)[:, :, None] * q_hat.astype(jnp.float32)[:, None, :]
    ).astype(jnp.bfloat16)
    position = lax.axis_index("loop")

    def turn(step, carry):
        block, block_sum, query_sum = carry
        anchor = (position - step) % loops
        cols = lax.dynamic_slice_in_dim(coef_in, anchor * n_pass, n_pass, 1)
        query_sum = query_sum + jnp.dot(cols, block, preferred_element_type=jnp.float32)
        block_sum = block_sum + gather_back(cols, q_hat)
        block, block_sum = (
            passed_along(block, "loop", 1),
            passed_along(block_sum.astype(jnp.bfloat16), "loop", 1).astype(block_sum.dtype),
        )
        return (block, block_sum, query_sum)

    start_carry = (
        p_hat,
        jnp.zeros((n_pass, width), jnp.float32),
        jnp.zeros((n_query, width), jnp.float32),
    )
    unused, pass_part, in_part = lax.fori_loop(0, loops, turn, start_carry)
    grad_query = unit_back(inv_temp * (in_part + hard_part), q_unit, q_scale)
    grad_passage = unit_back(inv_temp * pass_part, p_unit, p_scale)
    outgoing = (
        jnp.zeros((groups * cap, width), jnp.bfloat16).at[place].set(neg_grad.reshape(-1, width))
    )
    incoming = lax.all_to_all(
        outgoing.reshape(groups, cap, width), "grp", split_axis=0, concat_axis=0, tiled=True
    )
    pool_sum = jax.ops.segment_sum(
        incoming.reshape(-1, width).astype(jnp.float32),
        requested.reshape(-1),
        num_segments=pool.shape[0],
    )
    grad_pool = unit_back(pool_sum, n_unit, n_scale)
    return (loss, grad_query, grad_passage, grad_pool)


def solution(mesh):
    return jax.shard_map(
        local,
        mesh=mesh,
        in_specs=(
            P(("loop", "grp"), None),
            P(("loop", "grp"), None),
            P(("loop", "grp"), None),
            P("loop", "grp"),
            P(("loop", "grp")),
            P(("loop", "grp"), None),
            P(("loop", "grp"), None),
        ),
        out_specs=(
            P(("loop", "grp")),
            P(("loop", "grp"), None),
            P(("loop", "grp"), None),
            P(("loop", "grp"), None),
        ),
        check_vma=False,
    )
```

profile of v0, /device:TPU:0, one launch (start us, length us, event | category | flops | bytes accessed | tf_op | source)
XLA Modules:
  0.0 697.3 jit_solution(12775351238228727009)
XLA Ops:
  9.4 2.0 reduce-window.6
  12.8 5.3 scatter_custom_fusion
  18.8 8.0 %all-to-all-start = ((s32[16,1,70]{2,1,0:T(1,128)}), s32[16,1,70]{2,1,0:T(1,128)S(1)}, u32[]{:S(2)}, u32[]{:S(2)}) async-start(s32[16,1,70]{2,1,0:T(1,128)} %all_to_all.14), calls=%async_computation | async-start | bytes 16384 | tf_op jit(solution)/shard_map/all_to_all | solution.py:55
  28.0 2.1 fusion.13
  30.1 2.2 fusion.8
  32.3 1.9 all-to-all-done
  34.4 7.9 %gather_fusion = bf16[1120,4096]{1,0:T(8,128)(2,1)} fusion(bf16[256,4096]{1,0:T(8,128)(2,1)S(1)} %fusion.8, s32[2048]{0:T(1024)S(1)} %pad_clamp_fusion), kind=kCustom, calls=%fused_computation | custom fusion | bytes 18354560 | tf_op jit(solution)/shard_map/gather | solution.py:56
  42.3 8.3 %reshape.175 = bf16[16,70,4096]{2,1,0:T(8,128)(2,1)} reshape(bf16[1120,4096]{1,0:T(8,128)(2,1)} %gather_fusion) | data formatting | bytes 18350080 | tf_op jit(solution)/shard_map/gather | solution.py:56
  50.6 5.5 all-to-all-start.1
  58.6 7.8 %mul.208 = f32[128,7,4096]{2,1,0:T(8,128)} broadcast(bf16[128,4096]{1,0:T(8,128)(2,1)S(1)} %fusion.16), dimensions={0,2} | broadcast | bytes 15728640 | tf_op jit(solution)/shard_map/mul | solution.py:71
  66.4 13.6 %mul.209 = f32[896,4096]{1,0:T(8,128)} reshape(f32[128,7,4096]{2,1,0:T(8,128)} %mul.208) | data formatting | bytes 29360128 | tf_op jit(solution)/shard_map/mul | solution.py:71
  81.3 71.0 %all-gather.2.cloned.1.call-done = bf16[512,4096]{1,0:T(8,128)(2,1)} async-done(((bf16[64,4096]{1,0:T(8,128)(2,1)}), bf16[512,4096]{1,0:T(8,128)(2,1)}) %all-gather.2.cloned.1.call-update) | async-done | bytes 4194320 | tf_op jit(solution)/shard_map/all_gather | solution.py:60
  152.3 3.8 fusion.33
  157.6 45.7 %all-to-all-done.1 = bf16[16,70,4096]{2,1,0:T(8,128)(2,1)} async-done(((bf16[16,70,4096]{2,1,0:T(8,128)(2,1)}), bf16[16,70,4096]{2,1,0:T(8,128)(2,1)}, u32[]{:S(2)}, u32[]{:S(2)}) %all-to-all-start.1) | async-done | bytes 9175072 | tf_op jit(solution)/shard_map/all_to_all | solution.py:57
  203.4 8.4 %reshape.169 = bf16[1120,4096]{1,0:T(8,128)(2,1)} reshape(bf16[16,70,4096]{2,1,0:T(8,128)(2,1)} %all-to-all-done.1) | data formatting | bytes 18350080 | tf_op jit(solution)/shard_map/reshape | solution.py:58
  211.8 19.8 %gather_fusion.1 = bf16[896,4096]{1,0:T(8,128)(2,1)} fusion(bf16[1120,4096]{1,0:T(8,128)(2,1)} %reshape.169, s32[1024]{0:T(1024)S(1)} %pad_clamp_fusion.1), kind=kCustom, calls=%fused_computation.1 | custom fusion | bytes 14683648 | tf_op jit(solution)/shard_map/gather | solution.py:58
  231.6 9.7 %reshape.170 = bf16[128,7,4096]{2,1,0:T(8,128)(2,1)} reshape(bf16[896,4096]{1,0:T(8,128)(2,1)} %gather_fusion.1) | data formatting | bytes 14680064 | tf_op jit(solution)/shard_map/reshape | solution.py:58
  241.2 8.8 %fusion.22 = f32[128,1,7]{2,1,0:T(1,128)S(1)} fusion(bf16[128,7,4096]{2,1,0:T(8,128)(2,1)} %reshape.170, bf16[128,4096,1]{1,0,2:T(8,128)(2,1)S(1)} %copy-done.7), kind=kOutput, calls=%fused_computation.36 | convolution fusion | flops 7340032 | bytes 8392192 | tf_op jit(solution)/shard_map/qd,qkd->qk/dot_general | solution.py:59
  251.1 6.2 mul.207
  257.3 22.8 %scatter_custom_fusion.1 = bf16[1120,4096]{1,0:T(8,128)(2,1)} fusion(s32[896]{0:T(1024)S(1)} %fusion.42, f32[896,4096]{1,0:T(8,128)} %mul.207, f32[896,4096]{1,0:T(8,128)} %mul.209, bf16[]{:T(256)} %constant.120.clone.1), kind=kCustom, calls=%fused_computation.14 | custom fusion | flops 7340032 | bytes 38535168 | tf_op jit(solution)/shard_map/scatter | solution.py:96
  280.1 8.4 %reshape.172 = bf16[16,70,4096]{2,1,0:T(8,128)(2,1)} reshape(bf16[1120,4096]{1,0:T(8,128)(2,1)} %scatter_custom_fusion.1) | data formatting | bytes 18350080 | tf_op jit(solution)/shard_map/reshape | solution.py:99
  288.6 4.8 all-to-all-start.2
  296.3 315.4 %while.20 = (s32[]{:T(128)}, bf16[64,4096]{1,0:T(8,128)(2,1)}, f32[64,4096]{1,0:T(8,128)}, f32[128,4096]{1,0:T(8,128)S(1)}, s32[]{:T(128)}, /*index=5*/bf16[128,...) while((s32[]{:T(128)}, bf16[64,4096]{1,0:T(8,128)(2,1)}, ...), condition=%wide.region_10.11_spmd.clone, body=%wide.region_9.10_spmd.clone.sunk | while | flops 136314896 | bytes 14221703 | solution.py:92
  301.3 110.5 %collective-permute-done.1 = bf16[64,4096]{1,0:T(8,128)(2,1)} collective-permute-done((bf16[64,4096]{1,0:T(8,128)(2,1)}, bf16[64,4096]{1,0:T(8,128)(2,1)}, u32[]{:S(2)}, u32[]{:S(2)}) %collective-permute-start.1) | collective-permute-done | bytes 524320 | tf_op jit(solution)/shard_map/while/body/eval_jaxpr/ppermute | solution.py:12
  411.8 2.1 convert_element_type.166
  413.9 8.9 %collective-permute-done = bf16[64,4096]{1,0:T(8,128)(2,1)} collective-permute-done((bf16[64,4096]{1,0:T(8,128)(2,1)}, bf16[64,4096]{1,0:T(8,128)(2,1)}, u32[]{:S(2)}, u32[]{:S(2)}) %collective-permute-start) | collective-permute-done | bytes 524320 | tf_op jit(solution)/shard_map/while/body/eval_jaxpr/ppermute | solution.py:12
  422.7 2.4 fusion.64
  425.1 1.9 copy.40
  428.9 13.5 %collective-permute-done.1 = bf16[64,4096]{1,0:T(8,128)(2,1)} collective-permute-done((bf16[64,4096]{1,0:T(8,128)(2,1)}, bf16[64,4096]{1,0:T(8,128)(2,1)}, u32[]{:S(2)}, u32[]{:S(2)}) %collective-permute-start.1) | collective-permute-done | bytes 524320 | tf_op jit(solution)/shard_map/while/body/eval_jaxpr/ppermute | solution.py:12
  442.4 2.1 convert_element_type.166
  444.5 8.0 %collective-permute-done = bf16[64,4096]{1,0:T(8,128)(2,1)} collective-permute-done((bf16[64,4096]{1,0:T(8,128)(2,1)}, bf16[64,4096]{1,0:T(8,128)(2,1)}, u32[]{:S(2)}, u32[]{:S(2)}) %collective-permute-start) | collective-permute-done | bytes 524320 | tf_op jit(solution)/shard_map/while/body/eval_jaxpr/ppermute | solution.py:12
  452.4 2.4 fusion.64
  454.9 1.9 copy.40
  458.6 13.6 %collective-permute-done.1 = bf16[64,4096]{1,0:T(8,128)(2,1)} collective-permute-done((bf16[64,4096]{1,0:T(8,128)(2,1)}, bf16[64,4096]{1,0:T(8,128)(2,1)}, u32[]{:S(2)}, u32[]{:S(2)}) %collective-permute-start.1) | collective-permute-done | bytes 524320 | tf_op jit(solution)/shard_map/while/body/eval_jaxpr/ppermute | solution.py:12
  472.2 2.1 convert_element_type.166
  474.2 7.1 %collective-permute-done = bf16[64,4096]{1,0:T(8,128)(2,1)} collective-permute-done((bf16[64,4096]{1,0:T(8,128)(2,1)}, bf16[64,4096]{1,0:T(8,128)(2,1)}, u32[]{:S(2)}, u32[]{:S(2)}) %collective-permute-start) | collective-permute-done | bytes 524320 | tf_op jit(solution)/shard_map/while/body/eval_jaxpr/ppermute | solution.py:12
  481.3 2.4 fusion.64
  483.7 1.9 copy.40
  487.5 13.6 %collective-permute-done.1 = bf16[64,4096]{1,0:T(8,128)(2,1)} collective-permute-done((bf16[64,4096]{1,0:T(8,128)(2,1)}, bf16[64,4096]{1,0:T(8,128)(2,1)}, u32[]{:S(2)}, u32[]{:S(2)}) %collective-permute-start.1) | collective-permute-done | bytes 524320 | tf_op jit(solution)/shard_map/while/body/eval_jaxpr/ppermute | solution.py:12
  501.0 2.1 convert_element_type.166
  503.1 6.1 collective-permute-done
  509.2 2.4 fusion.64
  511.7 1.9 copy.40
  515.4 13.6 %collective-permute-done.1 = bf16[64,4096]{1,0:T(8,128)(2,1)} collective-permute-done((bf16[64,4096]{1,0:T(8,128)(2,1)}, bf16[64,4096]{1,0:T(8,128)(2,1)}, u32[]{:S(2)}, u32[]{:S(2)}) %collective-permute-start.1) | collective-permute-done | bytes 524320 | tf_op jit(solution)/shard_map/while/body/eval_jaxpr/ppermute | solution.py:12
  529.0 2.1 convert_element_type.166
  531.0 5.2 collective-permute-done
  536.2 2.4 fusion.64
  542.4 13.6 %collective-permute-done.1 = bf16[64,4096]{1,0:T(8,128)(2,1)} collective-permute-done((bf16[64,4096]{1,0:T(8,128)(2,1)}, bf16[64,4096]{1,0:T(8,128)(2,1)}, u32[]{:S(2)}, u32[]{:S(2)}) %collective-permute-start.1) | collective-permute-done | bytes 524320 | tf_op jit(solution)/shard_map/while/body/eval_jaxpr/ppermute | solution.py:12
  556.0 2.1 convert_element_type.166
  558.1 4.3 collective-permute-done
  562.3 2.4 fusion.64
  568.5 13.4 %collective-permute-done.1 = bf16[64,4096]{1,0:T(8,128)(2,1)} collective-permute-done((bf16[64,4096]{1,0:T(8,128)(2,1)}, bf16[64,4096]{1,0:T(8,128)(2,1)}, u32[]{:S(2)}, u32[]{:S(2)}) %collective-permute-start.1) | collective-permute-done | bytes 524320 | tf_op jit(solution)/shard_map/while/body/eval_jaxpr/ppermute | solution.py:12
  581.9 2.1 convert_element_type.166
  584.0 3.5 collective-permute-done
  587.5 2.4 fusion.64
  593.7 12.5 %collective-permute-done.1 = bf16[64,4096]{1,0:T(8,128)(2,1)} collective-permute-done((bf16[64,4096]{1,0:T(8,128)(2,1)}, bf16[64,4096]{1,0:T(8,128)(2,1)}, u32[]{:S(2)}, u32[]{:S(2)}) %collective-permute-start.1) | collective-permute-done | bytes 524320 | tf_op jit(solution)/shard_map/while/body/eval_jaxpr/ppermute | solution.py:12
  606.1 2.1 convert_element_type.166
  608.2 3.5 collective-permute-done
  613.5 5.8 fusion.46
  622.1 3.6 fusion.19
  625.6 17.2 %reshape.218 = f32[1120,4096]{1,0:T(8,128)} reshape(bf16[16,70,4096]{2,1,0:T(8,128)(2,1)} %all-to-all-done.2) | data formatting | bytes 27525120 | tf_op jit(solution)/shard_map/convert_element_type | solution.py:102
  642.8 40.9 %scatter_custom_fusion.2 = f32[256,4096]{1,0:T(8,128)} fusion(s32[1120]{0:T(1024)S(1)} %reshape.216, f32[1120,4096]{1,0:T(8,128)} %reshape.218, f32[]{:T(128)} %constant.107.clone.1), kind=kCustom, calls=%fused_computation.38 | custom fusion | flops 4587520 | bytes 4194816 | tf_op jit(solution)/shard_map/scatter-add | solution.py:101
  683.7 3.0 fusion.10
  687.2 3.1 fusion.12
  (108 shorter events, 42.4 us)
Async XLA Ops:
  18.8 15.4 %all-to-all-start = ((s32[16,1,70]{2,1,0:T(1,128)}), s32[16,1,70]{2,1,0:T(1,128)S(1)}, u32[]{:S(2)}, u32[]{:S(2)}) async-start(s32[16,1,70]{2,1,0:T(1,128)} %all_to_all.14), calls=%async_computation | async-start | bytes 16384 | tf_op jit(solution)/shard_map/all_to_all | solution.py:55
  32.3 24.0 %copy-start.9 = (f32[64]{0:T(128)}, f32[64]{0:T(128)S(1)}, u32[]{:S(2)}) copy-start(f32[64]{0:T(128)S(1)} %add_rsqrt_fusion.1) | copy-start | bytes 772
  50.6 5.7 copy-start.5
  50.6 7.4 %copy-start.3 = (bf16[128,4096]{1,0:T(8,128)(2,1)S(1)}, bf16[128,4096]{1,0:T(8,128)(2,1)}, u32[]{:S(2)}) copy-start(bf16[128,4096]{1,0:T(8,128)(2,1)} %param.9) | copy-start | bytes 3145732
  50.6 152.7 %all-to-all-start.1 = ((bf16[16,70,4096]{2,1,0:T(8,128)(2,1)}), bf16[16,70,4096]{2,1,0:T(8,128)(2,1)}, u32[]{:S(2)}, u32[]{:S(2)}) async-start(bf16[16,70,4096]{2,1,0:T(8,128)(2,1)} %reshape.175), calls=%async_computation.1 | async-start | bytes 18874368 | tf_op jit(solution)/shard_map/all_to_all | solution.py:57
  56.1 96.2 %all-gather.2.cloned.1.call-start = ((), (), s32[]{:S(2)}) async-start(), calls=%async_computation.3 | async-start | bytes 4718592 | tf_op jit(solution)/shard_map/all_gather | solution.py:60
  66.4 13.6 %copy-start.12 = (s32[128]{0:T(128)S(1)}, s32[128]{0:T(128)}, u32[]{:S(2)}) copy-start(s32[128]{0:T(128)} %param.13) | copy-start | bytes 1540
  80.0 170.8 %copy-start.13 = (f32[128]{0:T(128)}, f32[128]{0:T(128)S(1)}, u32[]{:S(2)}) copy-start(f32[128]{0:T(128)S(1)} %compare_convert_fusion) | copy-start | bytes 1540
  231.6 9.7 %copy-start.7 = (bf16[128,4096,1]{1,0,2:T(8,128)(2,1)S(1)}, bf16[128,4096,1]{1,0,2:T(8,128)(2,1)}, u32[]{:S(2)}) copy-start(bf16[128,4096,1]{1,0,2:T(8,128)(2,1)} %fusion.54) | copy-start | bytes 3145732
  250.7 6.6 copy-start.11
  288.6 337.1 %all-to-all-start.2 = ((bf16[16,70,4096]{2,1,0:T(8,128)(2,1)}), bf16[16,70,4096]{2,1,0:T(8,128)(2,1)}, u32[]{:S(2)}, u32[]{:S(2)}) async-start(bf16[16,70,4096]{2,1,0:T(8,128)(2,1)} %reshape.172), calls=%async_computation.2 | async-start | bytes 18874368 | tf_op jit(solution)/shard_map/all_to_all | solution.py:98
  296.3 315.5 %copy-start.10 = (f32[64]{0:T(128)S(1)}, f32[64]{0:T(128)}, u32[]{:S(2)}) copy-start(f32[64]{0:T(128)} %copy-done.9) | copy-start | bytes 772
  296.3 317.2 %copy-start.8 = (bf16[128,7,1]{1,2,0:T(2,128)(2,1)S(1)}, bf16[128,7,1]{1,2,0:T(2,128)(2,1)}, u32[]{:S(2)}) copy-start(bf16[128,7,1]{1,2,0:T(2,128)(2,1)} %copy.24) | copy-start | bytes 5380
  297.6 114.2 %collective-permute-start.1 = (bf16[64,4096]{1,0:T(8,128)(2,1)}, bf16[64,4096]{1,0:T(8,128)(2,1)}, u32[]{:S(2)}, u32[]{:S(2)}) collective-permute-start(bf16[64,4096]{1,0:T(8,128)(2,1)} %fusion.64), channel_id=1, source_target_pairs={{0,16},{16,32},{32,48},{48,64},{64,80},{80,96},{96,112},{112,0},{1... | collective-permute-start | bytes 1572872 | tf_op jit(solution)/shard_map/while/body/eval_jaxpr/ppermute | solution.py:12
  299.4 123.3 %collective-permute-start = (bf16[64,4096]{1,0:T(8,128)(2,1)}, bf16[64,4096]{1,0:T(8,128)(2,1)}, u32[]{:S(2)}, u32[]{:S(2)}) collective-permute-start(bf16[64,4096]{1,0:T(8,128)(2,1)} %copy.40), channel_id=1, source_target_pairs={{0,16},{16,32},{32,48},{48,64},{64,80},{80,96},{96,112},{112,0},{1... | collective-permute-start | bytes 1572872 | tf_op jit(solution)/shard_map/while/body/eval_jaxpr/ppermute | solution.py:12
  425.1 17.2 %collective-permute-start.1 = (bf16[64,4096]{1,0:T(8,128)(2,1)}, bf16[64,4096]{1,0:T(8,128)(2,1)}, u32[]{:S(2)}, u32[]{:S(2)}) collective-permute-start(bf16[64,4096]{1,0:T(8,128)(2,1)} %fusion.64), channel_id=1, source_target_pairs={{0,16},{16,32},{32,48},{48,64},{64,80},{80,96},{96,112},{112,0},{1... | collective-permute-start | bytes 1572872 | tf_op jit(solution)/shard_map/while/body/eval_jaxpr/ppermute | solution.py:12
  427.0 25.4 %collective-permute-start = (bf16[64,4096]{1,0:T(8,128)(2,1)}, bf16[64,4096]{1,0:T(8,128)(2,1)}, u32[]{:S(2)}, u32[]{:S(2)}) collective-permute-start(bf16[64,4096]{1,0:T(8,128)(2,1)} %copy.40), channel_id=1, source_target_pairs={{0,16},{16,32},{32,48},{48,64},{64,80},{80,96},{96,112},{112,0},{1... | collective-permute-start | bytes 1572872 | tf_op jit(solution)/shard_map/while/body/eval_jaxpr/ppermute | solution.py:12
  454.9 17.3 %collective-permute-start.1 = (bf16[64,4096]{1,0:T(8,128)(2,1)}, bf16[64,4096]{1,0:T(8,128)(2,1)}, u32[]{:S(2)}, u32[]{:S(2)}) collective-permute-start(bf16[64,4096]{1,0:T(8,128)(2,1)} %fusion.64), channel_id=1, source_target_pairs={{0,16},{16,32},{32,48},{48,64},{64,80},{80,96},{96,112},{112,0},{1... | collective-permute-start | bytes 1572872 | tf_op jit(solution)/shard_map/while/body/eval_jaxpr/ppermute | solution.py:12
  456.8 24.5 %collective-permute-start = (bf16[64,4096]{1,0:T(8,128)(2,1)}, bf16[64,4096]{1,0:T(8,128)(2,1)}, u32[]{:S(2)}, u32[]{:S(2)}) collective-permute-start(bf16[64,4096]{1,0:T(8,128)(2,1)} %copy.40), channel_id=1, source_target_pairs={{0,16},{16,32},{32,48},{48,64},{64,80},{80,96},{96,112},{112,0},{1... | collective-permute-start | bytes 1572872 | tf_op jit(solution)/shard_map/while/body/eval_jaxpr/ppermute | solution.py:12
  483.7 17.3 %collective-permute-start.1 = (bf16[64,4096]{1,0:T(8,128)(2,1)}, bf16[64,4096]{1,0:T(8,128)(2,1)}, u32[]{:S(2)}, u32[]{:S(2)}) collective-permute-start(bf16[64,4096]{1,0:T(8,128)(2,1)} %fusion.64), channel_id=1, source_target_pairs={{0,16},{16,32},{32,48},{48,64},{64,80},{80,96},{96,112},{112,0},{1... | collective-permute-start | bytes 1572872 | tf_op jit(solution)/shard_map/while/body/eval_jaxpr/ppermute | solution.py:12
  485.6 23.6 %collective-permute-start = (bf16[64,4096]{1,0:T(8,128)(2,1)}, bf16[64,4096]{1,0:T(8,128)(2,1)}, u32[]{:S(2)}, u32[]{:S(2)}) collective-permute-start(bf16[64,4096]{1,0:T(8,128)(2,1)} %copy.40), channel_id=1, source_target_pairs={{0,16},{16,32},{32,48},{48,64},{64,80},{80,96},{96,112},{112,0},{1... | collective-permute-start | bytes 1572872 | tf_op jit(solution)/shard_map/while/body/eval_jaxpr/ppermute | solution.py:12
  511.7 17.3 %collective-permute-start.1 = (bf16[64,4096]{1,0:T(8,128)(2,1)}, bf16[64,4096]{1,0:T(8,128)(2,1)}, u32[]{:S(2)}, u32[]{:S(2)}) collective-permute-start(bf16[64,4096]{1,0:T(8,128)(2,1)} %fusion.64), channel_id=1, source_target_pairs={{0,16},{16,32},{32,48},{48,64},{64,80},{80,96},{96,112},{112,0},{1... | collective-permute-start | bytes 1572872 | tf_op jit(solution)/shard_map/while/body/eval_jaxpr/ppermute | solution.py:12
  513.5 22.7 %collective-permute-start = (bf16[64,4096]{1,0:T(8,128)(2,1)}, bf16[64,4096]{1,0:T(8,128)(2,1)}, u32[]{:S(2)}, u32[]{:S(2)}) collective-permute-start(bf16[64,4096]{1,0:T(8,128)(2,1)} %copy.40), channel_id=1, source_target_pairs={{0,16},{16,32},{32,48},{48,64},{64,80},{80,96},{96,112},{112,0},{1... | collective-permute-start | bytes 1572872 | tf_op jit(solution)/shard_map/while/body/eval_jaxpr/ppermute | solution.py:12
  538.7 17.3 %collective-permute-start.1 = (bf16[64,4096]{1,0:T(8,128)(2,1)}, bf16[64,4096]{1,0:T(8,128)(2,1)}, u32[]{:S(2)}, u32[]{:S(2)}) collective-permute-start(bf16[64,4096]{1,0:T(8,128)(2,1)} %fusion.64), channel_id=1, source_target_pairs={{0,16},{16,32},{32,48},{48,64},{64,80},{80,96},{96,112},{112,0},{1... | collective-permute-start | bytes 1572872 | tf_op jit(solution)/shard_map/while/body/eval_jaxpr/ppermute | solution.py:12
  540.6 21.8 %collective-permute-start = (bf16[64,4096]{1,0:T(8,128)(2,1)}, bf16[64,4096]{1,0:T(8,128)(2,1)}, u32[]{:S(2)}, u32[]{:S(2)}) collective-permute-start(bf16[64,4096]{1,0:T(8,128)(2,1)} %copy.40), channel_id=1, source_target_pairs={{0,16},{16,32},{32,48},{48,64},{64,80},{80,96},{96,112},{112,0},{1... | collective-permute-start | bytes 1572872 | tf_op jit(solution)/shard_map/while/body/eval_jaxpr/ppermute | solution.py:12
  564.8 17.1 %collective-permute-start.1 = (bf16[64,4096]{1,0:T(8,128)(2,1)}, bf16[64,4096]{1,0:T(8,128)(2,1)}, u32[]{:S(2)}, u32[]{:S(2)}) collective-permute-start(bf16[64,4096]{1,0:T(8,128)(2,1)} %fusion.64), channel_id=1, source_target_pairs={{0,16},{16,32},{32,48},{48,64},{64,80},{80,96},{96,112},{112,0},{1... | collective-permute-start | bytes 1572872 | tf_op jit(solution)/shard_map/while/body/eval_jaxpr/ppermute | solution.py:12
  566.6 20.9 %collective-permute-start = (bf16[64,4096]{1,0:T(8,128)(2,1)}, bf16[64,4096]{1,0:T(8,128)(2,1)}, u32[]{:S(2)}, u32[]{:S(2)}) collective-permute-start(bf16[64,4096]{1,0:T(8,128)(2,1)} %copy.40), channel_id=1, source_target_pairs={{0,16},{16,32},{32,48},{48,64},{64,80},{80,96},{96,112},{112,0},{1... | collective-permute-start | bytes 1572872 | tf_op jit(solution)/shard_map/while/body/eval_jaxpr/ppermute | solution.py:12
  589.9 16.2 %collective-permute-start.1 = (bf16[64,4096]{1,0:T(8,128)(2,1)}, bf16[64,4096]{1,0:T(8,128)(2,1)}, u32[]{:S(2)}, u32[]{:S(2)}) collective-permute-start(bf16[64,4096]{1,0:T(8,128)(2,1)} %fusion.64), channel_id=1, source_target_pairs={{0,16},{16,32},{32,48},{48,64},{64,80},{80,96},{96,112},{112,0},{1... | collective-permute-start | bytes 1572872 | tf_op jit(solution)/shard_map/while/body/eval_jaxpr/ppermute | solution.py:12
  591.8 19.9 %collective-permute-start = (bf16[64,4096]{1,0:T(8,128)(2,1)}, bf16[64,4096]{1,0:T(8,128)(2,1)}, u32[]{:S(2)}, u32[]{:S(2)}) collective-permute-start(bf16[64,4096]{1,0:T(8,128)(2,1)} %copy.40), channel_id=1, source_target_pairs={{0,16},{16,32},{32,48},{48,64},{64,80},{80,96},{96,112},{112,0},{1... | collective-permute-start | bytes 1572872 | tf_op jit(solution)/shard_map/while/body/eval_jaxpr/ppermute | solution.py:12
  613.5 5.8 copy-start.4
  619.3 1.5 copy-start
  619.3 1.5 copy-start.6
  642.8 40.9 %copy-start.2 = (bf16[256,4096]{1,0:T(8,128)(2,1)S(1)}, bf16[256,4096]{1,0:T(8,128)(2,1)}, u32[]{:S(2)}) copy-start(bf16[256,4096]{1,0:T(8,128)(2,1)} %param.11) | copy-start | bytes 6291460
  683.7 3.4 copy-start.1
Sparse Core Ops, SparseCore 0:
  58.6 93.6 all-gather.1
where the time goes:
time: 705 us; the launch traced here: 697 us
  waiting for transfers between devices  369 us (52%)
  local copies, waits for them, and re-layouts  135 us (19%)
  other arithmetic  108 us (15%)
  matrix products  51.4 us (7%)
  starting transfers between devices  18.5 us (3%)
  between operations  15.2 us (2%)
    ppermute x16, waiting for transfers between devices, passed_along(): lax.ppermute(shard, axis, [(i, (i + by) % peers) for i in range(peers)])  251 us
    all_gather x1, waiting for transfers between devices, local(): lax.all_gather(p_hat, 'loop', axis=0, tiled=True)  71 us
    all_to_all x1, waiting for transfers between devices, local(): lax.all_to_all(picked, 'grp', split_axis=0, concat_axis=0, tiled=True)  45.7 us
    scatter-add x1, other arithmetic, local(): jax.ops.segment_sum(incoming.reshape(-1, width).astype(jnp.float32), requ...  40.9 us
    mul x5, local copies, waits for them, and re-layouts, local(): inv_temp * coef_hard.astype(jnp.float32)[:, :, None]  28 us
    scatter x1, other arithmetic, local(): jnp.zeros((groups * cap, width), jnp.bfloat16).at[place]  22.8 us
    gather x1, local copies, waits for them, and re-layouts, local(): reply.reshape(groups * cap, width)[place]  19.8 us
    dot_general x8, matrix products, gather_back(): lax.dot_general(coef, rows, (((0,), (0,)), ((), ())), preferred_element_t...  18.3 us
  transfers between devices with their start and end apart: 20, of which 19 were waited for; matrix products, arithmetic and copies ran while one was open for 17% of the time, Pallas kernels for 0%

commit v1 on v0

v1 whole, which is shorter than its diff:
```python
import functools

import jax
import jax.numpy as jnp
from jax import lax
from jax.experimental import pallas as pl
from jax.experimental.pallas import tpu as pltpu
from jax.sharding import PartitionSpec as P

inv_temp = 50.0
eps = 1e-06
f32 = jnp.float32
bf16 = jnp.bfloat16
vmem_bytes = 56 << 20
step_rows = 64


def hop_z(x, by):
    return lax.ppermute(x, "grp", [(g, (g + 4 * by) % 16) for g in range(16)])


def hop_xh(x):
    return lax.ppermute(x, "grp", [(g, g ^ 2) for g in range(16)])


def hop_core(x):
    return lax.ppermute(x, "grp", [(g, g ^ 1) for g in range(16)])


def hop_xl(x):
    return lax.ppermute(x, "loop", [(l, l ^ 4) for l in range(8)])


def hop_y(x, by):
    return lax.ppermute(x, "loop", [(l, (l & 4) + (l + by) % 4) for l in range(8)])


def after(values, *first):
    got = lax.optimization_barrier((tuple(values), first))
    return got[0]


def dot_nt(a, b):
    return lax.dot_general(a, b, (((1,), (1,)), ((), ())), preferred_element_type=f32)


def dot_nn(a, b):
    return lax.dot_general(a, b, (((1,), (0,)), ((), ())), preferred_element_type=f32)


def lane_squares(block):
    wide = block.astype(f32)
    wide = wide * wide
    part = wide[:, :128]
    for at in range(128, wide.shape[1], 128):
        part = part + wide[:, at : at + 128]
    return part


def inverse_norm(part):
    return lax.rsqrt(jnp.sum(part, axis=1, keepdims=True) + eps)


def stacked(refs):
    parts = [r[...] for r in refs]
    return parts[0] if len(parts) == 1 else jnp.concatenate(parts, axis=0)


def cols_spec(x, chunk=2048):
    return pl.BlockSpec((x.shape[0], chunk), lambda k: (0, k))


def whole_spec(x):
    return pl.BlockSpec(x.shape, lambda k: (0,) * x.ndim)


def smem_spec():
    return pl.BlockSpec(memory_space=pltpu.SMEM)


def cost(flops, *arrays, early=False):
    moved = sum(a.size * a.dtype.itemsize for a in arrays)
    if not early:
        flops, moved = 1, 1
    return pl.CostEstimate(flops=flops, bytes_accessed=moved, transcendentals=0)


def params():
    return pltpu.CompilerParams(vmem_limit_bytes=vmem_bytes)


def shape_of(shape, dtype):
    return jax.ShapeDtypeStruct(shape, dtype)


message_rows = 144
sizes = (128, 128, 64, 64, 128) * 2


def q_specs(q_refs, chunk):
    return [
        pl.BlockSpec((size, chunk), lambda k: (0, k)) for size, q in zip(sizes, q_refs)
    ]


def hard_kernel(bases, infos, before, *rest):
    q_refs = rest[:10]
    n1, n2, e1, e2, row_sum, s1, s2, codes, acc1, acc2, sq1, sq2 = rest[10:]
    k = pl.program_id(0)

    @pl.when(k == 0)
    def _():
        for ref in (acc1, acc2, sq1, sq2):
            ref[...] = jnp.zeros_like(ref)

    q_all = stacked(q_refs)
    for n, acc, sq in ((n1[...], acc1, sq1), (n2[...], acc2, sq2)):
        acc[...] += dot_nt(n, q_all)
        sq[...] += lane_squares(n)

    @pl.when(k == pl.num_programs(0) - 1)
    def _():
        for slot in range(8):
            info = infos[slot].astype(f32)
            code = info[0:8, 0:128] * 256.0 + info[8:16, 0:128]
            q_scale = info[0:1, 128:256] + info[1:2, 128:256] + info[2:3, 128:256]
            codes[slot] = jnp.concatenate([code[0:7], q_scale], axis=0)
        sums = [before[0:1, :]] + [jnp.zeros((1, 128), f32) for _ in range(7)]
        for h, (acc, sq, e, s) in enumerate(((acc1, sq1, e1, s1), (acc2, sq2, e2, s2))):
            scale = inverse_norm(sq[...])
            s[...] = jnp.broadcast_to(scale, s.shape)
            rows = lax.broadcasted_iota(jnp.int32, (acc.shape[0], 128), 0).astype(f32) + bases[h]
            for slot in range(8):
                lanes = slice(slot * 128, slot * 128 + 128)
                score = acc[:, lanes] * (scale * inv_temp) * codes[slot, 7:8, :]
                hits = jnp.zeros(rows.shape, f32)
                for which in range(7):
                    hits += jnp.where(rows == codes[slot, which : which + 1, :], 1.0, 0.0)
                weight = hits * jnp.exp(score)
                e[:, lanes] = weight
                sums[slot] += jnp.sum(weight, axis=0, keepdims=True)
        for slot in range(8):
            row_sum[slot : slot + 1, :] = sums[slot]


def hard_scores(bases, infos, before, q_refs, n1, n2, chunk=1024):
    rows, width = n1.shape
    outs = (
        shape_of((rows, 1024), f32),
        shape_of((rows, 1024), f32),
        shape_of((8, 128), f32),
        shape_of((rows, 128), f32),
        shape_of((rows, 128), f32),
        shape_of((8, 8, 128), f32),
    )
    return pl.pallas_call(
        hard_kernel,
        grid=(width // chunk,),
        in_specs=[smem_spec(), whole_spec(infos), whole_spec(before)]
        + q_specs(q_refs, chunk)
        + [cols_spec(x, chunk) for x in (n1, *n2)],
        out_specs=[whole_spec(o) for o in outs],
        out_shape=outs,
        scratch_shapes=[pltpu.VMEM((rows, 1024), f32)] * 2 + [pltpu.VMEM((rows, 128), f32)] * 2,
        compiler_params=params(),
        cost_estimate=cost(4 * rows * 1024 * width, n1, *n2, *q_refs, *outs[:2]),
        name="hard_scores",
    )(bases, infos, before, *q_refs, n1, *n2)


def passage_rows(refs):
    pc, p1, p2, p2x, p3 = [r[...] for r in refs]
    near = [pc[:64], p1[:64], p2, p3[:64]]
    far = [pc[64:], p1[64:], p2x, p3[64:]]
    return jnp.concatenate(near + far, axis=0)


def hot(places, pos, block):
    rows = lax.broadcasted_iota(jnp.int32, (64, pos.shape[1]), 0).astype(f32)
    return jnp.where(rows + places[block] == pos, 1.0, 0.0)


def batch_kernel(places, about, *rest):
    p_refs = rest[:5]
    q_refs = rest[5:-5]
    e, stats, scales, acc, sq = rest[-5:]
    k = pl.program_id(0)

    @pl.when(k == 0)
    def _():
        acc[...] = jnp.zeros_like(acc)
        sq[...] = jnp.zeros_like(sq)

    p_all = passage_rows(p_refs)
    acc[...] += dot_nt(p_all, stacked(q_refs))
    sq[...] += lane_squares(p_all)

    @pl.when(k == pl.num_programs(0) - 1)
    def _():
        scale = inverse_norm(sq[...])
        scales[...] = jnp.broadcast_to(scale, scales.shape)
        score = acc[...] * (scale * inv_temp) * about[0:1, :]
        weight = jnp.exp(score)
        e[...] = weight
        chosen = jnp.zeros((1, 128), f32)
        for block in range(8):
            part = score[block * 64 : block * 64 + 64]
            chosen += jnp.sum(part * hot(places, about[1:2, :], block), axis=0, keepdims=True)
        stats[0:1, :] = jnp.sum(weight, axis=0, keepdims=True)
        stats[1:2, :] = chosen
        stats[2:8, :] = jnp.zeros((6, 128), f32)


def batch_scores(places, about, p_refs, q_refs):
    width = q_refs[0].shape[1]
    outs = (shape_of((512, 128), f32), shape_of((8, 128), f32), shape_of((512, 128), f32))
    return pl.pallas_call(
        batch_kernel,
        grid=(width // 2048,),
        in_specs=[smem_spec(), whole_spec(about)] + [cols_spec(x) for x in (*p_refs, *q_refs)],
        out_specs=[whole_spec(o) for o in outs],
        out_shape=outs,
        scratch_shapes=[pltpu.VMEM((512, 128), f32), pltpu.VMEM((512, 128), f32)],
        compiler_params=params(),
        cost_estimate=cost(2 * 512 * 128 * width, *q_refs, *p_refs, *outs),
        name="batch_scores",
    )(places, about, *p_refs, *q_refs)


def back_kernel(first, e1, e2, s1, s2, n1, n2, *rest):
    turned = rest[-1]

    @pl.when(pl.program_id(0) == 0)
    def _():
        rows = e1.shape[0]
        turned[:, :rows] = jnp.transpose(e1[...] * s1[:, 0:1]).astype(bf16)
        turned[:, rows:] = jnp.transpose(e2[...] * s2[:, 0:1]).astype(bf16)

    part = dot_nn(turned[...], stacked([n1, n2]))
    if first:
        rest[0][...] = part.astype(bf16)
    else:
        got, home, u1, u2, u3 = rest[:5]
        part = part + got[...].astype(f32)
        home[...] = part[:128]
        for at, ref in enumerate((u1, u2, u3)):
            ref[...] = part[128 + at * 128 : 256 + at * 128].astype(bf16)


def hard_back(half, e1, e2, s1, s2, n1, n2, got=None):
    rows, width = n1.shape
    first = got is None
    if first:
        outs = (shape_of((512, width), bf16),)
        extra = ()
    else:
        outs = (shape_of((128, width), f32),) + (shape_of((128, width), bf16),) * 3
        extra = (got,)
    e_spec = pl.BlockSpec((rows, 512), lambda k: (0, half))
    return pl.pallas_call(
        functools.partial(back_kernel, first),
        grid=(width // 2048,),
        in_specs=[e_spec, e_spec, whole_spec(s1), whole_spec(s2)]
        + [cols_spec(x) for x in (n1, *n2, *extra)],
        out_specs=[cols_spec(o) for o in outs],
        out_shape=outs,
        scratch_shapes=[pltpu.VMEM((512, 2 * rows), bf16)],
        compiler_params=params(),
        cost_estimate=cost(2 * 512 * 2 * rows * width, n1, *n2, e1, *outs),
        name="hard_back",
    )(e1, e2, s1, s2, n1, *n2, *extra)


def pool_kernel(e, fac, *rest):
    q_refs = rest[:10]
    out, coef = rest[10:]

    @pl.when(pl.program_id(0) == 0)
    def _():
        for slot in range(8):
            lanes = slice(slot * 128, slot * 128 + 128)
            coef[:, lanes] = (e[:, lanes] * fac[slot : slot + 1, :]).astype(bf16)

    out[...] = dot_nn(coef[...], stacked(q_refs)).astype(out.dtype)


def pool_part(e, fac, q_refs, dtype):
    rows = e.shape[0]
    width = q_refs[0].shape[1]
    out = shape_of((rows, width), dtype)
    return pl.pallas_call(
        pool_kernel,
        grid=(width // 2048,),
        in_specs=[whole_spec(e), whole_spec(fac)] + q_specs(q_refs, 2048),
        out_specs=cols_spec(out),
        out_shape=out,
        scratch_shapes=[pltpu.VMEM((rows, 1024), bf16)],
        compiler_params=params(),
        cost_estimate=cost(2 * rows * 1024 * width, e, out, *q_refs),
        name="pool_part",
    )(e, fac, *q_refs)


def query_kernel(places, about, e, scales, *rest):
    p_refs = rest[:5]
    out, turned = rest[5:]

    @pl.when(pl.program_id(0) == 0)
    def _():
        for block in range(8):
            rows = slice(block * 64, block * 64 + 64)
            coef = e[rows, :] * about[0:1, :] - about[1:2, :] * hot(places, about[2:3, :], block)
            turned[rows, :] = coef * scales[rows, 0:1]

    turn = jnp.transpose(turned[...]).astype(bf16)
    out[...] = dot_nn(turn, passage_rows(p_refs))


def query_part(places, about, e, scales, p_refs):
    width = p_refs[0].shape[1]
    out = shape_of((128, width), f32)
    return pl.pallas_call(
        query_kernel,
        grid=(width // 2048,),
        in_specs=[smem_spec(), whole_spec(about), whole_spec(e), whole_spec(scales)]
        + [cols_spec(p) for p in p_refs],
        out_specs=cols_spec(out),
        out_shape=out,
        scratch_shapes=[pltpu.VMEM((512, 128), f32)],
        compiler_params=params(),
        cost_estimate=cost(2 * 512 * 128 * width, out, *p_refs),
        name="query_part",
    )(places, about, e, scales, *p_refs)


def passage_kernel(places, about_a, about_b, e_a, e_b, q_a, q_b, q_c, home, d1, d2, d3, coef):
    @pl.when(pl.program_id(0) == 0)
    def _():
        for at, (about, e) in enumerate(((about_a, e_a), (about_b, e_b))):
            lanes = slice(at * 128, at * 128 + 128)
            for block in range(4):
                rows = slice(block * 64, block * 64 + 64)
                part = e[rows, :] * about[0:1, :] - about[1:2, :] * hot(places, about[2:3, :], block)
                coef[rows, lanes] = (part * about[3:4, :]).astype(bf16)

    part = dot_nn(coef[...], stacked([q_a, q_b, q_c]))
    home[...] = part[:64]
    for at, ref in enumerate((d1, d2, d3)):
        ref[...] = part[64 + at * 64 : 128 + at * 64].astype(bf16)


def passage_part(places, about_a, about_b, e_a, e_b, q_a, q_b):
    width = q_a.shape[1]
    outs = (shape_of((64, width), f32),) + (shape_of((64, width), bf16),) * 3
    near = pl.BlockSpec((256, 128), lambda k: (0, 0))
    return pl.pallas_call(
        passage_kernel,
        grid=(width // 2048,),
        in_specs=[smem_spec(), whole_spec(about_a), whole_spec(about_b), near, near]
        + [cols_spec(x) for x in (q_a, *q_b)],
        out_specs=[cols_spec(o) for o in outs],
        out_shape=outs,
        scratch_shapes=[pltpu.VMEM((256, 256), bf16)],
        compiler_params=params(),
        cost_estimate=cost(2 * 256 * 256 * width, q_a, *q_b, *outs),
        name="passage_part",
    )(places, about_a, about_b, e_a, e_b, q_a, *q_b)


def last_kernel(n_parts, has_fac, *refs):
    parts = refs[:n_parts]
    rest = list(refs[n_parts:])
    total = None
    for ref in parts:
        pieces = [ref[...]] if len(ref.shape) == 2 else [ref[i] for i in range(ref.shape[0])]
        for piece in pieces:
            piece = piece.astype(f32)
            total = piece if total is None else total + piece
    if has_fac:
        fac, plain = rest[0], rest[1]
        total = total * fac[:, 0:1] + plain[...]
        rest = rest[2:]
    raw, out = rest[0], rest[-1]
    rows = raw[...].astype(f32)
    scale = lax.rsqrt(jnp.sum(rows * rows, axis=1, keepdims=True) + eps)
    along = jnp.sum(rows * total, axis=1, keepdims=True) * (scale * scale)
    out[...] = (total - rows * along) * (scale * inv_temp)


def last_step(parts, raw, fac=None, plain=None, step=step_rows):
    width = raw.shape[1]
    rows = raw.shape[0]

    def spec(x):
        if len(x.shape) == 3:
            return pl.BlockSpec((x.shape[0], step, x.shape[2]), lambda i: (0, i, 0))
        return pl.BlockSpec((step, x.shape[1]), lambda i: (i, 0))

    extra = () if fac is None else (fac, plain)
    ins = (*parts, *extra, raw)
    out = shape_of(raw.shape, f32)
    return pl.pallas_call(
        functools.partial(last_kernel, len(parts), fac is not None),
        grid=(rows // step,),
        in_specs=[spec(x) for x in ins],
        out_specs=spec(out),
        out_shape=out,
        compiler_params=params(),
        cost_estimate=cost(8 * rows * width, out, *ins),
        name="last_step",
    )(*ins)


def local(queries, passages, pool, query_count, positive, neg_owner, neg_row):
    n_query = queries.shape[0]
    n_pool = pool.shape[0]
    grp = lax.axis_index("grp")
    loop = lax.axis_index("loop")
    zi, xh, ci = grp // 4, (grp // 2) % 2, grp % 2
    xl, yi = loop // 4, loop % 4

    valid = (lax.iota(jnp.int32, n_query) < query_count.reshape(())).astype(f32)
    wide = queries.astype(f32)
    q_scale = lax.rsqrt(jnp.sum(wide * wide, axis=1) + eps)
    high = lax.reduce_precision(q_scale, 8, 7)
    mid = lax.reduce_precision(q_scale - high, 8, 7)
    low = q_scale - high - mid
    zero_row = jnp.zeros((1, n_query), f32)
    owners = jnp.where(valid[None, :] > 0, neg_owner.T.astype(f32), -1.0)
    left = jnp.concatenate([owners, zero_row, neg_row.T.astype(f32), zero_row], axis=0)
    right = jnp.concatenate([high[None], mid[None], low[None], jnp.tile(zero_row, (13, 1))], axis=0)
    info = jnp.concatenate([left, right], axis=1).astype(bf16)
    info = jnp.pad(info, ((0, 0), (0, queries.shape[1] - 2 * n_query)))
    message = jnp.concatenate([queries, info], axis=0)

    px = hop_xl(passages)
    q1 = hop_z(message, -1)
    q3 = hop_z(message, 1)
    side0 = hop_core(message)
    pool_late, passages_late = after((pool, passages), px)
    pool_x = (hop_xh(pool_late),)
    pc = jnp.concatenate([passages_late, px], axis=0)
    p1 = hop_y(pc, -1)
    p3 = hop_y(pc, 1)
    q1_next, q3_next = after((q1, q3), pc)
    q2a = hop_z(q1_next[:64], -1)
    q2b = hop_z(q3_next[64:], 1)
    p2 = hop_y(p1[:64], -1)
    p2x = hop_y(p3[64:], 1)
    q1_late, q3_late = after((q1, q3), q2a, q2b)
    side1, side3 = hop_core(q1_late), hop_core(q3_late)
    side2a, side2b = hop_core(q2a), hop_core(q2b)
    q_refs = (message, q1, q2a, q2b, q3, side0, side1, side2a, side2b, side3)
    p_refs = (pc, p1, p2, p2x, p3)
    tails = (message[128:], q1[128:], q2b[64:], q3[128:], side0[128:], side1[128:], side2b[64:], side3[128:])
    infos = jnp.stack([x[:, :256] for x in tails])

    bases = jnp.stack([grp * n_pool, (grp ^ 2) * n_pool]).astype(f32)
    steps = jnp.arange(4, dtype=jnp.int32)
    y_places = (yi + steps) % 4
    places = (
        jnp.concatenate([xl * 4 + y_places, (1 - xl) * 4 + y_places]) * passages.shape[0]
    ).astype(f32)
    pos = positive.astype(f32)
    about_first = jnp.concatenate([q_scale[None], pos[None], jnp.tile(zero_row, (6, 1))], axis=0)

    e_batch, stats, p_scales = batch_scores(places, about_first, p_refs, (queries,))
    e1, e2, part, s1, s2, codes = hard_scores(bases, infos, stats, q_refs, pool, pool_x)
    q_late, about_late = after((queries, about_first), pool_x[0])
    q_xa = hop_xl(q_late[:64])
    about_first_x = hop_xl(about_late)

    (e1_side, e2_side) = after((e1, e2), part, q_xa, about_first_x)
    (q_later,) = after((queries,), q_xa)
    q_xb = hop_xl(q_later[64:])
    got = [hop_z(part, -by) for by in (1, 2, 3)]
    (u_side,) = hard_back(1, e1_side, e2_side, s1, s2, pool, pool_x)
    u_got = hop_core(u_side)
    got, _ = lax.optimization_barrier((got, u_side))
    total = part.reshape(2, 4, n_query)
    for by in (1, 2, 3):
        total = total + jnp.roll(got[by - 1].reshape(2, 4, n_query), by, axis=1)
    core_total = hop_core(total)
    total = total + core_total[::-1]
    live = (codes[:, 0, :] >= 0).astype(f32)
    fac = live * codes[:, 7, :] / total.reshape(8, n_query)
    own_total = total[0, 0]
    loss = valid * (jnp.log(own_total) - stats[1])
    own_fac = valid / own_total
    about = jnp.concatenate(
        [own_fac[None], valid[None], pos[None], q_scale[None], jnp.tile(zero_row, (4, 1))], axis=0
    )
    about_x = hop_xl(about)

    dn_far = pool_part(e2, fac, q_refs, bf16)
    dn_far, _ = lax.optimization_barrier((dn_far, (about_x, q_xb)))
    dn_x = hop_xh(dn_far)
    (u_got,) = after((u_got,), dn_far)
    u_home, u1, u2, u3 = hard_back(0, e1, e2, s1, s2, pool, pool_x, u_got)
    u_parts = (u_home, hop_z(u1, 1), hop_z(u2, 2), hop_z(u3, -1))
    q_x = after((q_xa, q_xb), u_home)
    e_batch_x, _, _ = batch_scores(places, about_first_x, p_refs, q_x)
    d_home, d1, d2, d3 = passage_part(places, about, about_x, e_batch, e_batch_x, queries, q_x)
    d_parts = (d_home, hop_y(d1, 1), hop_y(d2, 2), hop_y(d3, -1))

    (e1_late, e_late) = after((e1, e_batch), d_home)
    dn_home = pool_part(e1_late, fac, q_refs, f32)
    dq_batch = query_part(places, about, e_late, p_scales, p_refs)
    grad_passage = last_step(d_parts, passages)
    fac_rows = jnp.broadcast_to(own_fac[:, None], (n_query, 128))
    (dn_x,) = after((dn_x,), grad_passage)
    grad_pool = last_step((dn_home, dn_x), pool)
    (dq_batch,) = after((dq_batch,), grad_pool)
    grad_query = last_step(u_parts, queries, fac_rows, dq_batch)
    return (loss, grad_query, grad_passage, grad_pool)


def solution(mesh):
    both = ("loop", "grp")
    return jax.shard_map(
        local,
        mesh=mesh,
        in_specs=(
            P(both, None),
            P(both, None),
            P(both, None),
            P("loop", "grp"),
            P(both),
            P(both, None),
            P(both, None),
        ),
        out_specs=(P(both), P(both, None), P(both, None), P(both, None)),
        check_vma=False,
    )
```

time: 705 us -> 218 us (0.31)
  waiting for transfers between devices: 369 us -> 94.6 us
  local copies, waits for them, and re-layouts: 135 us -> 11.5 us
  other arithmetic: 108 us -> 9.33 us
  Pallas kernels: 0 us -> 70.2 us
  matrix products: 51.4 us -> 0 us
  between operations: 15.2 us -> 1.72 us
  starting transfers between devices: 18.5 us -> 29.7 us
    ppermute x16 -> x31, waiting for transfers between devices: 251 us -> 94.6 us  [the longest x10 50.7 us: hop_z(): return lax.ppermute(x, 'grp', [(g, (g + 4 * by) % 16) for g in range(16)])]
    all_gather x1 -> x0, waiting for transfers between devices: 71 us -> none  [local(): lax.all_gather(p_hat, 'loop', axis=0, tiled=True)]
    pallas_call x0 -> x12, Pallas kernels: none -> 70.2 us  [the longest x3 14.7 us: last_step(): pl.pallas_call(functools.partial(last_kernel, len(parts), fac is not None...]
    dot_general x19 -> x0, matrix products: 51.4 us -> none  [the longest x8 18.3 us: gather_back(): lax.dot_general(coef, rows, (((0,), (0,)), ((), ())), preferred_element_t...]
    all_to_all x3 -> x0, waiting for transfers between devices: 47.7 us -> none  [the longest x1 45.7 us: local(): lax.all_to_all(picked, 'grp', split_axis=0, concat_axis=0, tiled=True)]
    scatter-add x1 -> x0, other arithmetic: 40.9 us -> none  [local(): jax.ops.segment_sum(incoming.reshape(-1, width).astype(jnp.float32), requ...]
    gather x4 -> x0, local copies, waits for them, and re-layouts: 37.5 us -> none  [the longest x1 19.8 us: local(): reply.reshape(groups * cap, width)[place]]
    ppermute x16 -> x31, starting transfers between devices: 0.04 us -> 29.7 us  [the longest x10 13.2 us: hop_z(): return lax.ppermute(x, 'grp', [(g, (g + 4 * by) % 16) for g in range(16)])]
  transfers between devices with their start and end apart: 20 -> 31, of which waited for: 19 -> 12; matrix products, arithmetic and copies ran while one was open for 17% -> 7% of each run, Pallas kernels for 0% -> 27%
where the time goes in v1:
time: 218 us; the launch traced here: 217 us
  waiting for transfers between devices  94.6 us (43%)
  Pallas kernels  70.2 us (32%)
  starting transfers between devices  29.7 us (14%)
  local copies, waits for them, and re-layouts  11.5 us (5%)
  other arithmetic  9.33 us (4%)
    ppermute x10, waiting for transfers between devices, hop_z(): return lax.ppermute(x, 'grp', [(g, (g + 4 * by) % 16) for g in range(16)])  50.7 us
    ppermute x7, waiting for transfers between devices, hop_y(): lax.ppermute(x, 'loop', [(l, (l & 4) + (l + by) % 4) for l in range(8)])  36.4 us
    pallas_call x3, Pallas kernels, last_step(): pl.pallas_call(functools.partial(last_kernel, len(parts), fac is not None...  14.7 us
    pallas_call x2, Pallas kernels, pool_part(): pl.pallas_call(pool_kernel, grid=(width // 2048,), in_specs=[whole_spec(e...  14 us
    pallas_call x2, Pallas kernels, hard_back(): pl.pallas_call(functools.partial(back_kernel, first), grid=(width // 2048...  13.3 us
    ppermute x10, starting transfers between devices, hop_z(): return lax.ppermute(x, 'grp', [(g, (g + 4 * by) % 16) for g in range(16)])  13.2 us
    pallas_call x1, Pallas kernels, hard_scores(): pl.pallas_call(hard_kernel, grid=(width // chunk,), in_specs=[smem_spec()...  11.9 us
    pallas_call x2, Pallas kernels, batch_scores(): pl.pallas_call(batch_kernel, grid=(width // 2048,), in_specs=[smem_spec()...  8.6 us
  transfers between devices with their start and end apart: 31, of which 12 were waited for; matrix products, arithmetic and copies ran while one was open for 7% of the time, Pallas kernels for 27%

profile of v1, /device:TPU:0, one launch (start us, length us, event | category | flops | bytes accessed | tf_op | source)
XLA Modules:
  0.0 217.0 jit_solution(15809531687822755902)
XLA Ops:
  0.6 1.7 collective-permute-start.2
  2.9 1.5 multiply_reduce_fusion
  4.5 0.7 convert_bitcast_fusion
  5.3 0.7 select_bitcast_fusion
  6.1 2.4 %pad_maximum_fusion.rest_0_ = bf16[144,4096]{1,0:T(8,128)(2,1)} fusion(bf16[16,4096]{1,0:T(8,128)(2,1)S(1)} %fusion.2, bf16[128,4096]{1,0:T(8,128)(2,1)} %refs_6_.1), kind=kLoop, calls=%fused_computation.1 | loop fusion | flops 2359296 | bytes 2359296 | tf_op jit(solution)/shard_map/concatenate | solution.py:434
  8.4 4.0 %collective-permute-start = (bf16[144,4096]{1,0:T(8,128)(2,1)}, bf16[144,4096]{1,0:T(8,128)(2,1)S(1)}, u32[]{:S(2)}, u32[]{:S(2)}) collective-permute-start(bf16[144,4096]{1,0:T(8,128)(2,1)} %pad_maximum_fusion.rest_0_), channel_id=1, source_target_pairs={{0,12},{1,13},{2,14},{3,15},{4,0},{5,1},{6,2},{7,3},{8,4},{9,5},{1... | collective-permute-start | bytes 3538952 | tf_op jit(solution)/shard_map/ppermute | solution.py:19
  12.5 1.9 collective-permute-done.2
  14.4 0.8 constant_dynamic-update-slice_fusion.1
  15.3 0.8 constant_dynamic-update-slice_fusion.rest_0_
  16.1 21.6 %collective-permute-done.rest_1_ = bf16[144,4096]{1,0:T(8,128)(2,1)S(1)} collective-permute-done((bf16[144,4096]{1,0:T(8,128)(2,1)}, bf16[144,4096]{1,0:T(8,128)(2,1)S(1)}, u32[]{:S(2)}, u32[]{:S(2)}) %collective-permute-start) | collective-permute-done | bytes 1179680 | tf_op jit(solution)/shard_map/ppermute | solution.py:19
  37.7 3.3 %collective-permute-done.1.rest_4_ = bf16[144,4096]{1,0:T(8,128)(2,1)S(1)} collective-permute-done((bf16[144,4096]{1,0:T(8,128)(2,1)}, bf16[144,4096]{1,0:T(8,128)(2,1)S(1)}, u32[]{:S(2)}, u32[]{:S(2)}) %collective-permute-start.1) | collective-permute-done | bytes 1179680 | tf_op jit(solution)/shard_map/ppermute | solution.py:19
  41.1 0.9 slice.95
  42.0 0.3 collective-permute-start.5
  42.2 2.7 %collective-permute-start.14 = (bf16[256,4096]{1,0:T(8,128)(2,1)S(1)}, bf16[256,4096]{1,0:T(8,128)(2,1)}, u32[]{:S(2)}, u32[]{:S(2)}) collective-permute-start(bf16[256,4096]{1,0:T(8,128)(2,1)S(1)} %copy-done.1), channel_id=1, source_target_pairs={{0,2},{1,3},{2,0},{3,1},{4,6},{5,7},{6,4},{7,5},{8,10},{9,11},{10,... | collective-permute-start | bytes 6291464 | tf_op jit(solution)/shard_map/ppermute | solution.py:23
  45.0 3.0 %collective-permute-start.9 = (bf16[128,4096]{1,0:T(8,128)(2,1)}, bf16[128,4096]{1,0:T(8,128)(2,1)}, u32[]{:S(2)}, u32[]{:S(2)}) collective-permute-start(bf16[128,4096]{1,0:T(8,128)(2,1)} %constant_dynamic-update-slice_fusion.rest_0_), channel_id=1, source_target_pairs={{0,48},{16,0},{32,16},{48,32},{64,112},{80,64},{96,80},{112,96},{1... | collective-permute-start | bytes 3145736 | tf_op jit(solution)/shard_map/ppermute | solution.py:35
  48.1 6.3 %collective-permute-done.5.rest_2_ = bf16[64,4096]{1,0:T(8,128)(2,1)} collective-permute-done((bf16[64,4096]{1,0:T(8,128)(2,1)}, bf16[64,4096]{1,0:T(8,128)(2,1)}, u32[]{:S(2)}, u32[]{:S(2)}) %collective-permute-start.5) | collective-permute-done | bytes 524320 | tf_op jit(solution)/shard_map/ppermute | solution.py:19
  54.4 0.7 add_convert_fusion.bases
  55.1 14.6 %collective-permute-done.3.rest_3_ = bf16[80,4096]{1,0:T(8,128)(2,1)S(1)} collective-permute-done((bf16[80,4096]{1,0:T(8,128)(2,1)S(1)}, bf16[80,4096]{1,0:T(8,128)(2,1)S(1)}, u32[]{:S(2)}, u32[]{:S(2)}) %collective-permute-start.3) | collective-permute-done | bytes 655392 | tf_op jit(solution)/shard_map/ppermute | solution.py:19
  69.7 0.8 maximum_maximum_fusion.about
  70.5 1.1 slice.120
  71.6 3.1 %collective-permute-start.10 = (bf16[64,4096]{1,0:T(8,128)(2,1)S(1)}, bf16[64,4096]{1,0:T(8,128)(2,1)}, u32[]{:S(2)}, u32[]{:S(2)}) collective-permute-start(bf16[64,4096]{1,0:T(8,128)(2,1)S(1)} %slice.120), channel_id=1, source_target_pairs={{0,48},{16,0},{32,16},{48,32},{64,112},{80,64},{96,80},{112,96},{1... | collective-permute-start | bytes 1572872 | tf_op jit(solution)/shard_map/ppermute | solution.py:35
  74.6 0.7 fusion.10.places
  75.5 0.7 constant_dynamic-update-slice_fusion.8
  76.2 1.1 slice.121
  77.4 9.1 %collective-permute-done.10.rest_2_ = bf16[64,4096]{1,0:T(8,128)(2,1)} collective-permute-done((bf16[64,4096]{1,0:T(8,128)(2,1)S(1)}, bf16[64,4096]{1,0:T(8,128)(2,1)}, u32[]{:S(2)}, u32[]{:S(2)}) %collective-permute-start.10) | collective-permute-done | bytes 524320 | tf_op jit(solution)/shard_map/ppermute | solution.py:35
  86.4 0.7 constant_dynamic-update-slice_fusion.5
  87.1 5.7 %collective-permute-done.12.rest_3_ = bf16[64,4096]{1,0:T(8,128)(2,1)} collective-permute-done((bf16[64,4096]{1,0:T(8,128)(2,1)S(1)}, bf16[64,4096]{1,0:T(8,128)(2,1)}, u32[]{:S(2)}, u32[]{:S(2)}) %collective-permute-start.12) | collective-permute-done | bytes 524320 | tf_op jit(solution)/shard_map/ppermute | solution.py:35
  92.8 4.3 %batch_scores.2 = (f32[512,128]{1,0:T(8,128)}, f32[8,128]{1,0:T(8,128)}, f32[512,128]{1,0:T(8,128)}) custom-call(f32[8]{0:T(128)} %fusion.10.places, f32[8,128]{1,0:T(8,128)} %maximum_maximum_fusion.about, bf16[128,4096]{1,0:T(8,128)(2,1)} %constant_dynamic-update-slice_fusion.rest_0_, bf16[128,4096]{1,0:T(8,128)(2,1)} %collective-permute-done.9.rest_1_, ...), custom_call_target="tpu_custom_call" | custom-call | flops 1 | bytes 1 | tf_op jit(solution)/shard_map/batch_scores/pallas_call | solution.py:217
  97.2 0.6 collective-permute-start.18
  97.8 1.7 collective-permute-start.19
  99.6 0.8 copy-done.7
  100.4 0.4 copy-done.5
  100.8 11.9 %hard_scores.1 = (f32[256,1024]{1,0:T(8,128)}, f32[256,1024]{1,0:T(8,128)}, f32[8,128]{1,0:T(8,128)}, f32[256,128]{1,0:T(8,128)}, f32[256,128]{1,0:T(8,128)}, /*index=5*/f32[8,8,128]{2,1,0:T(8,128)}) custom-call(f32[2]{0:T(128)} %add_convert_fusion.bases, bf16[8,16,256]{2,1,0:T(8,128)(2,1)} %copy-done.18, f32[8,128]{1,0:T(8,128)} %get-tuple-element.49.before, ...), custom_call_target="tpu_custom_call" | custom-call | flops 1 | bytes 1 | tf_op jit(solution)/shard_map/hard_scores/pallas_call | solution.py:156
  112.7 6.2 %hard_back.2 = bf16[512,4096]{1,0:T(8,128)(2,1)} custom-call(f32[256,1024]{1,0:T(8,128)} %get-tuple-element.78.e1.e, f32[256,1024]{1,0:T(8,128)} %get-tuple-element.57.e2.e, f32[256,128]{1,0:T(8,128)} %get-tuple-element.58.s1, f32[256,128]{1,0:T(8,128)} %get-tuple-element.59.s2, bf16[256,4096]{1,0:T(8,128)(2,1)} %refs_2_.1, ...), custom_call_target="tpu_custom_call" | custom-call | flops 1 | bytes 1 | tf_op jit(solution)/shard_map/hard_back/pallas_call | solution.py:260
  119.1 0.9 collective-permute-start.15
  120.0 2.7 %collective-permute-start.16 = (f32[8,128]{1,0:T(8,128)S(1)}, f32[8,128]{1,0:T(8,128)S(1)}, u32[]{:S(2)}, u32[]{:S(2)}) collective-permute-start(f32[8,128]{1,0:T(8,128)S(1)} %copy-done.24), channel_id=1, source_target_pairs={{0,8},{1,9},{2,10},{3,11},{4,12},{5,13},{6,14},{7,15},{8,0},{9,1},... | collective-permute-start | bytes 12296 | tf_op jit(solution)/shard_map/ppermute | solution.py:19
  122.8 2.4 %collective-permute-done.16 = f32[8,128]{1,0:T(8,128)S(1)} collective-permute-done((f32[8,128]{1,0:T(8,128)S(1)}, f32[8,128]{1,0:T(8,128)S(1)}, u32[]{:S(2)}, u32[]{:S(2)}) %collective-permute-start.16) | collective-permute-done | bytes 4128 | tf_op jit(solution)/shard_map/ppermute | solution.py:19
  125.2 2.4 %collective-permute-done.17 = f32[8,128]{1,0:T(8,128)S(1)} collective-permute-done((f32[8,128]{1,0:T(8,128)S(1)}, f32[8,128]{1,0:T(8,128)S(1)}, u32[]{:S(2)}, u32[]{:S(2)}) %collective-permute-start.17) | collective-permute-done | bytes 4128 | tf_op jit(solution)/shard_map/ppermute | solution.py:19
  127.8 0.3 collective-permute-start.23
  128.1 0.7 collective-permute-done.20
  128.9 1.1 collective-permute-start.22
  130.0 0.6 fusion.4.fac
  130.6 6.8 %pool_part.2 = bf16[256,4096]{1,0:T(8,128)(2,1)} custom-call(f32[256,1024]{1,0:T(8,128)} %get-tuple-element.57.e2.e, f32[8,128]{1,0:T(8,128)} %fusion.4.fac, bf16[144,4096]{1,0:T(8,128)(2,1)} %pad_maximum_fusion.rest_0_, bf16[144,4096]{1,0:T(8,128)(2,1)} %copy-done.3, bf16[64,4096]{1,0:T(8,128)(2,1)} %collective-permute-done.5.rest_2_, ...), custom_call_target="tpu_custom_call" | custom-call | flops 1 | bytes 1 | tf_op jit(solution)/shard_map/pool_part/pallas_call | solution.py:291
  137.5 4.8 %collective-permute-done.22.about_b = f32[8,128]{1,0:T(8,128)S(1)} collective-permute-done((f32[8,128]{1,0:T(8,128)S(1)}, f32[8,128]{1,0:T(8,128)S(1)}, u32[]{:S(2)}, u32[]{:S(2)}) %collective-permute-start.22) | collective-permute-done | bytes 4128 | tf_op jit(solution)/shard_map/ppermute | solution.py:31
  142.3 0.9 collective-permute-start.27
  143.2 7.1 %hard_back.3 = (f32[128,4096]{1,0:T(8,128)}, bf16[128,4096]{1,0:T(8,128)(2,1)}, bf16[128,4096]{1,0:T(8,128)(2,1)}, bf16[128,4096]{1,0:T(8,128)(2,1)}) custom-call(f32[256,1024]{1,0:T(8,128)} %get-tuple-element.78.e1.e, f32[256,1024]{1,0:T(8,128)} %get-tuple-element.57.e2.e, f32[256,128]{1,0:T(8,128)} %get-tuple-element.58.s1, ...), custom_call_target="tpu_custom_call" | custom-call | flops 1 | bytes 1 | tf_op jit(solution)/shard_map/hard_back/pallas_call | solution.py:260
  150.3 4.3 %batch_scores.3 = (f32[512,128]{1,0:T(8,128)}, f32[8,128]{1,0:T(8,128)}, f32[512,128]{1,0:T(8,128)}) custom-call(f32[8]{0:T(128)} %fusion.10.places, f32[8,128]{1,0:T(8,128)} %copy-done.22, bf16[128,4096]{1,0:T(8,128)(2,1)} %constant_dynamic-update-slice_fusion.rest_0_, bf16[128,4096]{1,0:T(8,128)(2,1)} %collective-permute-done.9.rest_1_, ...), custom_call_target="tpu_custom_call" | custom-call | flops 1 | bytes 1 | tf_op jit(solution)/shard_map/batch_scores/pallas_call | solution.py:217
  154.6 3.5 %passage_part.1 = (f32[64,4096]{1,0:T(8,128)}, bf16[64,4096]{1,0:T(8,128)(2,1)}, bf16[64,4096]{1,0:T(8,128)(2,1)}, bf16[64,4096]{1,0:T(8,128)(2,1)}) custom-call(f32[8]{0:T(128)} %fusion.10.places, f32[8,128]{1,0:T(8,128)} %copy-done.19, f32[8,128]{1,0:T(8,128)} %copy-done.23, f32[512,128]{1,0:T(8,128)} %get-tuple-element.76.e_a.e, ...), custom_call_target="tpu_custom_call" | custom-call | flops 1 | bytes 1 | tf_op jit(solution)/shard_map/passage_part/pallas_call | solution.py:356
  158.2 0.9 collective-permute-start.29
  159.0 0.8 collective-permute-start.24
  159.8 2.6 %collective-permute-start.25 = (bf16[128,4096]{1,0:T(8,128)(2,1)}, bf16[128,4096]{1,0:T(8,128)(2,1)S(1)}, u32[]{:S(2)}, u32[]{:S(2)}) collective-permute-start(bf16[128,4096]{1,0:T(8,128)(2,1)} %get-tuple-element.69), channel_id=1, source_target_pairs={{0,8},{1,9},{2,10},{3,11},{4,12},{5,13},{6,14},{7,15},{8,0},{9,1},... | collective-permute-start | bytes 3145736 | tf_op jit(solution)/shard_map/ppermute | solution.py:19
  162.4 21.6 %collective-permute-done.28.refs_1_ = bf16[64,4096]{1,0:T(8,128)(2,1)S(1)} collective-permute-done((bf16[64,4096]{1,0:T(8,128)(2,1)}, bf16[64,4096]{1,0:T(8,128)(2,1)S(1)}, u32[]{:S(2)}, u32[]{:S(2)}) %collective-permute-start.28) | collective-permute-done | bytes 524320 | tf_op jit(solution)/shard_map/ppermute | solution.py:35
  184.1 1.8 collective-permute-start.26
  185.9 1.2 fusion.7
  187.1 7.2 %pool_part.3.refs_0_ = f32[256,4096]{1,0:T(8,128)} custom-call(f32[256,1024]{1,0:T(8,128)} %get-tuple-element.78.e1.e, f32[8,128]{1,0:T(8,128)} %fusion.4.fac, bf16[144,4096]{1,0:T(8,128)(2,1)} %pad_maximum_fusion.rest_0_, bf16[144,4096]{1,0:T(8,128)(2,1)} %copy-done.3, bf16[64,4096]{1,0:T(8,128)(2,1)} %collective-permute-done.5.rest_2_, ...), custom_call_target="tpu_custom_call" | custom-call | flops 1 | bytes 1 | tf_op jit(solution)/shard_map/pool_part/pallas_call | solution.py:291
  194.3 4.1 %query_part.1.refs_5_ = f32[128,4096]{1,0:T(8,128)} custom-call(f32[8]{0:T(128)} %fusion.10.places, f32[8,128]{1,0:T(8,128)} %copy-done.19, f32[512,128]{1,0:T(8,128)} %get-tuple-element.76.e_a.e, f32[512,128]{1,0:T(8,128)} %get-tuple-element.77.scales, bf16[128,4096]{1,0:T(8,128)(2,1)} %constant_dynamic-update-slice_fusion.rest_0_, ...), custom_call_target="tpu_custom_call" | custom-call | flops 1 | bytes 1 | tf_op jit(solution)/shard_map/query_part/pallas_call | solution.py:322
  198.4 0.8 copy-done.17
  199.2 3.4 %last_step.3 = f32[64,4096]{1,0:T(8,128)} custom-call(f32[64,4096]{1,0:T(8,128)} %get-tuple-element.75.refs_0_, bf16[64,4096]{1,0:T(8,128)(2,1)} %copy-done.15, bf16[64,4096]{1,0:T(8,128)(2,1)} %copy-done.16, bf16[64,4096]{1,0:T(8,128)(2,1)} %copy-done.17, bf16[64,4096]{1,0:T(8,128)(2,1)} %refs_4_.1), custom_call_target="tpu_custom_call" | custom-call | flops 1 | bytes 1 | tf_op jit(solution)/shard_map/last_step/pallas_call | solution.py:402
  202.6 1.3 copy-done.10
  203.9 6.3 %last_step.4 = f32[256,4096]{1,0:T(8,128)} custom-call(f32[256,4096]{1,0:T(8,128)} %pool_part.3.refs_0_, bf16[256,4096]{1,0:T(8,128)(2,1)} %copy-done.10, bf16[256,4096]{1,0:T(8,128)(2,1)} %refs_2_.1), custom_call_target="tpu_custom_call" | custom-call | flops 1 | bytes 1 | tf_op jit(solution)/shard_map/last_step/pallas_call | solution.py:402
  210.3 0.8 broadcast_in_dim.19.refs_4_
  211.2 0.4 copy-done.13
  211.6 0.3 copy-done.14
  211.9 5.0 %last_step.5 = f32[128,4096]{1,0:T(8,128)} custom-call(f32[128,4096]{1,0:T(8,128)} %get-tuple-element.67.refs_0_, bf16[128,4096]{1,0:T(8,128)(2,1)} %copy-done.12, bf16[128,4096]{1,0:T(8,128)(2,1)} %copy-done.13, bf16[128,4096]{1,0:T(8,128)(2,1)} %copy-done.14, f32[128,128]{1,0:T(8,128)} %broadcast_in_dim.19.refs_4_, f32[128,4096]{1,0:T(8,128)} %query_part.1.refs_5_, ...), custom_call_target="tpu_custom_call" | custom-call | flops 1 | bytes 1 | tf_op jit(solution)/shard_map/last_step/pallas_call | solution.py:402
  (113 shorter events, 1.2 us)
Async XLA Ops:
  0.6 13.8 %copy-start.11 = (bf16[64,4096]{1,0:T(8,128)(2,1)S(1)}, bf16[64,4096]{1,0:T(8,128)(2,1)}, u32[]{:S(2)}) copy-start(bf16[64,4096]{1,0:T(8,128)(2,1)} %refs_4_.1) | copy-start | bytes 1572868
  0.6 13.8 %collective-permute-start.2 = (bf16[64,4096]{1,0:T(8,128)(2,1)}, bf16[64,4096]{1,0:T(8,128)(2,1)S(1)}, u32[]{:S(2)}, u32[]{:S(2)}) collective-permute-start(bf16[64,4096]{1,0:T(8,128)(2,1)} %refs_4_.1), channel_id=1, source_target_pairs={{0,64},{16,80},{32,96},{48,112},{64,0},{80,16},{96,32},{112,48},{1... | collective-permute-start | bytes 1572872 | tf_op jit(solution)/shard_map/ppermute | solution.py:31
  8.4 33.8 %copy-start.1 = (bf16[256,4096]{1,0:T(8,128)(2,1)S(1)}, bf16[256,4096]{1,0:T(8,128)(2,1)}, u32[]{:S(2)}) copy-start(bf16[256,4096]{1,0:T(8,128)(2,1)} %refs_2_.1) | copy-start | bytes 6291460
  8.4 46.7 %copy-start.26 = (s32[128]{0:T(128)S(1)}, s32[128]{0:T(128)}, u32[]{:S(2)}) copy-start(s32[128]{0:T(128)} %param.11) | copy-start | bytes 1540
  8.4 29.3 %collective-permute-start = (bf16[144,4096]{1,0:T(8,128)(2,1)}, bf16[144,4096]{1,0:T(8,128)(2,1)S(1)}, u32[]{:S(2)}, u32[]{:S(2)}) collective-permute-start(bf16[144,4096]{1,0:T(8,128)(2,1)} %pad_maximum_fusion.rest_0_), channel_id=1, source_target_pairs={{0,12},{1,13},{2,14},{3,15},{4,0},{5,1},{6,2},{7,3},{8,4},{9,5},{1... | collective-permute-start | bytes 3538952 | tf_op jit(solution)/shard_map/ppermute | solution.py:19
  12.5 28.6 %collective-permute-start.1 = (bf16[144,4096]{1,0:T(8,128)(2,1)}, bf16[144,4096]{1,0:T(8,128)(2,1)S(1)}, u32[]{:S(2)}, u32[]{:S(2)}) collective-permute-start(bf16[144,4096]{1,0:T(8,128)(2,1)} %pad_maximum_fusion.rest_0_), channel_id=1, source_target_pairs={{0,4},{1,5},{2,6},{3,7},{4,8},{5,9},{6,10},{7,11},{8,12},{9,13},{1... | collective-permute-start | bytes 3538952 | tf_op jit(solution)/shard_map/ppermute | solution.py:19
  37.7 7.2 %copy-start.3 = (bf16[144,4096]{1,0:T(8,128)(2,1)}, bf16[144,4096]{1,0:T(8,128)(2,1)S(1)}, u32[]{:S(2)}) copy-start(bf16[144,4096]{1,0:T(8,128)(2,1)S(1)} %collective-permute-done.rest_1_) | copy-start | bytes 3538948
  41.0 58.6 %copy-start.2 = (bf16[144,4096]{1,0:T(8,128)(2,1)}, bf16[144,4096]{1,0:T(8,128)(2,1)S(1)}, u32[]{:S(2)}) copy-start(bf16[144,4096]{1,0:T(8,128)(2,1)S(1)} %collective-permute-done.1.rest_4_) | copy-start | bytes 3538948
  42.0 12.5 %collective-permute-start.5 = (bf16[64,4096]{1,0:T(8,128)(2,1)}, bf16[64,4096]{1,0:T(8,128)(2,1)}, u32[]{:S(2)}, u32[]{:S(2)}) collective-permute-start(bf16[64,4096]{1,0:T(8,128)(2,1)} %slice.95), channel_id=1, source_target_pairs={{0,12},{1,13},{2,14},{3,15},{4,0},{5,1},{6,2},{7,3},{8,4},{9,5},{1... | collective-permute-start | bytes 1572872 | tf_op jit(solution)/shard_map/ppermute | solution.py:19
  42.2 54.9 %collective-permute-start.14 = (bf16[256,4096]{1,0:T(8,128)(2,1)S(1)}, bf16[256,4096]{1,0:T(8,128)(2,1)}, u32[]{:S(2)}, u32[]{:S(2)}) collective-permute-start(bf16[256,4096]{1,0:T(8,128)(2,1)S(1)} %copy-done.1), channel_id=1, source_target_pairs={{0,2},{1,3},{2,0},{3,1},{4,6},{5,7},{6,4},{7,5},{8,10},{9,11},{10,... | collective-permute-start | bytes 6291464 | tf_op jit(solution)/shard_map/ppermute | solution.py:23
  45.0 25.5 %collective-permute-start.9 = (bf16[128,4096]{1,0:T(8,128)(2,1)}, bf16[128,4096]{1,0:T(8,128)(2,1)}, u32[]{:S(2)}, u32[]{:S(2)}) collective-permute-start(bf16[128,4096]{1,0:T(8,128)(2,1)} %constant_dynamic-update-slice_fusion.rest_0_), channel_id=1, source_target_pairs={{0,48},{16,0},{32,16},{48,32},{64,112},{80,64},{96,80},{112,96},{1... | collective-permute-start | bytes 3145736 | tf_op jit(solution)/shard_map/ppermute | solution.py:35
  48.0 29.3 %collective-permute-start.4 = (bf16[144,4096]{1,0:T(8,128)(2,1)}, bf16[144,4096]{1,0:T(8,128)(2,1)}, u32[]{:S(2)}, u32[]{:S(2)}) collective-permute-start(bf16[144,4096]{1,0:T(8,128)(2,1)} %pad_maximum_fusion.rest_0_), channel_id=1, source_target_pairs={{0,1},{1,0},{2,3},{3,2},{4,5},{5,4},{6,7},{7,6},{8,9},{9,8},{10,11... | collective-permute-start | bytes 3538952 | tf_op jit(solution)/shard_map/ppermute | solution.py:27
  48.0 27.3 %collective-permute-start.11 = (bf16[128,4096]{1,0:T(8,128)(2,1)}, bf16[128,4096]{1,0:T(8,128)(2,1)}, u32[]{:S(2)}, u32[]{:S(2)}) collective-permute-start(bf16[128,4096]{1,0:T(8,128)(2,1)} %constant_dynamic-update-slice_fusion.rest_0_), channel_id=1, source_target_pairs={{0,16},{16,32},{32,48},{48,0},{64,80},{80,96},{96,112},{112,64},{1... | collective-permute-start | bytes 3145736 | tf_op jit(solution)/shard_map/ppermute | solution.py:35
  54.4 15.3 %collective-permute-start.3 = (bf16[80,4096]{1,0:T(8,128)(2,1)S(1)}, bf16[80,4096]{1,0:T(8,128)(2,1)S(1)}, u32[]{:S(2)}, u32[]{:S(2)}) collective-permute-start(bf16[80,4096]{1,0:T(8,128)(2,1)S(1)} %slice.91), channel_id=1, source_target_pairs={{0,4},{1,5},{2,6},{3,7},{4,8},{5,9},{6,10},{7,11},{8,12},{9,13},{1... | collective-permute-start | bytes 1966088 | tf_op jit(solution)/shard_map/ppermute | solution.py:19
  69.7 27.4 %copy-start.6 = (bf16[80,4096]{1,0:T(8,128)(2,1)}, bf16[80,4096]{1,0:T(8,128)(2,1)S(1)}, u32[]{:S(2)}) copy-start(bf16[80,4096]{1,0:T(8,128)(2,1)S(1)} %collective-permute-done.3.rest_3_) | copy-start | bytes 1966084
  69.7 28.1 %collective-permute-start.6 = (bf16[144,4096]{1,0:T(8,128)(2,1)}, bf16[144,4096]{1,0:T(8,128)(2,1)S(1)}, u32[]{:S(2)}, u32[]{:S(2)}) collective-permute-start(bf16[144,4096]{1,0:T(8,128)(2,1)} %copy-done.3), channel_id=1, source_target_pairs={{0,1},{1,0},{2,3},{3,2},{4,5},{5,4},{6,7},{7,6},{8,9},{9,8},{10,11... | collective-permute-start | bytes 3538952 | tf_op jit(solution)/shard_map/ppermute | solution.py:27
  71.6 14.9 %collective-permute-start.10 = (bf16[64,4096]{1,0:T(8,128)(2,1)S(1)}, bf16[64,4096]{1,0:T(8,128)(2,1)}, u32[]{:S(2)}, u32[]{:S(2)}) collective-permute-start(bf16[64,4096]{1,0:T(8,128)(2,1)S(1)} %slice.120), channel_id=1, source_target_pairs={{0,48},{16,0},{32,16},{48,32},{64,112},{80,64},{96,80},{112,96},{1... | collective-permute-start | bytes 1572872 | tf_op jit(solution)/shard_map/ppermute | solution.py:35
  75.3 24.2 %collective-permute-start.8 = (bf16[144,4096]{1,0:T(8,128)(2,1)S(1)}, bf16[144,4096]{1,0:T(8,128)(2,1)S(1)}, u32[]{:S(2)}, u32[]{:S(2)}) collective-permute-start(bf16[144,4096]{1,0:T(8,128)(2,1)S(1)} %collective-permute-done.1.rest_4_), channel_id=1, source_target_pairs={{0,1},{1,0},{2,3},{3,2},{4,5},{5,4},{6,7},{7,6},{8,9},{9,8},{10,11... | collective-permute-start | bytes 3538952 | tf_op jit(solution)/shard_map/ppermute | solution.py:27
  77.3 15.6 %collective-permute-start.12 = (bf16[64,4096]{1,0:T(8,128)(2,1)S(1)}, bf16[64,4096]{1,0:T(8,128)(2,1)}, u32[]{:S(2)}, u32[]{:S(2)}) collective-permute-start(bf16[64,4096]{1,0:T(8,128)(2,1)S(1)} %slice.121), channel_id=1, source_target_pairs={{0,16},{16,32},{32,48},{48,0},{64,80},{80,96},{96,112},{112,64},{1... | collective-permute-start | bytes 1572872 | tf_op jit(solution)/shard_map/ppermute | solution.py:35
  86.4 13.1 %collective-permute-start.7 = (bf16[80,4096]{1,0:T(8,128)(2,1)S(1)}, bf16[80,4096]{1,0:T(8,128)(2,1)S(1)}, u32[]{:S(2)}, u32[]{:S(2)}) collective-permute-start(bf16[80,4096]{1,0:T(8,128)(2,1)S(1)} %collective-permute-done.3.rest_3_), channel_id=1, source_target_pairs={{0,1},{1,0},{2,3},{3,2},{4,5},{5,4},{6,7},{7,6},{8,9},{9,8},{10,11... | collective-permute-start | bytes 1966088 | tf_op jit(solution)/shard_map/ppermute | solution.py:27
  87.1 10.0 %copy-start = (bf16[128,4096]{1,0:T(8,128)(2,1)S(1)}, bf16[128,4096]{1,0:T(8,128)(2,1)}, u32[]{:S(2)}) copy-start(bf16[128,4096]{1,0:T(8,128)(2,1)} %refs_6_.1) | copy-start | bytes 3145732
  87.1 10.7 %copy-start.21 = (f32[8,128]{1,0:T(8,128)S(1)}, f32[8,128]{1,0:T(8,128)}, u32[]{:S(2)}) copy-start(f32[8,128]{1,0:T(8,128)} %maximum_maximum_fusion.about) | copy-start | bytes 12292
  92.8 6.8 %collective-permute-start.13 = (bf16[64,4096]{1,0:T(8,128)(2,1)}, bf16[64,4096]{1,0:T(8,128)(2,1)}, u32[]{:S(2)}, u32[]{:S(2)}) collective-permute-start(bf16[64,4096]{1,0:T(8,128)(2,1)} %collective-permute-done.5.rest_2_), channel_id=1, source_target_pairs={{0,1},{1,0},{2,3},{3,2},{4,5},{5,4},{6,7},{7,6},{8,9},{9,8},{10,11... | collective-permute-start | bytes 1572872 | tf_op jit(solution)/shard_map/ppermute | solution.py:27
  97.2 15.5 %collective-permute-start.18 = (bf16[64,4096]{1,0:T(8,128)(2,1)S(1)}, bf16[64,4096]{1,0:T(8,128)(2,1)S(1)}, u32[]{:S(2)}, u32[]{:S(2)}) collective-permute-start(bf16[64,4096]{1,0:T(8,128)(2,1)S(1)} %slice.101), channel_id=1, source_target_pairs={{0,64},{16,80},{32,96},{48,112},{64,0},{80,16},{96,32},{112,48},{1... | collective-permute-start | bytes 1572872 | tf_op jit(solution)/shard_map/ppermute | solution.py:31
  97.8 1.8 copy-start.4
  97.8 14.9 %collective-permute-start.19 = (f32[8,128]{1,0:T(8,128)S(1)}, f32[8,128]{1,0:T(8,128)S(1)}, u32[]{:S(2)}, u32[]{:S(2)}) collective-permute-start(f32[8,128]{1,0:T(8,128)S(1)} %copy-done.21), channel_id=1, source_target_pairs={{0,64},{16,80},{32,96},{48,112},{64,0},{80,16},{96,32},{112,48},{1... | collective-permute-start | bytes 12296 | tf_op jit(solution)/shard_map/ppermute | solution.py:31
  99.5 0.8 copy-start.7
  99.6 1.2 copy-start.5
  99.6 1.2 copy-start.18
  112.7 6.3 %copy-start.22 = (f32[8,128]{1,0:T(8,128)}, f32[8,128]{1,0:T(8,128)S(1)}, u32[]{:S(2)}) copy-start(f32[8,128]{1,0:T(8,128)S(1)} %collective-permute-done.19.about) | copy-start | bytes 12292
  112.7 6.3 %copy-start.8 = (bf16[64,4096]{1,0:T(8,128)(2,1)}, bf16[64,4096]{1,0:T(8,128)(2,1)S(1)}, u32[]{:S(2)}) copy-start(bf16[64,4096]{1,0:T(8,128)(2,1)S(1)} %collective-permute-done.18.rest_5_.q_b) | copy-start | bytes 1572868
  112.7 6.4 %copy-start.24 = (f32[8,128]{1,0:T(8,128)S(1)}, f32[8,128]{1,0:T(8,128)}, u32[]{:S(2)}) copy-start(f32[8,128]{1,0:T(8,128)} %get-tuple-element.51) | copy-start | bytes 12292
  112.7 15.0 %copy-start.20 = (f32[8,8,128]{2,1,0:T(8,128)S(1)}, f32[8,8,128]{2,1,0:T(8,128)}, u32[]{:S(2)}) copy-start(f32[8,8,128]{2,1,0:T(8,128)} %get-tuple-element.63) | copy-start | bytes 98308
  119.0 24.2 %collective-permute-start.21 = (bf16[512,4096]{1,0:T(8,128)(2,1)}, bf16[512,4096]{1,0:T(8,128)(2,1)}, u32[]{:S(2)}, u32[]{:S(2)}) collective-permute-start(bf16[512,4096]{1,0:T(8,128)(2,1)} %hard_back.2), channel_id=1, source_target_pairs={{0,1},{1,0},{2,3},{3,2},{4,5},{5,4},{6,7},{7,6},{8,9},{9,8},{10,11... | collective-permute-start | bytes 12582920 | tf_op jit(solution)/shard_map/ppermute | solution.py:27
  119.1 3.7 %collective-permute-start.15 = (f32[8,128]{1,0:T(8,128)S(1)}, f32[8,128]{1,0:T(8,128)S(1)}, u32[]{:S(2)}, u32[]{:S(2)}) collective-permute-start(f32[8,128]{1,0:T(8,128)S(1)} %copy-done.24), channel_id=1, source_target_pairs={{0,12},{1,13},{2,14},{3,15},{4,0},{5,1},{6,2},{7,3},{8,4},{9,5},{1... | collective-permute-start | bytes 12296 | tf_op jit(solution)/shard_map/ppermute | solution.py:19
  120.0 5.1 %collective-permute-start.16 = (f32[8,128]{1,0:T(8,128)S(1)}, f32[8,128]{1,0:T(8,128)S(1)}, u32[]{:S(2)}, u32[]{:S(2)}) collective-permute-start(f32[8,128]{1,0:T(8,128)S(1)} %copy-done.24), channel_id=1, source_target_pairs={{0,8},{1,9},{2,10},{3,11},{4,12},{5,13},{6,14},{7,15},{8,0},{9,1},... | collective-permute-start | bytes 12296 | tf_op jit(solution)/shard_map/ppermute | solution.py:19
  122.7 4.8 %collective-permute-start.17 = (f32[8,128]{1,0:T(8,128)S(1)}, f32[8,128]{1,0:T(8,128)S(1)}, u32[]{:S(2)}, u32[]{:S(2)}) collective-permute-start(f32[8,128]{1,0:T(8,128)S(1)} %copy-done.24), channel_id=1, source_target_pairs={{0,4},{1,5},{2,6},{3,7},{4,8},{5,9},{6,10},{7,11},{8,12},{9,13},{1... | collective-permute-start | bytes 12296 | tf_op jit(solution)/shard_map/ppermute | solution.py:19
  127.6 1.2 collective-permute-start.20
  127.8 14.5 %collective-permute-start.23 = (bf16[64,4096]{1,0:T(8,128)(2,1)S(1)}, bf16[64,4096]{1,0:T(8,128)(2,1)S(1)}, u32[]{:S(2)}, u32[]{:S(2)}) collective-permute-start(bf16[64,4096]{1,0:T(8,128)(2,1)S(1)} %slice.112), channel_id=1, source_target_pairs={{0,64},{16,80},{32,96},{48,112},{64,0},{80,16},{96,32},{112,48},{1... | collective-permute-start | bytes 1572872 | tf_op jit(solution)/shard_map/ppermute | solution.py:31
  128.9 8.6 %copy-start.19 = (f32[8,128]{1,0:T(8,128)}, f32[8,128]{1,0:T(8,128)S(1)}, u32[]{:S(2)}) copy-start(f32[8,128]{1,0:T(8,128)S(1)} %concatenate.64.about_a.about) | copy-start | bytes 12292
  128.9 13.3 %collective-permute-start.22 = (f32[8,128]{1,0:T(8,128)S(1)}, f32[8,128]{1,0:T(8,128)S(1)}, u32[]{:S(2)}, u32[]{:S(2)}) collective-permute-start(f32[8,128]{1,0:T(8,128)S(1)} %concatenate.64.about_a.about), channel_id=1, source_target_pairs={{0,64},{16,80},{32,96},{48,112},{64,0},{80,16},{96,32},{112,48},{1... | collective-permute-start | bytes 12296 | tf_op jit(solution)/shard_map/ppermute | solution.py:31
  142.3 8.0 %copy-start.23 = (f32[8,128]{1,0:T(8,128)}, f32[8,128]{1,0:T(8,128)S(1)}, u32[]{:S(2)}) copy-start(f32[8,128]{1,0:T(8,128)S(1)} %collective-permute-done.22.about_b) | copy-start | bytes 12292
  142.3 8.0 %copy-start.9 = (bf16[64,4096]{1,0:T(8,128)(2,1)}, bf16[64,4096]{1,0:T(8,128)(2,1)S(1)}, u32[]{:S(2)}) copy-start(bf16[64,4096]{1,0:T(8,128)(2,1)S(1)} %collective-permute-done.23.rest_6_.q_c) | copy-start | bytes 1572868
  142.3 60.3 %collective-permute-start.27 = (bf16[256,4096]{1,0:T(8,128)(2,1)}, bf16[256,4096]{1,0:T(8,128)(2,1)S(1)}, u32[]{:S(2)}, u32[]{:S(2)}) collective-permute-start(bf16[256,4096]{1,0:T(8,128)(2,1)} %pool_part.2), channel_id=1, source_target_pairs={{0,2},{1,3},{2,0},{3,1},{4,6},{5,7},{6,4},{7,5},{8,10},{9,11},{10,... | collective-permute-start | bytes 6291464 | tf_op jit(solution)/shard_map/ppermute | solution.py:23
  154.6 29.4 %copy-start.25 = (bf16[128,4096]{1,0:T(8,128)(2,1)S(1)}, bf16[128,4096]{1,0:T(8,128)(2,1)}, u32[]{:S(2)}) copy-start(bf16[128,4096]{1,0:T(8,128)(2,1)} %get-tuple-element.70) | copy-start | bytes 3145732
  158.1 25.9 %collective-permute-start.28 = (bf16[64,4096]{1,0:T(8,128)(2,1)}, bf16[64,4096]{1,0:T(8,128)(2,1)S(1)}, u32[]{:S(2)}, u32[]{:S(2)}) collective-permute-start(bf16[64,4096]{1,0:T(8,128)(2,1)} %get-tuple-element.79), channel_id=1, source_target_pairs={{0,16},{16,32},{32,48},{48,0},{64,80},{80,96},{96,112},{112,64},{1... | collective-permute-start | bytes 1572872 | tf_op jit(solution)/shard_map/ppermute | solution.py:35
  158.2 27.7 %collective-permute-start.29 = (bf16[64,4096]{1,0:T(8,128)(2,1)}, bf16[64,4096]{1,0:T(8,128)(2,1)S(1)}, u32[]{:S(2)}, u32[]{:S(2)}) collective-permute-start(bf16[64,4096]{1,0:T(8,128)(2,1)} %get-tuple-element.80), channel_id=1, source_target_pairs={{0,32},{16,48},{32,0},{48,16},{64,96},{80,112},{96,64},{112,80},{1... | collective-permute-start | bytes 1572872 | tf_op jit(solution)/shard_map/ppermute | solution.py:35
  159.0 51.2 %collective-permute-start.24 = (bf16[128,4096]{1,0:T(8,128)(2,1)}, bf16[128,4096]{1,0:T(8,128)(2,1)S(1)}, u32[]{:S(2)}, u32[]{:S(2)}) collective-permute-start(bf16[128,4096]{1,0:T(8,128)(2,1)} %get-tuple-element.68), channel_id=1, source_target_pairs={{0,4},{1,5},{2,6},{3,7},{4,8},{5,9},{6,10},{7,11},{8,12},{9,13},{1... | collective-permute-start | bytes 3145736 | tf_op jit(solution)/shard_map/ppermute | solution.py:19
  159.8 50.4 %collective-permute-start.25 = (bf16[128,4096]{1,0:T(8,128)(2,1)}, bf16[128,4096]{1,0:T(8,128)(2,1)S(1)}, u32[]{:S(2)}, u32[]{:S(2)}) collective-permute-start(bf16[128,4096]{1,0:T(8,128)(2,1)} %get-tuple-element.69), channel_id=1, source_target_pairs={{0,8},{1,9},{2,10},{3,11},{4,12},{5,13},{6,14},{7,15},{8,0},{9,1},... | collective-permute-start | bytes 3145736 | tf_op jit(solution)/shard_map/ppermute | solution.py:19
  184.0 10.2 %copy-start.15 = (bf16[64,4096]{1,0:T(8,128)(2,1)}, bf16[64,4096]{1,0:T(8,128)(2,1)S(1)}, u32[]{:S(2)}) copy-start(bf16[64,4096]{1,0:T(8,128)(2,1)S(1)} %collective-permute-done.28.refs_1_) | copy-start | bytes 1572868
  184.1 26.2 %collective-permute-start.26 = (bf16[128,4096]{1,0:T(8,128)(2,1)S(1)}, bf16[128,4096]{1,0:T(8,128)(2,1)S(1)}, u32[]{:S(2)}, u32[]{:S(2)}) collective-permute-start(bf16[128,4096]{1,0:T(8,128)(2,1)S(1)} %copy-done.25), channel_id=1, source_target_pairs={{0,12},{1,13},{2,14},{3,15},{4,0},{5,1},{6,2},{7,3},{8,4},{9,5},{1... | collective-permute-start | bytes 3145736 | tf_op jit(solution)/shard_map/ppermute | solution.py:19
  185.9 8.4 %copy-start.16 = (bf16[64,4096]{1,0:T(8,128)(2,1)}, bf16[64,4096]{1,0:T(8,128)(2,1)S(1)}, u32[]{:S(2)}) copy-start(bf16[64,4096]{1,0:T(8,128)(2,1)S(1)} %collective-permute-done.29.refs_2_) | copy-start | bytes 1572868
  185.9 12.5 %collective-permute-start.30 = (bf16[64,4096]{1,0:T(8,128)(2,1)}, bf16[64,4096]{1,0:T(8,128)(2,1)S(1)}, u32[]{:S(2)}, u32[]{:S(2)}) collective-permute-start(bf16[64,4096]{1,0:T(8,128)(2,1)} %get-tuple-element.81), channel_id=1, source_target_pairs={{0,48},{16,0},{32,16},{48,32},{64,112},{80,64},{96,80},{112,96},{1... | collective-permute-start | bytes 1572872 | tf_op jit(solution)/shard_map/ppermute | solution.py:35
  198.4 0.8 copy-start.17
  202.6 1.3 copy-start.10
  210.2 1.0 copy-start.12
  210.2 1.4 copy-start.13
  210.3 1.7 copy-start.14

commit v2 on v1

--- a/solution.py
+++ b/solution.py
@@ -103,7 +103,8 @@
     ]
 
 
-def hard_kernel(bases, infos, before, *rest):
+def hard_kernel(bases, *rest):
+    infos, rest = rest[:8], rest[8:]
     q_refs = rest[:10]
     n1, n2, e1, e2, row_sum, s1, s2, codes, acc1, acc2, sq1, sq2 = rest[10:]
     k = pl.program_id(0)
@@ -121,11 +122,11 @@
     @pl.when(k == pl.num_programs(0) - 1)
     def _():
         for slot in range(8):
-            info = infos[slot].astype(f32)
+            info = infos[slot][...].astype(f32)
             code = info[0:8, 0:128] * 256.0 + info[8:16, 0:128]
             q_scale = info[0:1, 128:256] + info[1:2, 128:256] + info[2:3, 128:256]
             codes[slot] = jnp.concatenate([code[0:7], q_scale], axis=0)
-        sums = [before[0:1, :]] + [jnp.zeros((1, 128), f32) for _ in range(7)]
+        sums = [jnp.zeros((1, 128), f32) for _ in range(8)]
         for h, (acc, sq, e, s) in enumerate(((acc1, sq1, e1, s1), (acc2, sq2, e2, s2))):
             scale = inverse_norm(sq[...])
             s[...] = jnp.broadcast_to(scale, s.shape)
@@ -143,8 +144,9 @@
             row_sum[slot : slot + 1, :] = sums[slot]
 
 
-def hard_scores(bases, infos, before, q_refs, n1, n2, chunk=1024):
+def hard_scores(bases, q_refs, n1, n2, chunk=1024):
     rows, width = n1.shape
+    tails = [q for q in q_refs if q.shape[0] % 128 == 16 or q.shape[0] % 64 == 16]
     outs = (
         shape_of((rows, 1024), f32),
         shape_of((rows, 1024), f32),
@@ -156,7 +158,8 @@
     return pl.pallas_call(
         hard_kernel,
         grid=(width // chunk,),
-        in_specs=[smem_spec(), whole_spec(infos), whole_spec(before)]
+        in_specs=[smem_spec()]
+        + [pl.BlockSpec((16, 256), lambda k, at=x.shape[0] // 16 - 1: (at, 0)) for x in tails]
         + q_specs(q_refs, chunk)
         + [cols_spec(x, chunk) for x in (n1, *n2)],
         out_specs=[whole_spec(o) for o in outs],
@@ -165,25 +168,21 @@
         compiler_params=params(),
         cost_estimate=cost(4 * rows * 1024 * width, n1, *n2, *q_refs, *outs[:2]),
         name="hard_scores",
-    )(bases, infos, before, *q_refs, n1, *n2)
-
-
-def passage_rows(refs):
-    pc, p1, p2, p2x, p3 = [r[...] for r in refs]
-    near = [pc[:64], p1[:64], p2, p3[:64]]
-    far = [pc[64:], p1[64:], p2x, p3[64:]]
-    return jnp.concatenate(near + far, axis=0)
-
-
-def hot(places, pos, block):
-    rows = lax.broadcasted_iota(jnp.int32, (64, pos.shape[1]), 0).astype(f32)
-    return jnp.where(rows + places[block] == pos, 1.0, 0.0)
-
-
-def batch_kernel(places, about, *rest):
-    p_refs = rest[:5]
-    q_refs = rest[5:-5]
-    e, stats, scales, acc, sq = rest[-5:]
+    )(bases, *tails, *q_refs, n1, *n2)
+
+
+def hot(start, count, pos):
+    rows = lax.broadcasted_iota(jnp.int32, (count, pos.shape[1]), 0) + start
+    return jnp.where(rows.astype(f32) == pos, 1.0, 0.0)
+
+
+def hot_all(places, pos):
+    return jnp.concatenate([hot(places[block], 64, pos) for block in range(8)], axis=0)
+
+
+def batch_kernel(places, about, sums, p_all, *rest):
+    q_refs = rest[:-6]
+    e, total, stats, scales, acc, sq = rest[-6:]
     k = pl.program_id(0)
 
     @pl.when(k == 0)
@@ -191,9 +190,8 @@
         acc[...] = jnp.zeros_like(acc)
         sq[...] = jnp.zeros_like(sq)
 
-    p_all = passage_rows(p_refs)
-    acc[...] += dot_nt(p_all, stacked(q_refs))
-    sq[...] += lane_squares(p_all)
+    acc[...] += dot_nt(p_all[...], stacked(q_refs))
+    sq[...] += lane_squares(p_all[...])
 
     @pl.when(k == pl.num_programs(0) - 1)
     def _():
@@ -202,29 +200,32 @@
         score = acc[...] * (scale * inv_temp) * about[0:1, :]
         weight = jnp.exp(score)
         e[...] = weight
-        chosen = jnp.zeros((1, 128), f32)
-        for block in range(8):
-            part = score[block * 64 : block * 64 + 64]
-            chosen += jnp.sum(part * hot(places, about[1:2, :], block), axis=0, keepdims=True)
-        stats[0:1, :] = jnp.sum(weight, axis=0, keepdims=True)
-        stats[1:2, :] = chosen
-        stats[2:8, :] = jnp.zeros((6, 128), f32)
-
-
-def batch_scores(places, about, p_refs, q_refs):
-    width = q_refs[0].shape[1]
-    outs = (shape_of((512, 128), f32), shape_of((8, 128), f32), shape_of((512, 128), f32))
+        total[0:1, :] = sums[0:1, :] + jnp.sum(weight, axis=0, keepdims=True)
+        total[1:8, :] = sums[1:8, :]
+        chosen = score * hot_all(places, about[1:2, :])
+        stats[...] = jnp.broadcast_to(jnp.sum(chosen, axis=0, keepdims=True), stats.shape)
+
+
+def batch_scores(places, about, sums, p_all, q_refs):
+    rows, width = p_all.shape
+    outs = (
+        shape_of((rows, 128), f32),
+        shape_of((8, 128), f32),
+        shape_of((8, 128), f32),
+        shape_of((rows, 128), f32),
+    )
     return pl.pallas_call(
         batch_kernel,
         grid=(width // 2048,),
-        in_specs=[smem_spec(), whole_spec(about)] + [cols_spec(x) for x in (*p_refs, *q_refs)],
+        in_specs=[smem_spec(), whole_spec(about), whole_spec(sums)]
+        + [cols_spec(x) for x in (p_all, *q_refs)],
         out_specs=[whole_spec(o) for o in outs],
         out_shape=outs,
-        scratch_shapes=[pltpu.VMEM((512, 128), f32), pltpu.VMEM((512, 128), f32)],
-        compiler_params=params(),
-        cost_estimate=cost(2 * 512 * 128 * width, *q_refs, *p_refs, *outs),
+        scratch_shapes=[pltpu.VMEM((rows, 128), f32), pltpu.VMEM((rows, 128), f32)],
+        compiler_params=params(),
+        cost_estimate=cost(2 * rows * 128 * width, p_all, *q_refs, *outs),
         name="batch_scores",
-    )(places, about, *p_refs, *q_refs)
+    )(places, about, sums, p_all, *q_refs)
 
 
 def back_kernel(first, e1, e2, s1, s2, n1, n2, *rest):
@@ -301,70 +302,68 @@
     )(e, fac, *q_refs)
 
 
-def query_kernel(places, about, e, scales, *rest):
-    p_refs = rest[:5]
-    out, turned = rest[5:]
-
+def query_kernel(places, about, e, scales, p_all, out, turned):
     @pl.when(pl.program_id(0) == 0)
     def _():
-        for block in range(8):
-            rows = slice(block * 64, block * 64 + 64)
-            coef = e[rows, :] * about[0:1, :] - about[1:2, :] * hot(places, about[2:3, :], block)
-            turned[rows, :] = coef * scales[rows, 0:1]
-
-    turn = jnp.transpose(turned[...]).astype(bf16)
-    out[...] = dot_nn(turn, passage_rows(p_refs))
-
-
-def query_part(places, about, e, scales, p_refs):
-    width = p_refs[0].shape[1]
+        target = hot_all(places, about[2:3, :])
+        coef = (e[...] * about[0:1, :] - about[1:2, :] * target) * scales[:, 0:1]
+        turned[...] = jnp.transpose(coef).astype(bf16)
+
+    out[...] = dot_nn(turned[...], p_all[...])
+
+
+def query_part(places, about, e, scales, p_all):
+    rows, width = p_all.shape
     out = shape_of((128, width), f32)
     return pl.pallas_call(
         query_kernel,
         grid=(width // 2048,),
-        in_specs=[smem_spec(), whole_spec(about), whole_spec(e), whole_spec(scales)]
-        + [cols_spec(p) for p in p_refs],
+        in_specs=[smem_spec()] + [whole_spec(x) for x in (about, e, scales)] + [cols_spec(p_all)],
         out_specs=cols_spec(out),
         out_shape=out,
-        scratch_shapes=[pltpu.VMEM((512, 128), f32)],
-        compiler_params=params(),
-        cost_estimate=cost(2 * 512 * 128 * width, out, *p_refs),
+        scratch_shapes=[pltpu.VMEM((128, rows), bf16)],
+        compiler_params=params(),
+        cost_estimate=cost(2 * rows * 128 * width, out, p_all),
         name="query_part",
-    )(places, about, e, scales, *p_refs)
-
-
-def passage_kernel(places, about_a, about_b, e_a, e_b, q_a, q_b, q_c, home, d1, d2, d3, coef):
+    )(places, about, e, scales, p_all)
+
+
+def passage_kernel(turns, places, about_a, about_b, e_a, e_b, *rest):
+    home, d1, d2, d3, coef = rest[-5:]
+    q_refs = rest[:-5]
+
     @pl.when(pl.program_id(0) == 0)
     def _():
         for at, (about, e) in enumerate(((about_a, e_a), (about_b, e_b))):
             lanes = slice(at * 128, at * 128 + 128)
             for block in range(4):
-                rows = slice(block * 64, block * 64 + 64)
-                part = e[rows, :] * about[0:1, :] - about[1:2, :] * hot(places, about[2:3, :], block)
-                coef[rows, lanes] = (part * about[3:4, :]).astype(bf16)
-
-    part = dot_nn(coef[...], stacked([q_a, q_b, q_c]))
+                start = pl.multiple_of(turns[block] * 128, 128)
+                target = hot(places[2 * turns[block]], 64, about[2:3, :])
+                part = e[pl.ds(start, 64), :] * about[0:1, :] - about[1:2, :] * target
+                coef[block * 64 : block * 64 + 64, lanes] = (part * about[3:4, :]).astype(bf16)
+
+    part = dot_nn(coef[...], stacked(q_refs))
     home[...] = part[:64]
     for at, ref in enumerate((d1, d2, d3)):
         ref[...] = part[64 + at * 64 : 128 + at * 64].astype(bf16)
 
 
-def passage_part(places, about_a, about_b, e_a, e_b, q_a, q_b):
-    width = q_a.shape[1]
+def passage_part(turns, places, about_a, about_b, e_a, e_b, q_refs):
+    width = q_refs[0].shape[1]
     outs = (shape_of((64, width), f32),) + (shape_of((64, width), bf16),) * 3
-    near = pl.BlockSpec((256, 128), lambda k: (0, 0))
     return pl.pallas_call(
         passage_kernel,
         grid=(width // 2048,),
-        in_specs=[smem_spec(), whole_spec(about_a), whole_spec(about_b), near, near]
-        + [cols_spec(x) for x in (q_a, *q_b)],
+        in_specs=[smem_spec(), smem_spec()]
+        + [whole_spec(x) for x in (about_a, about_b, e_a, e_b)]
+        + [cols_spec(x) for x in q_refs],
         out_specs=[cols_spec(o) for o in outs],
         out_shape=outs,
         scratch_shapes=[pltpu.VMEM((256, 256), bf16)],
         compiler_params=params(),
-        cost_estimate=cost(2 * 256 * 256 * width, q_a, *q_b, *outs),
+        cost_estimate=cost(2 * 256 * 256 * width, *q_refs, *outs),
         name="passage_part",
-    )(places, about_a, about_b, e_a, e_b, q_a, *q_b)
+    )(turns, places, about_a, about_b, e_a, e_b, *q_refs)
 
 
 def last_kernel(n_parts, has_fac, *refs):
@@ -436,46 +435,38 @@
     px = hop_xl(passages)
     q1 = hop_z(message, -1)
     q3 = hop_z(message, 1)
+    pool_late, px_late, passages_late = after((pool, px, passages), px, message)
+    pool_x = (hop_xh(pool_late),)
+    pc = jnp.concatenate([passages_late, px_late], axis=0)
+    y_groups = [[l * 4 + y for y in range(4)] for l in range(2)]
+    p_all = lax.all_gather(pc, "loop", axis=0, tiled=True, axis_index_groups=y_groups)
     side0 = hop_core(message)
-    pool_late, passages_late = after((pool, passages), px)
-    pool_x = (hop_xh(pool_late),)
-    pc = jnp.concatenate([passages_late, px], axis=0)
-    p1 = hop_y(pc, -1)
-    p3 = hop_y(pc, 1)
-    q1_next, q3_next = after((q1, q3), pc)
-    q2a = hop_z(q1_next[:64], -1)
-    q2b = hop_z(q3_next[64:], 1)
-    p2 = hop_y(p1[:64], -1)
-    p2x = hop_y(p3[64:], 1)
+    q2a = hop_z(q1[:64], -1)
+    q2b = hop_z(q3[64:], 1)
     q1_late, q3_late = after((q1, q3), q2a, q2b)
     side1, side3 = hop_core(q1_late), hop_core(q3_late)
     side2a, side2b = hop_core(q2a), hop_core(q2b)
     q_refs = (message, q1, q2a, q2b, q3, side0, side1, side2a, side2b, side3)
-    p_refs = (pc, p1, p2, p2x, p3)
-    tails = (message[128:], q1[128:], q2b[64:], q3[128:], side0[128:], side1[128:], side2b[64:], side3[128:])
-    infos = jnp.stack([x[:, :256] for x in tails])
-
     bases = jnp.stack([grp * n_pool, (grp ^ 2) * n_pool]).astype(f32)
     steps = jnp.arange(4, dtype=jnp.int32)
-    y_places = (yi + steps) % 4
-    places = (
-        jnp.concatenate([xl * 4 + y_places, (1 - xl) * 4 + y_places]) * passages.shape[0]
-    ).astype(f32)
+    turns = (yi + steps) % 4
+    places = jnp.stack([xl * 4 + steps, (1 - xl) * 4 + steps], axis=1).reshape(8) * passages.shape[0]
     pos = positive.astype(f32)
     about_first = jnp.concatenate([q_scale[None], pos[None], jnp.tile(zero_row, (6, 1))], axis=0)
 
-    e_batch, stats, p_scales = batch_scores(places, about_first, p_refs, (queries,))
-    e1, e2, part, s1, s2, codes = hard_scores(bases, infos, stats, q_refs, pool, pool_x)
+    e1, e2, hard_sums, s1, s2, codes = hard_scores(bases, q_refs, pool, pool_x)
     q_late, about_late = after((queries, about_first), pool_x[0])
     q_xa = hop_xl(q_late[:64])
     about_first_x = hop_xl(about_late)
-
-    (e1_side, e2_side) = after((e1, e2), part, q_xa, about_first_x)
+    (e1_side,) = after((e1,), q_xa, about_first_x)
     (q_later,) = after((queries,), q_xa)
     q_xb = hop_xl(q_later[64:])
+    (u_side,) = hard_back(1, e1_side, e2, s1, s2, pool, pool_x)
+    u_got = hop_core(u_side)
+    (hard_sums,) = after((hard_sums,), u_side)
+    e_batch, part, chosen, p_scales = batch_scores(places, about_first, hard_sums, p_all, (queries,))
+
     got = [hop_z(part, -by) for by in (1, 2, 3)]
-    (u_side,) = hard_back(1, e1_side, e2_side, s1, s2, pool, pool_x)
-    u_got = hop_core(u_side)
     got, _ = lax.optimization_barrier((got, u_side))
     total = part.reshape(2, 4, n_query)
     for by in (1, 2, 3):
@@ -485,7 +476,7 @@
     live = (codes[:, 0, :] >= 0).astype(f32)
     fac = live * codes[:, 7, :] / total.reshape(8, n_query)
     own_total = total[0, 0]
-    loss = valid * (jnp.log(own_total) - stats[1])
+    loss = valid * (jnp.log(own_total) - chosen[0])
     own_fac = valid / own_total
     about = jnp.concatenate(
         [own_fac[None], valid[None], pos[None], q_scale[None], jnp.tile(zero_row, (4, 1))], axis=0
@@ -498,20 +489,24 @@
     (u_got,) = after((u_got,), dn_far)
     u_home, u1, u2, u3 = hard_back(0, e1, e2, s1, s2, pool, pool_x, u_got)
     u_parts = (u_home, hop_z(u1, 1), hop_z(u2, 2), hop_z(u3, -1))
-    q_x = after((q_xa, q_xb), u_home)
-    e_batch_x, _, _ = batch_scores(places, about_first_x, p_refs, q_x)
-    d_home, d1, d2, d3 = passage_part(places, about, about_x, e_batch, e_batch_x, queries, q_x)
-    d_parts = (d_home, hop_y(d1, 1), hop_y(d2, 2), hop_y(d3, -1))
-
-    (e1_late, e_late) = after((e1, e_batch), d_home)
+    q_xa, q_xb = after((q_xa, q_xb), u_home)
+    e_batch_x, _, _, _ = batch_scores(places, about_first_x, hard_sums, p_all, (q_xa, q_xb))
+    d_home, d1, d2, d3 = passage_part(
+        turns, places, about, about_x, e_batch, e_batch_x, (queries, q_xa, q_xb)
+    )
+    (e1_late,) = after((e1,), d_home)
     dn_home = pool_part(e1_late, fac, q_refs, f32)
-    dq_batch = query_part(places, about, e_late, p_scales, p_refs)
-    grad_passage = last_step(d_parts, passages)
+    (e_late,) = after((e_batch,), dn_home)
+    dq_batch = query_part(places, about, e_late, p_scales, p_all)
     fac_rows = jnp.broadcast_to(own_fac[:, None], (n_query, 128))
-    (dn_x,) = after((dn_x,), grad_passage)
+    d_one = hop_y(d1, 1)
     grad_pool = last_step((dn_home, dn_x), pool)
-    (dq_batch,) = after((dq_batch,), grad_pool)
+    (d2, d3, dq_batch) = after((d2, d3, dq_batch), grad_pool, d_one)
+    d_two = hop_y(d2, 2)
+    d_three = hop_y(d3, -1)
     grad_query = last_step(u_parts, queries, fac_rows, dq_batch)
+    (d_one, d_two, d_three), _ = lax.optimization_barrier(((d_one, d_two, d_three), grad_query))
+    grad_passage = last_step((d_home, d_one, d_two, d_three), passages)
     return (loss, grad_query, grad_passage, grad_pool)
 
 

time: 218 us -> 221 us (1.014)
  waiting for transfers between devices: 94.6 us -> 77.5 us
  between operations: 1.72 us -> 15 us
  starting transfers between devices: 29.7 us -> 34.8 us
  Pallas kernels: 70.2 us -> 73.7 us
  local copies, waits for them, and re-layouts: 11.5 us -> 8.88 us
    ppermute x7 -> x3, waiting for transfers between devices: 36.4 us -> 13.5 us  [hop_y(): lax.ppermute(x, 'loop', [(l, (l & 4) + (l + by) % 4) for l in range(8)])]
    ppermute x2, waiting for transfers between devices: 0.01 us -> 15.4 us  [hop_xh(): return lax.ppermute(x, 'grp', [(g, g ^ 2) for g in range(16)])]
    ppermute x10, waiting for transfers between devices: 50.7 us -> 38.2 us  [hop_z(): return lax.ppermute(x, 'grp', [(g, (g + 4 * by) % 16) for g in range(16)])]
    pallas_call x2, Pallas kernels: 8.6 us -> 12.3 us  [batch_scores(): pl.pallas_call(batch_kernel, grid=(width // 2048,), in_specs=[smem_spec()...]
    ppermute x5, waiting for transfers between devices: 6.75 us -> 10.4 us  [hop_xl(): return lax.ppermute(x, 'loop', [(l, l ^ 4) for l in range(8)])]
    ppermute x2, starting transfers between devices: 3.61 us -> 6.09 us  [hop_xh(): return lax.ppermute(x, 'grp', [(g, g ^ 2) for g in range(16)])]
    ppermute x10, starting transfers between devices: 13.2 us -> 15.6 us  [hop_z(): return lax.ppermute(x, 'grp', [(g, (g + 4 * by) % 16) for g in range(16)])]
    unnamed x61 -> x50, local copies, waits for them, and re-layouts: 6.47 us -> 5.01 us
  transfers between devices with their start and end apart: 31 -> 28, of which waited for: 12 -> 11; matrix products, arithmetic and copies ran while one was open for 7% -> 6% of each run, Pallas kernels for 27% -> 32%
where the time goes in v2:
time: 221 us; the launch traced here: 220 us
  waiting for transfers between devices  77.5 us (35%)
  Pallas kernels  73.7 us (33%)
  starting transfers between devices  34.8 us (16%)
  between operations  15 us (7%)
  other arithmetic  10.1 us (5%)
  local copies, waits for them, and re-layouts  8.88 us (4%)
    ppermute x10, waiting for transfers between devices, hop_z(): return lax.ppermute(x, 'grp', [(g, (g + 4 * by) % 16) for g in range(16)])  38.2 us
    ppermute x10, starting transfers between devices, hop_z(): return lax.ppermute(x, 'grp', [(g, (g + 4 * by) % 16) for g in range(16)])  15.6 us
    ppermute x2, waiting for transfers between devices, hop_xh(): return lax.ppermute(x, 'grp', [(g, g ^ 2) for g in range(16)])  15.4 us
    pallas_call x3, Pallas kernels, last_step(): pl.pallas_call(functools.partial(last_kernel, len(parts), fac is not None...  14.7 us
    pallas_call x2, Pallas kernels, pool_part(): pl.pallas_call(pool_kernel, grid=(width // 2048,), in_specs=[whole_spec(e...  14.1 us
    ppermute x3, waiting for transfers between devices, hop_y(): lax.ppermute(x, 'loop', [(l, (l & 4) + (l + by) % 4) for l in range(8)])  13.5 us
    pallas_call x2, Pallas kernels, hard_back(): pl.pallas_call(functools.partial(back_kernel, first), grid=(width // 2048...  13.3 us
    pallas_call x2, Pallas kernels, batch_scores(): pl.pallas_call(batch_kernel, grid=(width // 2048,), in_specs=[smem_spec()...  12.3 us
  transfers between devices with their start and end apart: 28, of which 11 were waited for; matrix products, arithmetic and copies ran while one was open for 6% of the time, Pallas kernels for 32%

profile of v2, /device:TPU:0, one launch (start us, length us, event | category | flops | bytes accessed | tf_op | source)
XLA Modules:
  0.0 220.0 jit_solution(11516606918041334509)
XLA Ops:
  7.2 1.7 collective-permute-start.9
  9.5 1.5 multiply_reduce_fusion
  11.1 0.7 fusion.20
  11.8 0.7 fusion.19
  12.5 2.4 %pad_maximum_fusion.rest_0_.rest_8_ = bf16[144,4096]{1,0:T(8,128)(2,1)} fusion(bf16[16,4096]{1,0:T(8,128)(2,1)S(1)} %fusion.11, bf16[128,4096]{1,0:T(8,128)(2,1)} %refs_6_.1), kind=kLoop, calls=%fused_computation.1 | loop fusion | flops 2359296 | bytes 2359296 | tf_op jit(solution)/shard_map/concatenate | solution.py:433
  14.9 6.2 %collective-permute-done.9 = bf16[64,4096]{1,0:T(8,128)(2,1)S(1)} collective-permute-done((bf16[64,4096]{1,0:T(8,128)(2,1)}, bf16[64,4096]{1,0:T(8,128)(2,1)S(1)}, u32[]{:S(2)}, u32[]{:S(2)}) %collective-permute-start.9) | collective-permute-done | bytes 524320 | tf_op jit(solution)/shard_map/ppermute | solution.py:31
  21.0 1.1 pad_maximum_fusion.1
  22.1 2.2 %collective-permute-start.1 = (bf16[144,4096]{1,0:T(8,128)(2,1)}, bf16[144,4096]{1,0:T(8,128)(2,1)}, u32[]{:S(2)}, u32[]{:S(2)}) collective-permute-start(bf16[144,4096]{1,0:T(8,128)(2,1)} %pad_maximum_fusion.rest_0_.rest_8_), channel_id=1, source_target_pairs={{0,4},{1,5},{2,6},{3,7},{4,8},{5,9},{6,10},{7,11},{8,12},{9,13},{1... | collective-permute-start | bytes 3538952 | tf_op jit(solution)/shard_map/ppermute | solution.py:19
  24.3 2.2 %collective-permute-start = (bf16[144,4096]{1,0:T(8,128)(2,1)}, bf16[144,4096]{1,0:T(8,128)(2,1)}, u32[]{:S(2)}, u32[]{:S(2)}) collective-permute-start(bf16[144,4096]{1,0:T(8,128)(2,1)} %pad_maximum_fusion.rest_0_.rest_8_), channel_id=1, source_target_pairs={{0,12},{1,13},{2,14},{3,15},{4,0},{5,1},{6,2},{7,3},{8,4},{9,5},{1... | collective-permute-start | bytes 3538952 | tf_op jit(solution)/shard_map/ppermute | solution.py:19
  26.5 3.0 %collective-permute-start.10 = (bf16[256,4096]{1,0:T(8,128)(2,1)S(1)}, bf16[256,4096]{1,0:T(8,128)(2,1)S(1)}, u32[]{:S(2)}, u32[]{:S(2)}) collective-permute-start(bf16[256,4096]{1,0:T(8,128)(2,1)S(1)} %copy-done.2), channel_id=1, source_target_pairs={{0,2},{1,3},{2,0},{3,1},{4,6},{5,7},{6,4},{7,5},{8,10},{9,11},{10,... | collective-permute-start | bytes 6291464 | tf_op jit(solution)/shard_map/ppermute | solution.py:23
  29.6 22.3 %collective-permute-done.1.rest_3_.rest_12_.rest_4_ = bf16[144,4096]{1,0:T(8,128)(2,1)} collective-permute-done((bf16[144,4096]{1,0:T(8,128)(2,1)}, bf16[144,4096]{1,0:T(8,128)(2,1)}, u32[]{:S(2)}, u32[]{:S(2)}) %collective-permute-start.1) | collective-permute-done | bytes 1179680 | tf_op jit(solution)/shard_map/ppermute | solution.py:19
  51.9 1.1 slice.62
  53.1 1.1 slice.63
  54.2 3.3 %collective-permute-start.4 = (bf16[64,4096]{1,0:T(8,128)(2,1)S(1)}, bf16[64,4096]{1,0:T(8,128)(2,1)}, u32[]{:S(2)}, u32[]{:S(2)}) collective-permute-start(bf16[64,4096]{1,0:T(8,128)(2,1)S(1)} %slice.63), channel_id=1, source_target_pairs={{0,12},{1,13},{2,14},{3,15},{4,0},{5,1},{6,2},{7,3},{8,4},{9,5},{1... | collective-permute-start | bytes 1572872 | tf_op jit(solution)/shard_map/ppermute | solution.py:19
  57.6 9.3 %collective-permute-done.4.rest_10_.rest_2_ = bf16[64,4096]{1,0:T(8,128)(2,1)} collective-permute-done((bf16[64,4096]{1,0:T(8,128)(2,1)S(1)}, bf16[64,4096]{1,0:T(8,128)(2,1)}, u32[]{:S(2)}, u32[]{:S(2)}) %collective-permute-start.4) | collective-permute-done | bytes 524320 | tf_op jit(solution)/shard_map/ppermute | solution.py:19
  66.9 2.5 %collective-permute-done.2.rest_2_.rest_11_.rest_3_ = bf16[80,4096]{1,0:T(8,128)(2,1)} collective-permute-done((bf16[80,4096]{1,0:T(8,128)(2,1)S(1)}, bf16[80,4096]{1,0:T(8,128)(2,1)}, u32[]{:S(2)}, u32[]{:S(2)}) %collective-permute-start.2) | collective-permute-done | bytes 655392 | tf_op jit(solution)/shard_map/ppermute | solution.py:19
  69.4 0.5 collective-permute-start.7
  70.0 4.3 %collective-permute-done.10.rest_19_.n2 = bf16[256,4096]{1,0:T(8,128)(2,1)S(1)} collective-permute-done((bf16[256,4096]{1,0:T(8,128)(2,1)S(1)}, bf16[256,4096]{1,0:T(8,128)(2,1)S(1)}, u32[]{:S(2)}, u32[]{:S(2)}) %collective-permute-start.10) | collective-permute-done | bytes 2097184 | tf_op jit(solution)/shard_map/ppermute | solution.py:23
  74.4 1.2 copy-done.4
  75.6 1.5 collective-permute-start.11
  77.1 0.5 collective-permute-start.12
  77.7 0.6 add_convert_fusion.bases
  78.3 0.8 copy-done.6
  79.1 11.7 %hard_scores.1 = (f32[256,1024]{1,0:T(8,128)}, f32[256,1024]{1,0:T(8,128)}, f32[8,128]{1,0:T(8,128)}, f32[256,128]{1,0:T(8,128)}, f32[256,128]{1,0:T(8,128)}, /*index=5*/f32[8,8,128]{2,1,0:T(8,128)}) custom-call(f32[2]{0:T(128)} %add_convert_fusion.bases, bf16[144,4096]{1,0:T(8,128)(2,1)} %pad_maximum_fusion.rest_0_.rest_8_, ...), custom_call_target="tpu_custom_call" | custom-call | flops 1 | bytes 1 | tf_op jit(solution)/shard_map/hard_scores/pallas_call | solution.py:158
  90.9 6.3 %hard_back.2 = bf16[512,4096]{1,0:T(8,128)(2,1)} custom-call(f32[256,1024]{1,0:T(8,128)} %get-tuple-element.82.e1.e, f32[256,1024]{1,0:T(8,128)} %get-tuple-element.56.e2.e, f32[256,128]{1,0:T(8,128)} %get-tuple-element.57.s1, f32[256,128]{1,0:T(8,128)} %get-tuple-element.58.s2, bf16[256,4096]{1,0:T(8,128)(2,1)} %refs_2_.1, bf16[256,4096]{1,0:T(8,128)(2,1)} %copy-done.5), custom_call_target="tpu_custom_call" | custom-call | flops 1 | bytes 1 | tf_op jit(solution)/shard_map/hard_back/pallas_call | solution.py:261
  97.3 0.6 mul.31.places
  97.9 6.2 %batch_scores.2 = (f32[512,128]{1,0:T(8,128)}, f32[8,128]{1,0:T(8,128)}, f32[8,128]{1,0:T(8,128)}, f32[512,128]{1,0:T(8,128)}) custom-call(s32[8]{0:T(128)} %mul.31.places, f32[8,128]{1,0:T(8,128)} %copy-done.19, f32[8,128]{1,0:T(8,128)} %get-tuple-element.59.sums, bf16[512,4096]{1,0:T(8,128)(2,1)} %all-gather.2.cloned.1.call-done.p_all, ...), custom_call_target="tpu_custom_call" | custom-call | flops 1 | bytes 1 | tf_op jit(solution)/shard_map/batch_scores/pallas_call | solution.py:217
  104.1 1.8 collective-permute-start.13
  106.0 0.1 collective-permute-start.14
  106.1 1.1 collective-permute-start.15
  107.2 0.9 collective-permute-done.13
  108.1 3.2 %collective-permute-done.14 = f32[8,128]{1,0:T(8,128)S(1)} collective-permute-done((f32[8,128]{1,0:T(8,128)}, f32[8,128]{1,0:T(8,128)S(1)}, u32[]{:S(2)}, u32[]{:S(2)}) %collective-permute-start.14) | collective-permute-done | bytes 4128 | tf_op jit(solution)/shard_map/ppermute | solution.py:19
  111.3 0.7 fusion.18
  112.2 1.6 collective-permute-start.19
  113.8 1.1 collective-permute-start.18
  114.9 0.6 fusion.16.fac
  115.5 6.9 %pool_part.2 = bf16[256,4096]{1,0:T(8,128)(2,1)} custom-call(f32[256,1024]{1,0:T(8,128)} %get-tuple-element.56.e2.e, f32[8,128]{1,0:T(8,128)} %fusion.16.fac, bf16[144,4096]{1,0:T(8,128)(2,1)} %pad_maximum_fusion.rest_0_.rest_8_, bf16[144,4096]{1,0:T(8,128)(2,1)} %collective-permute-done.rest_1_.rest_9_, ...), custom_call_target="tpu_custom_call" | custom-call | flops 1 | bytes 1 | tf_op jit(solution)/shard_map/pool_part/pallas_call | solution.py:292
  122.4 4.2 %collective-permute-done.19.rest_1_.rest_2_ = bf16[64,4096]{1,0:T(8,128)(2,1)S(1)} collective-permute-done((bf16[64,4096]{1,0:T(8,128)(2,1)S(1)}, bf16[64,4096]{1,0:T(8,128)(2,1)S(1)}, u32[]{:S(2)}, u32[]{:S(2)}) %collective-permute-start.19) | collective-permute-done | bytes 524320 | tf_op jit(solution)/shard_map/ppermute | solution.py:31
  126.7 3.1 %collective-permute-start.23 = (bf16[256,4096]{1,0:T(8,128)(2,1)}, bf16[256,4096]{1,0:T(8,128)(2,1)S(1)}, u32[]{:S(2)}, u32[]{:S(2)}) collective-permute-start(bf16[256,4096]{1,0:T(8,128)(2,1)} %pool_part.2), channel_id=1, source_target_pairs={{0,2},{1,3},{2,0},{3,1},{4,6},{5,7},{6,4},{7,5},{8,10},{9,11},{10,... | collective-permute-start | bytes 6291464 | tf_op jit(solution)/shard_map/ppermute | solution.py:23
  129.7 0.5 and_select_fusion.turns
  130.3 7.1 %hard_back.3 = (f32[128,4096]{1,0:T(8,128)}, bf16[128,4096]{1,0:T(8,128)(2,1)}, bf16[128,4096]{1,0:T(8,128)(2,1)}, bf16[128,4096]{1,0:T(8,128)(2,1)}) custom-call(f32[256,1024]{1,0:T(8,128)} %get-tuple-element.82.e1.e, f32[256,1024]{1,0:T(8,128)} %get-tuple-element.56.e2.e, f32[256,128]{1,0:T(8,128)} %get-tuple-element.57.s1, ...), custom_call_target="tpu_custom_call" | custom-call | flops 1 | bytes 1 | tf_op jit(solution)/shard_map/hard_back/pallas_call | solution.py:261
  137.4 0.4 collective-permute-start.20
  137.8 2.6 %collective-permute-start.21 = (bf16[128,4096]{1,0:T(8,128)(2,1)}, bf16[128,4096]{1,0:T(8,128)(2,1)S(1)}, u32[]{:S(2)}, u32[]{:S(2)}) collective-permute-start(bf16[128,4096]{1,0:T(8,128)(2,1)} %get-tuple-element.73), channel_id=1, source_target_pairs={{0,8},{1,9},{2,10},{3,11},{4,12},{5,13},{6,14},{7,15},{8,0},{9,1},... | collective-permute-start | bytes 3145736 | tf_op jit(solution)/shard_map/ppermute | solution.py:19
  140.4 6.1 %batch_scores.3 = (f32[512,128]{1,0:T(8,128)}, f32[8,128]{1,0:T(8,128)}, f32[8,128]{1,0:T(8,128)}, f32[512,128]{1,0:T(8,128)}) custom-call(s32[8]{0:T(128)} %mul.31.places, f32[8,128]{1,0:T(8,128)} %copy-done.21, f32[8,128]{1,0:T(8,128)} %get-tuple-element.59.sums, bf16[512,4096]{1,0:T(8,128)(2,1)} %all-gather.2.cloned.1.call-done.p_all, ...), custom_call_target="tpu_custom_call" | custom-call | flops 1 | bytes 1 | tf_op jit(solution)/shard_map/batch_scores/pallas_call | solution.py:217
  146.5 3.6 %passage_part.1 = (f32[64,4096]{1,0:T(8,128)}, bf16[64,4096]{1,0:T(8,128)(2,1)}, bf16[64,4096]{1,0:T(8,128)(2,1)}, bf16[64,4096]{1,0:T(8,128)(2,1)}) custom-call(s32[4]{0:T(128)} %and_select_fusion.turns, s32[8]{0:T(128)} %mul.31.places, f32[8,128]{1,0:T(8,128)} %copy-done.17, f32[8,128]{1,0:T(8,128)} %copy-done.20, f32[512,128]{1,0:T(8,128)} %get-tuple-element.83.e_a.e, ...), custom_call_target="tpu_custom_call" | custom-call | flops 1 | bytes 1 | tf_op jit(solution)/shard_map/passage_part/pallas_call | solution.py:354
  150.1 1.6 collective-permute-start.24
  151.7 1.6 collective-permute-start.22
  153.4 7.2 %pool_part.3.refs_0_ = f32[256,4096]{1,0:T(8,128)} custom-call(f32[256,1024]{1,0:T(8,128)} %get-tuple-element.82.e1.e, f32[8,128]{1,0:T(8,128)} %fusion.16.fac, bf16[144,4096]{1,0:T(8,128)(2,1)} %pad_maximum_fusion.rest_0_.rest_8_, bf16[144,4096]{1,0:T(8,128)(2,1)} %collective-permute-done.rest_1_.rest_9_, ...), custom_call_target="tpu_custom_call" | custom-call | flops 1 | bytes 1 | tf_op jit(solution)/shard_map/pool_part/pallas_call | solution.py:292
  160.6 3.9 %query_part.1.refs_5_ = f32[128,4096]{1,0:T(8,128)} custom-call(s32[8]{0:T(128)} %mul.31.places, f32[8,128]{1,0:T(8,128)} %copy-done.17, f32[512,128]{1,0:T(8,128)} %get-tuple-element.83.e_a.e, f32[512,128]{1,0:T(8,128)} %get-tuple-element.84.scales, bf16[512,4096]{1,0:T(8,128)(2,1)} %all-gather.2.cloned.1.call-done.p_all), custom_call_target="tpu_custom_call" | custom-call | flops 1 | bytes 1 | tf_op jit(solution)/shard_map/query_part/pallas_call | solution.py:318
  164.5 11.1 %collective-permute-done.23.refs_1_ = bf16[256,4096]{1,0:T(8,128)(2,1)S(1)} collective-permute-done((bf16[256,4096]{1,0:T(8,128)(2,1)}, bf16[256,4096]{1,0:T(8,128)(2,1)S(1)}, u32[]{:S(2)}, u32[]{:S(2)}) %collective-permute-start.23) | collective-permute-done | bytes 2097184 | tf_op jit(solution)/shard_map/ppermute | solution.py:23
  175.6 1.3 copy-done.7
  176.9 6.3 %last_step.3 = f32[256,4096]{1,0:T(8,128)} custom-call(f32[256,4096]{1,0:T(8,128)} %pool_part.3.refs_0_, bf16[256,4096]{1,0:T(8,128)(2,1)} %copy-done.7, bf16[256,4096]{1,0:T(8,128)(2,1)} %refs_2_.1), custom_call_target="tpu_custom_call" | custom-call | flops 1 | bytes 1 | tf_op jit(solution)/shard_map/last_step/pallas_call | solution.py:401
  183.2 3.3 %collective-permute-start.25 = (bf16[64,4096]{1,0:T(8,128)(2,1)S(1)}, bf16[64,4096]{1,0:T(8,128)(2,1)S(1)}, u32[]{:S(2)}, u32[]{:S(2)}) collective-permute-start(bf16[64,4096]{1,0:T(8,128)(2,1)S(1)} %copy-done.23), channel_id=1, source_target_pairs={{0,32},{16,48},{32,0},{48,16},{64,96},{80,112},{96,64},{112,80},{1... | collective-permute-start | bytes 1572872 | tf_op jit(solution)/shard_map/ppermute | solution.py:35
  186.5 1.1 collective-permute-start.26
  187.6 1.2 fusion.21
  188.8 0.9 broadcast_in_dim.19.refs_4_
  189.7 0.1 copy-done.11
  189.8 0.4 copy-done.12
  190.2 0.3 copy-done.13
  190.5 5.0 %last_step.4 = f32[128,4096]{1,0:T(8,128)} custom-call(f32[128,4096]{1,0:T(8,128)} %get-tuple-element.71.refs_0_, bf16[128,4096]{1,0:T(8,128)(2,1)} %copy-done.11, bf16[128,4096]{1,0:T(8,128)(2,1)} %copy-done.12, bf16[128,4096]{1,0:T(8,128)(2,1)} %copy-done.13, f32[128,128]{1,0:T(8,128)} %broadcast_in_dim.19.refs_4_, f32[128,4096]{1,0:T(8,128)} %query_part.1.refs_5_, ...), custom_call_target="tpu_custom_call" | custom-call | flops 1 | bytes 1 | tf_op jit(solution)/shard_map/last_step/pallas_call | solution.py:401
  195.5 1.9 collective-permute-done.25.refs_2_
  197.4 11.6 %collective-permute-done.26.refs_3_ = bf16[64,4096]{1,0:T(8,128)(2,1)S(1)} collective-permute-done((bf16[64,4096]{1,0:T(8,128)(2,1)S(1)}, bf16[64,4096]{1,0:T(8,128)(2,1)S(1)}, u32[]{:S(2)}, u32[]{:S(2)}) %collective-permute-start.26) | collective-permute-done | bytes 524320 | tf_op jit(solution)/shard_map/ppermute | solution.py:35
  209.0 0.8 copy-done.16
  209.8 3.4 %last_step.5 = f32[64,4096]{1,0:T(8,128)} custom-call(f32[64,4096]{1,0:T(8,128)} %get-tuple-element.81.refs_0_, bf16[64,4096]{1,0:T(8,128)(2,1)} %copy-done.14, bf16[64,4096]{1,0:T(8,128)(2,1)} %copy-done.15, bf16[64,4096]{1,0:T(8,128)(2,1)} %copy-done.16, bf16[64,4096]{1,0:T(8,128)(2,1)} %refs_4_.1), custom_call_target="tpu_custom_call" | custom-call | flops 1 | bytes 1 | tf_op jit(solution)/shard_map/last_step/pallas_call | solution.py:401
  (93 shorter events, 1.0 us)
Async XLA Ops:
  7.2 13.8 %copy-start.10 = (bf16[64,4096]{1,0:T(8,128)(2,1)S(1)}, bf16[64,4096]{1,0:T(8,128)(2,1)}, u32[]{:S(2)}) copy-start(bf16[64,4096]{1,0:T(8,128)(2,1)} %refs_4_.1) | copy-start | bytes 1572868
  7.2 90.8 %all-gather.2.cloned.1.call-start = ((), (), s32[]{:S(2)}) async-start(), calls=%async_computation | async-start | bytes 5242880 | tf_op jit(solution)/shard_map/all_gather | solution.py:442
  7.2 13.8 %collective-permute-start.9 = (bf16[64,4096]{1,0:T(8,128)(2,1)}, bf16[64,4096]{1,0:T(8,128)(2,1)S(1)}, u32[]{:S(2)}, u32[]{:S(2)}) collective-permute-start(bf16[64,4096]{1,0:T(8,128)(2,1)} %refs_4_.1), channel_id=1, source_target_pairs={{0,64},{16,80},{32,96},{48,112},{64,0},{80,16},{96,32},{112,48},{1... | collective-permute-start | bytes 1572872 | tf_op jit(solution)/shard_map/ppermute | solution.py:31
  14.9 11.7 %copy-start.2 = (bf16[256,4096]{1,0:T(8,128)(2,1)S(1)}, bf16[256,4096]{1,0:T(8,128)(2,1)}, u32[]{:S(2)}) copy-start(bf16[256,4096]{1,0:T(8,128)(2,1)} %refs_2_.1) | copy-start | bytes 6291460
  22.1 47.8 %copy-start.24 = (s32[128]{0:T(128)S(1)}, s32[128]{0:T(128)}, u32[]{:S(2)}) copy-start(s32[128]{0:T(128)} %param.11) | copy-start | bytes 1540
  22.1 52.3 %copy-start = (bf16[128,4096]{1,0:T(8,128)(2,1)S(1)}, bf16[128,4096]{1,0:T(8,128)(2,1)}, u32[]{:S(2)}) copy-start(bf16[128,4096]{1,0:T(8,128)(2,1)} %refs_6_.1) | copy-start | bytes 3145732
  22.1 35.4 %copy-start.3 = (bf16[144,4096]{1,0:T(8,128)(2,1)S(1)}, bf16[144,4096]{1,0:T(8,128)(2,1)}, u32[]{:S(2)}) copy-start(bf16[144,4096]{1,0:T(8,128)(2,1)} %pad_maximum_fusion.rest_0_.rest_8_) | copy-start | bytes 3538948
  22.1 29.8 %collective-permute-start.1 = (bf16[144,4096]{1,0:T(8,128)(2,1)}, bf16[144,4096]{1,0:T(8,128)(2,1)}, u32[]{:S(2)}, u32[]{:S(2)}) collective-permute-start(bf16[144,4096]{1,0:T(8,128)(2,1)} %pad_maximum_fusion.rest_0_.rest_8_), channel_id=1, source_target_pairs={{0,4},{1,5},{2,6},{3,7},{4,8},{5,9},{6,10},{7,11},{8,12},{9,13},{1... | collective-permute-start | bytes 3538952 | tf_op jit(solution)/shard_map/ppermute | solution.py:19
  24.3 28.8 %collective-permute-start = (bf16[144,4096]{1,0:T(8,128)(2,1)}, bf16[144,4096]{1,0:T(8,128)(2,1)}, u32[]{:S(2)}, u32[]{:S(2)}) collective-permute-start(bf16[144,4096]{1,0:T(8,128)(2,1)} %pad_maximum_fusion.rest_0_.rest_8_), channel_id=1, source_target_pairs={{0,12},{1,13},{2,14},{3,15},{4,0},{5,1},{6,2},{7,3},{8,4},{9,5},{1... | collective-permute-start | bytes 3538952 | tf_op jit(solution)/shard_map/ppermute | solution.py:19
  26.5 47.7 %collective-permute-start.10 = (bf16[256,4096]{1,0:T(8,128)(2,1)S(1)}, bf16[256,4096]{1,0:T(8,128)(2,1)S(1)}, u32[]{:S(2)}, u32[]{:S(2)}) collective-permute-start(bf16[256,4096]{1,0:T(8,128)(2,1)S(1)} %copy-done.2), channel_id=1, source_target_pairs={{0,2},{1,3},{2,0},{3,1},{4,6},{5,7},{6,4},{7,5},{8,10},{9,11},{10,... | collective-permute-start | bytes 6291464 | tf_op jit(solution)/shard_map/ppermute | solution.py:23
  53.0 16.3 %collective-permute-start.2 = (bf16[80,4096]{1,0:T(8,128)(2,1)S(1)}, bf16[80,4096]{1,0:T(8,128)(2,1)}, u32[]{:S(2)}, u32[]{:S(2)}) collective-permute-start(bf16[80,4096]{1,0:T(8,128)(2,1)S(1)} %slice.62), channel_id=1, source_target_pairs={{0,4},{1,5},{2,6},{3,7},{4,8},{5,9},{6,10},{7,11},{8,12},{9,13},{1... | collective-permute-start | bytes 1966088 | tf_op jit(solution)/shard_map/ppermute | solution.py:19
  54.2 12.7 %collective-permute-start.4 = (bf16[64,4096]{1,0:T(8,128)(2,1)S(1)}, bf16[64,4096]{1,0:T(8,128)(2,1)}, u32[]{:S(2)}, u32[]{:S(2)}) collective-permute-start(bf16[64,4096]{1,0:T(8,128)(2,1)S(1)} %slice.63), channel_id=1, source_target_pairs={{0,12},{1,13},{2,14},{3,15},{4,0},{5,1},{6,2},{7,3},{8,4},{9,5},{1... | collective-permute-start | bytes 1572872 | tf_op jit(solution)/shard_map/ppermute | solution.py:19
  57.5 16.9 %collective-permute-start.3 = (bf16[144,4096]{1,0:T(8,128)(2,1)S(1)}, bf16[144,4096]{1,0:T(8,128)(2,1)S(1)}, u32[]{:S(2)}, u32[]{:S(2)}) collective-permute-start(bf16[144,4096]{1,0:T(8,128)(2,1)S(1)} %copy-done.3), channel_id=1, source_target_pairs={{0,1},{1,0},{2,3},{3,2},{4,5},{5,4},{6,7},{7,6},{8,9},{9,8},{10,11... | collective-permute-start | bytes 3538952 | tf_op jit(solution)/shard_map/ppermute | solution.py:27
  69.3 8.9 %collective-permute-start.5 = (bf16[144,4096]{1,0:T(8,128)(2,1)}, bf16[144,4096]{1,0:T(8,128)(2,1)}, u32[]{:S(2)}, u32[]{:S(2)}) collective-permute-start(bf16[144,4096]{1,0:T(8,128)(2,1)} %collective-permute-done.rest_1_.rest_9_), channel_id=1, source_target_pairs={{0,1},{1,0},{2,3},{3,2},{4,5},{5,4},{6,7},{7,6},{8,9},{9,8},{10,11... | collective-permute-start | bytes 3538952 | tf_op jit(solution)/shard_map/ppermute | solution.py:27
  69.4 8.9 %collective-permute-start.7 = (bf16[144,4096]{1,0:T(8,128)(2,1)}, bf16[144,4096]{1,0:T(8,128)(2,1)}, u32[]{:S(2)}, u32[]{:S(2)}) collective-permute-start(bf16[144,4096]{1,0:T(8,128)(2,1)} %collective-permute-done.1.rest_3_.rest_12_.rest_4_), channel_id=1, source_target_pairs={{0,1},{1,0},{2,3},{3,2},{4,5},{5,4},{6,7},{7,6},{8,9},{9,8},{10,11... | collective-permute-start | bytes 3538952 | tf_op jit(solution)/shard_map/ppermute | solution.py:27
  69.9 7.3 %collective-permute-start.8 = (bf16[64,4096]{1,0:T(8,128)(2,1)}, bf16[64,4096]{1,0:T(8,128)(2,1)}, u32[]{:S(2)}, u32[]{:S(2)}) collective-permute-start(bf16[64,4096]{1,0:T(8,128)(2,1)} %collective-permute-done.4.rest_10_.rest_2_), channel_id=1, source_target_pairs={{0,1},{1,0},{2,3},{3,2},{4,5},{5,4},{6,7},{7,6},{8,9},{9,8},{10,11... | collective-permute-start | bytes 1572872 | tf_op jit(solution)/shard_map/ppermute | solution.py:27
  74.3 2.9 %copy-start.5 = (bf16[256,4096]{1,0:T(8,128)(2,1)}, bf16[256,4096]{1,0:T(8,128)(2,1)S(1)}, u32[]{:S(2)}) copy-start(bf16[256,4096]{1,0:T(8,128)(2,1)S(1)} %collective-permute-done.10.rest_19_.n2) | copy-start | bytes 6291460
  74.3 4.0 %collective-permute-start.6 = (bf16[80,4096]{1,0:T(8,128)(2,1)}, bf16[80,4096]{1,0:T(8,128)(2,1)S(1)}, u32[]{:S(2)}, u32[]{:S(2)}) collective-permute-start(bf16[80,4096]{1,0:T(8,128)(2,1)} %collective-permute-done.2.rest_2_.rest_11_.rest_3_), channel_id=1, source_target_pairs={{0,1},{1,0},{2,3},{3,2},{4,5},{5,4},{6,7},{7,6},{8,9},{9,8},{10,11... | collective-permute-start | bytes 1966088 | tf_op jit(solution)/shard_map/ppermute | solution.py:27
  74.3 16.5 %copy-start.19 = (f32[8,128]{1,0:T(8,128)}, f32[8,128]{1,0:T(8,128)S(1)}, u32[]{:S(2)}) copy-start(f32[8,128]{1,0:T(8,128)S(1)} %maximum_maximum_fusion.about) | copy-start | bytes 12292
  74.4 1.2 copy-start.4
  75.6 15.3 %collective-permute-start.11 = (bf16[64,4096]{1,0:T(8,128)(2,1)S(1)}, bf16[64,4096]{1,0:T(8,128)(2,1)S(1)}, u32[]{:S(2)}, u32[]{:S(2)}) collective-permute-start(bf16[64,4096]{1,0:T(8,128)(2,1)S(1)} %slice.50), channel_id=1, source_target_pairs={{0,64},{16,80},{32,96},{48,112},{64,0},{80,16},{96,32},{112,48},{1... | collective-permute-start | bytes 1572872 | tf_op jit(solution)/shard_map/ppermute | solution.py:31
  77.1 13.7 %collective-permute-start.12 = (f32[8,128]{1,0:T(8,128)S(1)}, f32[8,128]{1,0:T(8,128)S(1)}, u32[]{:S(2)}, u32[]{:S(2)}) collective-permute-start(f32[8,128]{1,0:T(8,128)S(1)} %maximum_maximum_fusion.about), channel_id=1, source_target_pairs={{0,64},{16,80},{32,96},{48,112},{64,0},{80,16},{96,32},{112,48},{1... | collective-permute-start | bytes 12296 | tf_op jit(solution)/shard_map/ppermute | solution.py:31
  78.2 0.8 copy-start.6
  90.8 6.3 %copy-start.21 = (f32[8,128]{1,0:T(8,128)}, f32[8,128]{1,0:T(8,128)S(1)}, u32[]{:S(2)}) copy-start(f32[8,128]{1,0:T(8,128)S(1)} %collective-permute-done.12.about) | copy-start | bytes 12292
  90.9 6.3 %copy-start.8 = (bf16[64,4096]{1,0:T(8,128)(2,1)}, bf16[64,4096]{1,0:T(8,128)(2,1)S(1)}, u32[]{:S(2)}) copy-start(bf16[64,4096]{1,0:T(8,128)(2,1)S(1)} %collective-permute-done.11.rest_0_.rest_1_) | copy-start | bytes 1572868
  97.1 33.1 %collective-permute-start.17 = (bf16[512,4096]{1,0:T(8,128)(2,1)}, bf16[512,4096]{1,0:T(8,128)(2,1)}, u32[]{:S(2)}, u32[]{:S(2)}) collective-permute-start(bf16[512,4096]{1,0:T(8,128)(2,1)} %hard_back.2), channel_id=1, source_target_pairs={{0,1},{1,0},{2,3},{3,2},{4,5},{5,4},{6,7},{7,6},{8,9},{9,8},{10,11... | collective-permute-start | bytes 12582920 | tf_op jit(solution)/shard_map/ppermute | solution.py:27
  97.9 14.2 %copy-start.18 = (f32[8,8,128]{2,1,0:T(8,128)S(1)}, f32[8,8,128]{2,1,0:T(8,128)}, u32[]{:S(2)}) copy-start(f32[8,8,128]{2,1,0:T(8,128)} %get-tuple-element.67) | copy-start | bytes 98308
  97.9 14.2 %copy-start.1 = (bf16[128,4096]{1,0:T(8,128)(2,1)S(1)}, bf16[128,4096]{1,0:T(8,128)(2,1)}, u32[]{:S(2)}) copy-start(bf16[128,4096]{1,0:T(8,128)(2,1)} %refs_6_.1) | copy-start | bytes 3145732
  104.1 4.0 %collective-permute-start.13 = (f32[8,128]{1,0:T(8,128)}, f32[8,128]{1,0:T(8,128)S(1)}, u32[]{:S(2)}, u32[]{:S(2)}) collective-permute-start(f32[8,128]{1,0:T(8,128)} %get-tuple-element.62), channel_id=1, source_target_pairs={{0,12},{1,13},{2,14},{3,15},{4,0},{5,1},{6,2},{7,3},{8,4},{9,5},{1... | collective-permute-start | bytes 12296 | tf_op jit(solution)/shard_map/ppermute | solution.py:19
  106.0 5.3 %collective-permute-start.14 = (f32[8,128]{1,0:T(8,128)}, f32[8,128]{1,0:T(8,128)S(1)}, u32[]{:S(2)}, u32[]{:S(2)}) collective-permute-start(f32[8,128]{1,0:T(8,128)} %get-tuple-element.62), channel_id=1, source_target_pairs={{0,8},{1,9},{2,10},{3,11},{4,12},{5,13},{6,14},{7,15},{8,0},{9,1},... | collective-permute-start | bytes 12296 | tf_op jit(solution)/shard_map/ppermute | solution.py:19
  106.1 5.2 %collective-permute-start.15 = (f32[8,128]{1,0:T(8,128)}, f32[8,128]{1,0:T(8,128)S(1)}, u32[]{:S(2)}, u32[]{:S(2)}) collective-permute-start(f32[8,128]{1,0:T(8,128)} %get-tuple-element.62), channel_id=1, source_target_pairs={{0,4},{1,5},{2,6},{3,7},{4,8},{5,9},{6,10},{7,11},{8,12},{9,13},{1... | collective-permute-start | bytes 12296 | tf_op jit(solution)/shard_map/ppermute | solution.py:19
  112.0 1.8 collective-permute-start.16
  112.2 14.4 %collective-permute-start.19 = (bf16[64,4096]{1,0:T(8,128)(2,1)S(1)}, bf16[64,4096]{1,0:T(8,128)(2,1)S(1)}, u32[]{:S(2)}, u32[]{:S(2)}) collective-permute-start(bf16[64,4096]{1,0:T(8,128)(2,1)S(1)} %slice.61), channel_id=1, source_target_pairs={{0,64},{16,80},{32,96},{48,112},{64,0},{80,16},{96,32},{112,48},{1... | collective-permute-start | bytes 1572872 | tf_op jit(solution)/shard_map/ppermute | solution.py:31
  113.8 8.6 %copy-start.17 = (f32[8,128]{1,0:T(8,128)}, f32[8,128]{1,0:T(8,128)S(1)}, u32[]{:S(2)}) copy-start(f32[8,128]{1,0:T(8,128)S(1)} %concatenate.45.about_a.about) | copy-start | bytes 12292
  113.8 12.8 %collective-permute-start.18 = (f32[8,128]{1,0:T(8,128)S(1)}, f32[8,128]{1,0:T(8,128)S(1)}, u32[]{:S(2)}, u32[]{:S(2)}) collective-permute-start(f32[8,128]{1,0:T(8,128)S(1)} %concatenate.45.about_a.about), channel_id=1, source_target_pairs={{0,64},{16,80},{32,96},{48,112},{64,0},{80,16},{96,32},{112,48},{1... | collective-permute-start | bytes 12296 | tf_op jit(solution)/shard_map/ppermute | solution.py:31
  126.6 10.7 %copy-start.9 = (bf16[64,4096]{1,0:T(8,128)(2,1)}, bf16[64,4096]{1,0:T(8,128)(2,1)S(1)}, u32[]{:S(2)}) copy-start(bf16[64,4096]{1,0:T(8,128)(2,1)S(1)} %collective-permute-done.19.rest_1_.rest_2_) | copy-start | bytes 1572868
  126.7 10.7 %copy-start.20 = (f32[8,128]{1,0:T(8,128)}, f32[8,128]{1,0:T(8,128)S(1)}, u32[]{:S(2)}) copy-start(f32[8,128]{1,0:T(8,128)S(1)} %collective-permute-done.18.about_b) | copy-start | bytes 12292
  126.7 48.9 %collective-permute-start.23 = (bf16[256,4096]{1,0:T(8,128)(2,1)}, bf16[256,4096]{1,0:T(8,128)(2,1)S(1)}, u32[]{:S(2)}, u32[]{:S(2)}) collective-permute-start(bf16[256,4096]{1,0:T(8,128)(2,1)} %pool_part.2), channel_id=1, source_target_pairs={{0,2},{1,3},{2,0},{3,1},{4,6},{5,7},{6,4},{7,5},{8,10},{9,11},{10,... | collective-permute-start | bytes 6291464 | tf_op jit(solution)/shard_map/ppermute | solution.py:23
  137.4 51.4 %collective-permute-start.20 = (bf16[128,4096]{1,0:T(8,128)(2,1)}, bf16[128,4096]{1,0:T(8,128)(2,1)S(1)}, u32[]{:S(2)}, u32[]{:S(2)}) collective-permute-start(bf16[128,4096]{1,0:T(8,128)(2,1)} %get-tuple-element.72), channel_id=1, source_target_pairs={{0,4},{1,5},{2,6},{3,7},{4,8},{5,9},{6,10},{7,11},{8,12},{9,13},{1... | collective-permute-start | bytes 3145736 | tf_op jit(solution)/shard_map/ppermute | solution.py:19
  137.8 51.0 %collective-permute-start.21 = (bf16[128,4096]{1,0:T(8,128)(2,1)}, bf16[128,4096]{1,0:T(8,128)(2,1)S(1)}, u32[]{:S(2)}, u32[]{:S(2)}) collective-permute-start(bf16[128,4096]{1,0:T(8,128)(2,1)} %get-tuple-element.73), channel_id=1, source_target_pairs={{0,8},{1,9},{2,10},{3,11},{4,12},{5,13},{6,14},{7,15},{8,0},{9,1},... | collective-permute-start | bytes 3145736 | tf_op jit(solution)/shard_map/ppermute | solution.py:19
  150.1 33.1 %collective-permute-start.24 = (bf16[64,4096]{1,0:T(8,128)(2,1)}, bf16[64,4096]{1,0:T(8,128)(2,1)S(1)}, u32[]{:S(2)}, u32[]{:S(2)}) collective-permute-start(bf16[64,4096]{1,0:T(8,128)(2,1)} %get-tuple-element.85), channel_id=1, source_target_pairs={{0,16},{16,32},{32,48},{48,0},{64,80},{80,96},{96,112},{112,64},{1... | collective-permute-start | bytes 1572872 | tf_op jit(solution)/shard_map/ppermute | solution.py:35
  151.7 37.1 %collective-permute-start.22 = (bf16[128,4096]{1,0:T(8,128)(2,1)}, bf16[128,4096]{1,0:T(8,128)(2,1)S(1)}, u32[]{:S(2)}, u32[]{:S(2)}) collective-permute-start(bf16[128,4096]{1,0:T(8,128)(2,1)} %get-tuple-element.74), channel_id=1, source_target_pairs={{0,12},{1,13},{2,14},{3,15},{4,0},{5,1},{6,2},{7,3},{8,4},{9,5},{1... | collective-permute-start | bytes 3145736 | tf_op jit(solution)/shard_map/ppermute | solution.py:19
  164.5 18.7 %copy-start.23 = (bf16[64,4096]{1,0:T(8,128)(2,1)S(1)}, bf16[64,4096]{1,0:T(8,128)(2,1)}, u32[]{:S(2)}) copy-start(bf16[64,4096]{1,0:T(8,128)(2,1)} %get-tuple-element.87) | copy-start | bytes 1572868
  164.5 22.0 %copy-start.22 = (bf16[64,4096]{1,0:T(8,128)(2,1)S(1)}, bf16[64,4096]{1,0:T(8,128)(2,1)}, u32[]{:S(2)}) copy-start(bf16[64,4096]{1,0:T(8,128)(2,1)} %get-tuple-element.88) | copy-start | bytes 1572868
  175.6 1.3 copy-start.7
  183.2 25.8 %copy-start.14 = (bf16[64,4096]{1,0:T(8,128)(2,1)}, bf16[64,4096]{1,0:T(8,128)(2,1)S(1)}, u32[]{:S(2)}) copy-start(bf16[64,4096]{1,0:T(8,128)(2,1)S(1)} %collective-permute-done.24.refs_1_) | copy-start | bytes 1572868
  183.2 14.2 %collective-permute-start.25 = (bf16[64,4096]{1,0:T(8,128)(2,1)S(1)}, bf16[64,4096]{1,0:T(8,128)(2,1)S(1)}, u32[]{:S(2)}, u32[]{:S(2)}) collective-permute-start(bf16[64,4096]{1,0:T(8,128)(2,1)S(1)} %copy-done.23), channel_id=1, source_target_pairs={{0,32},{16,48},{32,0},{48,16},{64,96},{80,112},{96,64},{112,80},{1... | collective-permute-start | bytes 1572872 | tf_op jit(solution)/shard_map/ppermute | solution.py:35
  186.5 22.5 %collective-permute-start.26 = (bf16[64,4096]{1,0:T(8,128)(2,1)S(1)}, bf16[64,4096]{1,0:T(8,128)(2,1)S(1)}, u32[]{:S(2)}, u32[]{:S(2)}) collective-permute-start(bf16[64,4096]{1,0:T(8,128)(2,1)S(1)} %copy-done.22), channel_id=1, source_target_pairs={{0,48},{16,0},{32,16},{48,32},{64,112},{80,64},{96,80},{112,96},{1... | collective-permute-start | bytes 1572872 | tf_op jit(solution)/shard_map/ppermute | solution.py:35
  188.8 1.0 copy-start.11
  188.8 1.4 copy-start.12
  188.8 1.7 copy-start.13
  197.4 11.6 %copy-start.15 = (bf16[64,4096]{1,0:T(8,128)(2,1)}, bf16[64,4096]{1,0:T(8,128)(2,1)S(1)}, u32[]{:S(2)}) copy-start(bf16[64,4096]{1,0:T(8,128)(2,1)S(1)} %collective-permute-done.25.refs_2_) | copy-start | bytes 1572868
  209.0 0.8 copy-start.16
Sparse Core Ops, SparseCore 0:
  22.2 50.9 all-gather.1

commit v3 on v2

--- a/solution.py
+++ b/solution.py
@@ -501,7 +501,7 @@
     fac_rows = jnp.broadcast_to(own_fac[:, None], (n_query, 128))
     d_one = hop_y(d1, 1)
     grad_pool = last_step((dn_home, dn_x), pool)
-    (d2, d3, dq_batch) = after((d2, d3, dq_batch), grad_pool, d_one)
+    (d2, d3, dq_batch) = after((d2, d3, dq_batch), grad_pool)
     d_two = hop_y(d2, 2)
     d_three = hop_y(d3, -1)
     grad_query = last_step(u_parts, queries, fac_rows, dq_batch)

time: 221 us -> 221 us (level)
    unnamed x50 -> x48, local copies, waits for them, and re-layouts: 5.01 us -> 4.17 us
where the time goes in v3:
time: 221 us; the launch traced here: 220 us
  waiting for transfers between devices  77.5 us (35%)
  Pallas kernels  74 us (33%)
  starting transfers between devices  35.6 us (16%)
  between operations  15 us (7%)
  other arithmetic  10.2 us (5%)
  local copies, waits for them, and re-layouts  7.89 us (4%)
    ppermute x10, waiting for transfers between devices, hop_z(): return lax.ppermute(x, 'grp', [(g, (g + 4 * by) % 16) for g in range(16)])  38.2 us
    ppermute x10, starting transfers between devices, hop_z(): return lax.ppermute(x, 'grp', [(g, (g + 4 * by) % 16) for g in range(16)])  15.6 us
    ppermute x2, waiting for transfers between devices, hop_xh(): return lax.ppermute(x, 'grp', [(g, g ^ 2) for g in range(16)])  15.2 us
    pallas_call x3, Pallas kernels, last_step(): pl.pallas_call(functools.partial(last_kernel, len(parts), fac is not None...  14.7 us
    pallas_call x2, Pallas kernels, pool_part(): pl.pallas_call(pool_kernel, grid=(width // 2048,), in_specs=[whole_spec(e...  14.2 us
    ppermute x3, waiting for transfers between devices, hop_y(): lax.ppermute(x, 'loop', [(l, (l & 4) + (l + by) % 4) for l in range(8)])  13.7 us
    pallas_call x2, Pallas kernels, hard_back(): pl.pallas_call(functools.partial(back_kernel, first), grid=(width // 2048...  13.5 us
    pallas_call x2, Pallas kernels, batch_scores(): pl.pallas_call(batch_kernel, grid=(width // 2048,), in_specs=[smem_spec()...  12.3 us
  transfers between devices with their start and end apart: 28, of which 11 were waited for; matrix products, arithmetic and copies ran while one was open for 6% of the time, Pallas kernels for 32%

profile of v3, /device:TPU:0, one launch (start us, length us, event | category | flops | bytes accessed | tf_op | source)
XLA Modules:
  0.0 220.2 jit_solution(2991184813103460959)
XLA Ops:
  7.2 1.7 collective-permute-start.9
  9.5 1.5 multiply_reduce_fusion
  11.1 0.7 fusion.20
  11.8 0.7 fusion.19
  12.5 2.3 %pad_maximum_fusion.rest_0_.rest_8_ = bf16[144,4096]{1,0:T(8,128)(2,1)} fusion(bf16[16,4096]{1,0:T(8,128)(2,1)S(1)} %fusion.11, bf16[128,4096]{1,0:T(8,128)(2,1)} %refs_6_.1), kind=kLoop, calls=%fused_computation.1 | loop fusion | flops 2359296 | bytes 2359296 | tf_op jit(solution)/shard_map/concatenate | solution.py:433
  14.8 6.2 %collective-permute-done.9 = bf16[64,4096]{1,0:T(8,128)(2,1)S(1)} collective-permute-done((bf16[64,4096]{1,0:T(8,128)(2,1)}, bf16[64,4096]{1,0:T(8,128)(2,1)S(1)}, u32[]{:S(2)}, u32[]{:S(2)}) %collective-permute-start.9) | collective-permute-done | bytes 524320 | tf_op jit(solution)/shard_map/ppermute | solution.py:31
  21.0 1.1 pad_maximum_fusion.1
  22.1 2.2 %collective-permute-start.1 = (bf16[144,4096]{1,0:T(8,128)(2,1)}, bf16[144,4096]{1,0:T(8,128)(2,1)}, u32[]{:S(2)}, u32[]{:S(2)}) collective-permute-start(bf16[144,4096]{1,0:T(8,128)(2,1)} %pad_maximum_fusion.rest_0_.rest_8_), channel_id=1, source_target_pairs={{0,4},{1,5},{2,6},{3,7},{4,8},{5,9},{6,10},{7,11},{8,12},{9,13},{1... | collective-permute-start | bytes 3538952 | tf_op jit(solution)/shard_map/ppermute | solution.py:19
  24.3 2.2 %collective-permute-start = (bf16[144,4096]{1,0:T(8,128)(2,1)}, bf16[144,4096]{1,0:T(8,128)(2,1)}, u32[]{:S(2)}, u32[]{:S(2)}) collective-permute-start(bf16[144,4096]{1,0:T(8,128)(2,1)} %pad_maximum_fusion.rest_0_.rest_8_), channel_id=1, source_target_pairs={{0,12},{1,13},{2,14},{3,15},{4,0},{5,1},{6,2},{7,3},{8,4},{9,5},{1... | collective-permute-start | bytes 3538952 | tf_op jit(solution)/shard_map/ppermute | solution.py:19
  26.6 3.0 %collective-permute-start.10 = (bf16[256,4096]{1,0:T(8,128)(2,1)S(1)}, bf16[256,4096]{1,0:T(8,128)(2,1)S(1)}, u32[]{:S(2)}, u32[]{:S(2)}) collective-permute-start(bf16[256,4096]{1,0:T(8,128)(2,1)S(1)} %copy-done.2), channel_id=1, source_target_pairs={{0,2},{1,3},{2,0},{3,1},{4,6},{5,7},{6,4},{7,5},{8,10},{9,11},{10,... | collective-permute-start | bytes 6291464 | tf_op jit(solution)/shard_map/ppermute | solution.py:23
  29.6 22.3 %collective-permute-done.1.rest_3_.rest_12_.rest_4_ = bf16[144,4096]{1,0:T(8,128)(2,1)} collective-permute-done((bf16[144,4096]{1,0:T(8,128)(2,1)}, bf16[144,4096]{1,0:T(8,128)(2,1)}, u32[]{:S(2)}, u32[]{:S(2)}) %collective-permute-start.1) | collective-permute-done | bytes 1179680 | tf_op jit(solution)/shard_map/ppermute | solution.py:19
  51.9 1.1 slice.62
  53.1 1.1 slice.63
  54.2 3.3 %collective-permute-start.4 = (bf16[64,4096]{1,0:T(8,128)(2,1)S(1)}, bf16[64,4096]{1,0:T(8,128)(2,1)}, u32[]{:S(2)}, u32[]{:S(2)}) collective-permute-start(bf16[64,4096]{1,0:T(8,128)(2,1)S(1)} %slice.63), channel_id=1, source_target_pairs={{0,12},{1,13},{2,14},{3,15},{4,0},{5,1},{6,2},{7,3},{8,4},{9,5},{1... | collective-permute-start | bytes 1572872 | tf_op jit(solution)/shard_map/ppermute | solution.py:19
  57.6 9.3 %collective-permute-done.4.rest_10_.rest_2_ = bf16[64,4096]{1,0:T(8,128)(2,1)} collective-permute-done((bf16[64,4096]{1,0:T(8,128)(2,1)S(1)}, bf16[64,4096]{1,0:T(8,128)(2,1)}, u32[]{:S(2)}, u32[]{:S(2)}) %collective-permute-start.4) | collective-permute-done | bytes 524320 | tf_op jit(solution)/shard_map/ppermute | solution.py:19
  66.9 2.5 %collective-permute-done.2.rest_2_.rest_11_.rest_3_ = bf16[80,4096]{1,0:T(8,128)(2,1)} collective-permute-done((bf16[80,4096]{1,0:T(8,128)(2,1)S(1)}, bf16[80,4096]{1,0:T(8,128)(2,1)}, u32[]{:S(2)}, u32[]{:S(2)}) %collective-permute-start.2) | collective-permute-done | bytes 655392 | tf_op jit(solution)/shard_map/ppermute | solution.py:19
  69.4 0.5 collective-permute-start.7
  69.9 0.1 collective-permute-start.8
  70.0 4.3 %collective-permute-done.10.rest_19_.n2 = bf16[256,4096]{1,0:T(8,128)(2,1)S(1)} collective-permute-done((bf16[256,4096]{1,0:T(8,128)(2,1)S(1)}, bf16[256,4096]{1,0:T(8,128)(2,1)S(1)}, u32[]{:S(2)}, u32[]{:S(2)}) %collective-permute-start.10) | collective-permute-done | bytes 2097184 | tf_op jit(solution)/shard_map/ppermute | solution.py:23
  74.4 1.1 copy-done.4
  75.6 1.5 collective-permute-start.11
  77.1 0.5 collective-permute-start.12
  77.6 0.6 add_convert_fusion.bases
  78.2 0.8 copy-done.6
  79.0 11.9 %hard_scores.1 = (f32[256,1024]{1,0:T(8,128)}, f32[256,1024]{1,0:T(8,128)}, f32[8,128]{1,0:T(8,128)}, f32[256,128]{1,0:T(8,128)}, f32[256,128]{1,0:T(8,128)}, /*index=5*/f32[8,8,128]{2,1,0:T(8,128)}) custom-call(f32[2]{0:T(128)} %add_convert_fusion.bases, bf16[144,4096]{1,0:T(8,128)(2,1)} %pad_maximum_fusion.rest_0_.rest_8_, ...), custom_call_target="tpu_custom_call" | custom-call | flops 1 | bytes 1 | tf_op jit(solution)/shard_map/hard_scores/pallas_call | solution.py:158
  91.0 6.3 %hard_back.2 = bf16[512,4096]{1,0:T(8,128)(2,1)} custom-call(f32[256,1024]{1,0:T(8,128)} %get-tuple-element.82.e1.e, f32[256,1024]{1,0:T(8,128)} %get-tuple-element.56.e2.e, f32[256,128]{1,0:T(8,128)} %get-tuple-element.57.s1, f32[256,128]{1,0:T(8,128)} %get-tuple-element.58.s2, bf16[256,4096]{1,0:T(8,128)(2,1)} %refs_2_.1, bf16[256,4096]{1,0:T(8,128)(2,1)} %copy-done.5), custom_call_target="tpu_custom_call" | custom-call | flops 1 | bytes 1 | tf_op jit(solution)/shard_map/hard_back/pallas_call | solution.py:261
  97.3 0.1 collective-permute-start.17
  97.5 0.6 mul.31.places
  98.1 6.2 %batch_scores.2 = (f32[512,128]{1,0:T(8,128)}, f32[8,128]{1,0:T(8,128)}, f32[8,128]{1,0:T(8,128)}, f32[512,128]{1,0:T(8,128)}) custom-call(s32[8]{0:T(128)} %mul.31.places, f32[8,128]{1,0:T(8,128)} %copy-done.17, f32[8,128]{1,0:T(8,128)} %get-tuple-element.59.sums, bf16[512,4096]{1,0:T(8,128)(2,1)} %all-gather.2.cloned.1.call-done.p_all, ...), custom_call_target="tpu_custom_call" | custom-call | flops 1 | bytes 1 | tf_op jit(solution)/shard_map/batch_scores/pallas_call | solution.py:217
  104.3 1.8 collective-permute-start.13
  106.1 0.1 collective-permute-start.14
  106.2 1.1 collective-permute-start.15
  107.3 0.9 collective-permute-done.13
  108.2 3.2 %collective-permute-done.14 = f32[8,128]{1,0:T(8,128)S(1)} collective-permute-done((f32[8,128]{1,0:T(8,128)}, f32[8,128]{1,0:T(8,128)S(1)}, u32[]{:S(2)}, u32[]{:S(2)}) %collective-permute-start.14) | collective-permute-done | bytes 4128 | tf_op jit(solution)/shard_map/ppermute | solution.py:19
  111.4 0.7 fusion.18
  112.1 0.1 collective-permute-start.16
  112.3 1.6 collective-permute-start.19
  113.9 1.1 collective-permute-start.18
  115.0 0.6 fusion.16.fac
  115.6 6.9 %pool_part.2 = bf16[256,4096]{1,0:T(8,128)(2,1)} custom-call(f32[256,1024]{1,0:T(8,128)} %get-tuple-element.56.e2.e, f32[8,128]{1,0:T(8,128)} %fusion.16.fac, bf16[144,4096]{1,0:T(8,128)(2,1)} %pad_maximum_fusion.rest_0_.rest_8_, bf16[144,4096]{1,0:T(8,128)(2,1)} %collective-permute-done.rest_1_.rest_9_, ...), custom_call_target="tpu_custom_call" | custom-call | flops 1 | bytes 1 | tf_op jit(solution)/shard_map/pool_part/pallas_call | solution.py:292
  122.5 4.2 %collective-permute-done.19.rest_1_.rest_2_ = bf16[64,4096]{1,0:T(8,128)(2,1)S(1)} collective-permute-done((bf16[64,4096]{1,0:T(8,128)(2,1)S(1)}, bf16[64,4096]{1,0:T(8,128)(2,1)S(1)}, u32[]{:S(2)}, u32[]{:S(2)}) %collective-permute-start.19) | collective-permute-done | bytes 524320 | tf_op jit(solution)/shard_map/ppermute | solution.py:31
  126.8 3.0 %collective-permute-start.23 = (bf16[256,4096]{1,0:T(8,128)(2,1)}, bf16[256,4096]{1,0:T(8,128)(2,1)S(1)}, u32[]{:S(2)}, u32[]{:S(2)}) collective-permute-start(bf16[256,4096]{1,0:T(8,128)(2,1)} %pool_part.2), channel_id=1, source_target_pairs={{0,2},{1,3},{2,0},{3,1},{4,6},{5,7},{6,4},{7,5},{8,10},{9,11},{10,... | collective-permute-start | bytes 6291464 | tf_op jit(solution)/shard_map/ppermute | solution.py:23
  129.8 7.2 %hard_back.3 = (f32[128,4096]{1,0:T(8,128)}, bf16[128,4096]{1,0:T(8,128)(2,1)}, bf16[128,4096]{1,0:T(8,128)(2,1)}, bf16[128,4096]{1,0:T(8,128)(2,1)}) custom-call(f32[256,1024]{1,0:T(8,128)} %get-tuple-element.82.e1.e, f32[256,1024]{1,0:T(8,128)} %get-tuple-element.56.e2.e, f32[256,128]{1,0:T(8,128)} %get-tuple-element.57.s1, ...), custom_call_target="tpu_custom_call" | custom-call | flops 1 | bytes 1 | tf_op jit(solution)/shard_map/hard_back/pallas_call | solution.py:261
  137.1 0.4 collective-permute-start.20
  137.5 2.6 %collective-permute-start.21 = (bf16[128,4096]{1,0:T(8,128)(2,1)}, bf16[128,4096]{1,0:T(8,128)(2,1)}, u32[]{:S(2)}, u32[]{:S(2)}) collective-permute-start(bf16[128,4096]{1,0:T(8,128)(2,1)} %get-tuple-element.73), channel_id=1, source_target_pairs={{0,8},{1,9},{2,10},{3,11},{4,12},{5,13},{6,14},{7,15},{8,0},{9,1},... | collective-permute-start | bytes 3145736 | tf_op jit(solution)/shard_map/ppermute | solution.py:19
  140.2 1.7 collective-permute-start.22
  141.8 0.6 and_select_fusion.turns
  142.4 6.1 %batch_scores.3 = (f32[512,128]{1,0:T(8,128)}, f32[8,128]{1,0:T(8,128)}, f32[8,128]{1,0:T(8,128)}, f32[512,128]{1,0:T(8,128)}) custom-call(s32[8]{0:T(128)} %mul.31.places, f32[8,128]{1,0:T(8,128)} %copy-done.19, f32[8,128]{1,0:T(8,128)} %get-tuple-element.59.sums, bf16[512,4096]{1,0:T(8,128)(2,1)} %all-gather.2.cloned.1.call-done.p_all, ...), custom_call_target="tpu_custom_call" | custom-call | flops 1 | bytes 1 | tf_op jit(solution)/shard_map/batch_scores/pallas_call | solution.py:217
  148.5 3.5 %passage_part.1 = (f32[64,4096]{1,0:T(8,128)}, bf16[64,4096]{1,0:T(8,128)(2,1)}, bf16[64,4096]{1,0:T(8,128)(2,1)}, bf16[64,4096]{1,0:T(8,128)(2,1)}) custom-call(s32[4]{0:T(128)} %and_select_fusion.turns, s32[8]{0:T(128)} %mul.31.places, f32[8,128]{1,0:T(8,128)} %copy-done.15, f32[8,128]{1,0:T(8,128)} %copy-done.18, f32[512,128]{1,0:T(8,128)} %get-tuple-element.83.e_a.e, ...), custom_call_target="tpu_custom_call" | custom-call | flops 1 | bytes 1 | tf_op jit(solution)/shard_map/passage_part/pallas_call | solution.py:354
  152.0 7.3 %pool_part.3.refs_0_ = f32[256,4096]{1,0:T(8,128)} custom-call(f32[256,1024]{1,0:T(8,128)} %get-tuple-element.82.e1.e, f32[8,128]{1,0:T(8,128)} %fusion.16.fac, bf16[144,4096]{1,0:T(8,128)(2,1)} %pad_maximum_fusion.rest_0_.rest_8_, bf16[144,4096]{1,0:T(8,128)(2,1)} %collective-permute-done.rest_1_.rest_9_, ...), custom_call_target="tpu_custom_call" | custom-call | flops 1 | bytes 1 | tf_op jit(solution)/shard_map/pool_part/pallas_call | solution.py:292
  159.3 1.7 collective-permute-start.24
  160.9 3.8 %query_part.1.refs_5_ = f32[128,4096]{1,0:T(8,128)} custom-call(s32[8]{0:T(128)} %mul.31.places, f32[8,128]{1,0:T(8,128)} %copy-done.15, f32[512,128]{1,0:T(8,128)} %get-tuple-element.83.e_a.e, f32[512,128]{1,0:T(8,128)} %get-tuple-element.84.scales, bf16[512,4096]{1,0:T(8,128)(2,1)} %all-gather.2.cloned.1.call-done.p_all), custom_call_target="tpu_custom_call" | custom-call | flops 1 | bytes 1 | tf_op jit(solution)/shard_map/query_part/pallas_call | solution.py:318
  164.8 10.9 %collective-permute-done.23.refs_1_ = bf16[256,4096]{1,0:T(8,128)(2,1)S(1)} collective-permute-done((bf16[256,4096]{1,0:T(8,128)(2,1)}, bf16[256,4096]{1,0:T(8,128)(2,1)S(1)}, u32[]{:S(2)}, u32[]{:S(2)}) %collective-permute-start.23) | collective-permute-done | bytes 2097184 | tf_op jit(solution)/shard_map/ppermute | solution.py:23
  175.7 1.3 copy-done.7
  177.0 6.3 %last_step.3 = f32[256,4096]{1,0:T(8,128)} custom-call(f32[256,4096]{1,0:T(8,128)} %pool_part.3.refs_0_, bf16[256,4096]{1,0:T(8,128)(2,1)} %copy-done.7, bf16[256,4096]{1,0:T(8,128)(2,1)} %refs_2_.1), custom_call_target="tpu_custom_call" | custom-call | flops 1 | bytes 1 | tf_op jit(solution)/shard_map/last_step/pallas_call | solution.py:401
  183.4 3.2 %collective-permute-start.25 = (bf16[64,4096]{1,0:T(8,128)(2,1)S(1)}, bf16[64,4096]{1,0:T(8,128)(2,1)S(1)}, u32[]{:S(2)}, u32[]{:S(2)}) collective-permute-start(bf16[64,4096]{1,0:T(8,128)(2,1)S(1)} %copy-done.21), channel_id=1, source_target_pairs={{0,32},{16,48},{32,0},{48,16},{64,96},{80,112},{96,64},{112,80},{1... | collective-permute-start | bytes 1572872 | tf_op jit(solution)/shard_map/ppermute | solution.py:35
  186.5 2.0 collective-permute-start.26
  188.5 1.2 fusion.21
  189.7 0.7 broadcast_in_dim.19.refs_4_
  190.5 5.0 %last_step.4 = f32[128,4096]{1,0:T(8,128)} custom-call(f32[128,4096]{1,0:T(8,128)} %get-tuple-element.71.refs_0_, bf16[128,4096]{1,0:T(8,128)(2,1)} %copy-done.11, bf16[128,4096]{1,0:T(8,128)(2,1)} %collective-permute-done.21.refs_2_, bf16[128,4096]{1,0:T(8,128)(2,1)} %collective-permute-done.22.refs_3_, f32[128,128]{1,0:T(8,128)} %broadcast_in_dim.19.refs_4_, ...), custom_call_target="tpu_custom_call" | custom-call | flops 1 | bytes 1 | tf_op jit(solution)/shard_map/last_step/pallas_call | solution.py:401
  195.5 2.0 collective-permute-done.25.refs_2_
  197.6 11.6 %collective-permute-done.26.refs_3_ = bf16[64,4096]{1,0:T(8,128)(2,1)S(1)} collective-permute-done((bf16[64,4096]{1,0:T(8,128)(2,1)S(1)}, bf16[64,4096]{1,0:T(8,128)(2,1)S(1)}, u32[]{:S(2)}, u32[]{:S(2)}) %collective-permute-start.26) | collective-permute-done | bytes 524320 | tf_op jit(solution)/shard_map/ppermute | solution.py:35
  209.2 0.8 copy-done.14
  210.0 3.4 %last_step.5 = f32[64,4096]{1,0:T(8,128)} custom-call(f32[64,4096]{1,0:T(8,128)} %get-tuple-element.81.refs_0_, bf16[64,4096]{1,0:T(8,128)(2,1)} %copy-done.12, bf16[64,4096]{1,0:T(8,128)(2,1)} %copy-done.13, bf16[64,4096]{1,0:T(8,128)(2,1)} %copy-done.14, bf16[64,4096]{1,0:T(8,128)(2,1)} %refs_4_.1), custom_call_target="tpu_custom_call" | custom-call | flops 1 | bytes 1 | tf_op jit(solution)/shard_map/last_step/pallas_call | solution.py:401
  (91 shorter events, 0.7 us)
Async XLA Ops:
  7.2 13.8 %copy-start.10 = (bf16[64,4096]{1,0:T(8,128)(2,1)S(1)}, bf16[64,4096]{1,0:T(8,128)(2,1)}, u32[]{:S(2)}) copy-start(bf16[64,4096]{1,0:T(8,128)(2,1)} %refs_4_.1) | copy-start | bytes 1572868
  7.2 90.9 %all-gather.2.cloned.1.call-start = ((), (), s32[]{:S(2)}) async-start(), calls=%async_computation | async-start | bytes 5242880 | tf_op jit(solution)/shard_map/all_gather | solution.py:442
  7.2 13.8 %collective-permute-start.9 = (bf16[64,4096]{1,0:T(8,128)(2,1)}, bf16[64,4096]{1,0:T(8,128)(2,1)S(1)}, u32[]{:S(2)}, u32[]{:S(2)}) collective-permute-start(bf16[64,4096]{1,0:T(8,128)(2,1)} %refs_4_.1), channel_id=1, source_target_pairs={{0,64},{16,80},{32,96},{48,112},{64,0},{80,16},{96,32},{112,48},{1... | collective-permute-start | bytes 1572872 | tf_op jit(solution)/shard_map/ppermute | solution.py:31
  14.8 11.7 %copy-start.2 = (bf16[256,4096]{1,0:T(8,128)(2,1)S(1)}, bf16[256,4096]{1,0:T(8,128)(2,1)}, u32[]{:S(2)}) copy-start(bf16[256,4096]{1,0:T(8,128)(2,1)} %refs_2_.1) | copy-start | bytes 6291460
  22.1 47.8 %copy-start.23 = (s32[128]{0:T(128)S(1)}, s32[128]{0:T(128)}, u32[]{:S(2)}) copy-start(s32[128]{0:T(128)} %param.11) | copy-start | bytes 1540
  22.1 52.3 %copy-start = (bf16[128,4096]{1,0:T(8,128)(2,1)S(1)}, bf16[128,4096]{1,0:T(8,128)(2,1)}, u32[]{:S(2)}) copy-start(bf16[128,4096]{1,0:T(8,128)(2,1)} %refs_6_.1) | copy-start | bytes 3145732
  22.1 35.4 %copy-start.3 = (bf16[144,4096]{1,0:T(8,128)(2,1)S(1)}, bf16[144,4096]{1,0:T(8,128)(2,1)}, u32[]{:S(2)}) copy-start(bf16[144,4096]{1,0:T(8,128)(2,1)} %pad_maximum_fusion.rest_0_.rest_8_) | copy-start | bytes 3538948
  22.1 29.8 %collective-permute-start.1 = (bf16[144,4096]{1,0:T(8,128)(2,1)}, bf16[144,4096]{1,0:T(8,128)(2,1)}, u32[]{:S(2)}, u32[]{:S(2)}) collective-permute-start(bf16[144,4096]{1,0:T(8,128)(2,1)} %pad_maximum_fusion.rest_0_.rest_8_), channel_id=1, source_target_pairs={{0,4},{1,5},{2,6},{3,7},{4,8},{5,9},{6,10},{7,11},{8,12},{9,13},{1... | collective-permute-start | bytes 3538952 | tf_op jit(solution)/shard_map/ppermute | solution.py:19
  24.3 28.8 %collective-permute-start = (bf16[144,4096]{1,0:T(8,128)(2,1)}, bf16[144,4096]{1,0:T(8,128)(2,1)}, u32[]{:S(2)}, u32[]{:S(2)}) collective-permute-start(bf16[144,4096]{1,0:T(8,128)(2,1)} %pad_maximum_fusion.rest_0_.rest_8_), channel_id=1, source_target_pairs={{0,12},{1,13},{2,14},{3,15},{4,0},{5,1},{6,2},{7,3},{8,4},{9,5},{1... | collective-permute-start | bytes 3538952 | tf_op jit(solution)/shard_map/ppermute | solution.py:19
  26.6 47.7 %collective-permute-start.10 = (bf16[256,4096]{1,0:T(8,128)(2,1)S(1)}, bf16[256,4096]{1,0:T(8,128)(2,1)S(1)}, u32[]{:S(2)}, u32[]{:S(2)}) collective-permute-start(bf16[256,4096]{1,0:T(8,128)(2,1)S(1)} %copy-done.2), channel_id=1, source_target_pairs={{0,2},{1,3},{2,0},{3,1},{4,6},{5,7},{6,4},{7,5},{8,10},{9,11},{10,... | collective-permute-start | bytes 6291464 | tf_op jit(solution)/shard_map/ppermute | solution.py:23
  53.0 16.3 %collective-permute-start.2 = (bf16[80,4096]{1,0:T(8,128)(2,1)S(1)}, bf16[80,4096]{1,0:T(8,128)(2,1)}, u32[]{:S(2)}, u32[]{:S(2)}) collective-permute-start(bf16[80,4096]{1,0:T(8,128)(2,1)S(1)} %slice.62), channel_id=1, source_target_pairs={{0,4},{1,5},{2,6},{3,7},{4,8},{5,9},{6,10},{7,11},{8,12},{9,13},{1... | collective-permute-start | bytes 1966088 | tf_op jit(solution)/shard_map/ppermute | solution.py:19
  54.2 12.7 %collective-permute-start.4 = (bf16[64,4096]{1,0:T(8,128)(2,1)S(1)}, bf16[64,4096]{1,0:T(8,128)(2,1)}, u32[]{:S(2)}, u32[]{:S(2)}) collective-permute-start(bf16[64,4096]{1,0:T(8,128)(2,1)S(1)} %slice.63), channel_id=1, source_target_pairs={{0,12},{1,13},{2,14},{3,15},{4,0},{5,1},{6,2},{7,3},{8,4},{9,5},{1... | collective-permute-start | bytes 1572872 | tf_op jit(solution)/shard_map/ppermute | solution.py:19
  57.5 16.9 %collective-permute-start.3 = (bf16[144,4096]{1,0:T(8,128)(2,1)S(1)}, bf16[144,4096]{1,0:T(8,128)(2,1)S(1)}, u32[]{:S(2)}, u32[]{:S(2)}) collective-permute-start(bf16[144,4096]{1,0:T(8,128)(2,1)S(1)} %copy-done.3), channel_id=1, source_target_pairs={{0,1},{1,0},{2,3},{3,2},{4,5},{5,4},{6,7},{7,6},{8,9},{9,8},{10,11... | collective-permute-start | bytes 3538952 | tf_op jit(solution)/shard_map/ppermute | solution.py:27
  69.4 8.8 %collective-permute-start.5 = (bf16[144,4096]{1,0:T(8,128)(2,1)}, bf16[144,4096]{1,0:T(8,128)(2,1)}, u32[]{:S(2)}, u32[]{:S(2)}) collective-permute-start(bf16[144,4096]{1,0:T(8,128)(2,1)} %collective-permute-done.rest_1_.rest_9_), channel_id=1, source_target_pairs={{0,1},{1,0},{2,3},{3,2},{4,5},{5,4},{6,7},{7,6},{8,9},{9,8},{10,11... | collective-permute-start | bytes 3538952 | tf_op jit(solution)/shard_map/ppermute | solution.py:27
  69.4 8.8 %collective-permute-start.7 = (bf16[144,4096]{1,0:T(8,128)(2,1)}, bf16[144,4096]{1,0:T(8,128)(2,1)}, u32[]{:S(2)}, u32[]{:S(2)}) collective-permute-start(bf16[144,4096]{1,0:T(8,128)(2,1)} %collective-permute-done.1.rest_3_.rest_12_.rest_4_), channel_id=1, source_target_pairs={{0,1},{1,0},{2,3},{3,2},{4,5},{5,4},{6,7},{7,6},{8,9},{9,8},{10,11... | collective-permute-start | bytes 3538952 | tf_op jit(solution)/shard_map/ppermute | solution.py:27
  69.9 7.2 %collective-permute-start.8 = (bf16[64,4096]{1,0:T(8,128)(2,1)}, bf16[64,4096]{1,0:T(8,128)(2,1)}, u32[]{:S(2)}, u32[]{:S(2)}) collective-permute-start(bf16[64,4096]{1,0:T(8,128)(2,1)} %collective-permute-done.4.rest_10_.rest_2_), channel_id=1, source_target_pairs={{0,1},{1,0},{2,3},{3,2},{4,5},{5,4},{6,7},{7,6},{8,9},{9,8},{10,11... | collective-permute-start | bytes 1572872 | tf_op jit(solution)/shard_map/ppermute | solution.py:27
  74.3 2.8 %copy-start.5 = (bf16[256,4096]{1,0:T(8,128)(2,1)}, bf16[256,4096]{1,0:T(8,128)(2,1)S(1)}, u32[]{:S(2)}) copy-start(bf16[256,4096]{1,0:T(8,128)(2,1)S(1)} %collective-permute-done.10.rest_19_.n2) | copy-start | bytes 6291460
  74.3 3.9 %collective-permute-start.6 = (bf16[80,4096]{1,0:T(8,128)(2,1)}, bf16[80,4096]{1,0:T(8,128)(2,1)S(1)}, u32[]{:S(2)}, u32[]{:S(2)}) collective-permute-start(bf16[80,4096]{1,0:T(8,128)(2,1)} %collective-permute-done.2.rest_2_.rest_11_.rest_3_), channel_id=1, source_target_pairs={{0,1},{1,0},{2,3},{3,2},{4,5},{5,4},{6,7},{7,6},{8,9},{9,8},{10,11... | collective-permute-start | bytes 1966088 | tf_op jit(solution)/shard_map/ppermute | solution.py:27
  74.4 16.6 %copy-start.17 = (f32[8,128]{1,0:T(8,128)}, f32[8,128]{1,0:T(8,128)S(1)}, u32[]{:S(2)}) copy-start(f32[8,128]{1,0:T(8,128)S(1)} %maximum_maximum_fusion.about) | copy-start | bytes 12292
  74.4 1.2 copy-start.4
  75.6 15.4 %collective-permute-start.11 = (bf16[64,4096]{1,0:T(8,128)(2,1)S(1)}, bf16[64,4096]{1,0:T(8,128)(2,1)S(1)}, u32[]{:S(2)}, u32[]{:S(2)}) collective-permute-start(bf16[64,4096]{1,0:T(8,128)(2,1)S(1)} %slice.50), channel_id=1, source_target_pairs={{0,64},{16,80},{32,96},{48,112},{64,0},{80,16},{96,32},{112,48},{1... | collective-permute-start | bytes 1572872 | tf_op jit(solution)/shard_map/ppermute | solution.py:31
  77.1 13.9 %collective-permute-start.12 = (f32[8,128]{1,0:T(8,128)S(1)}, f32[8,128]{1,0:T(8,128)S(1)}, u32[]{:S(2)}, u32[]{:S(2)}) collective-permute-start(f32[8,128]{1,0:T(8,128)S(1)} %maximum_maximum_fusion.about), channel_id=1, source_target_pairs={{0,64},{16,80},{32,96},{48,112},{64,0},{80,16},{96,32},{112,48},{1... | collective-permute-start | bytes 12296 | tf_op jit(solution)/shard_map/ppermute | solution.py:31
  78.2 0.8 copy-start.6
  91.0 6.3 %copy-start.19 = (f32[8,128]{1,0:T(8,128)}, f32[8,128]{1,0:T(8,128)S(1)}, u32[]{:S(2)}) copy-start(f32[8,128]{1,0:T(8,128)S(1)} %collective-permute-done.12.about) | copy-start | bytes 12292
  91.0 6.3 %copy-start.8 = (bf16[64,4096]{1,0:T(8,128)(2,1)}, bf16[64,4096]{1,0:T(8,128)(2,1)S(1)}, u32[]{:S(2)}) copy-start(bf16[64,4096]{1,0:T(8,128)(2,1)S(1)} %collective-permute-done.11.rest_0_.rest_1_) | copy-start | bytes 1572868
  97.3 32.6 %collective-permute-start.17 = (bf16[512,4096]{1,0:T(8,128)(2,1)}, bf16[512,4096]{1,0:T(8,128)(2,1)}, u32[]{:S(2)}, u32[]{:S(2)}) collective-permute-start(bf16[512,4096]{1,0:T(8,128)(2,1)} %hard_back.2), channel_id=1, source_target_pairs={{0,1},{1,0},{2,3},{3,2},{4,5},{5,4},{6,7},{7,6},{8,9},{9,8},{10,11... | collective-permute-start | bytes 12582920 | tf_op jit(solution)/shard_map/ppermute | solution.py:27
  98.1 14.2 %copy-start.16 = (f32[8,8,128]{2,1,0:T(8,128)S(1)}, f32[8,8,128]{2,1,0:T(8,128)}, u32[]{:S(2)}) copy-start(f32[8,8,128]{2,1,0:T(8,128)} %get-tuple-element.67) | copy-start | bytes 98308
  98.1 14.2 %copy-start.1 = (bf16[128,4096]{1,0:T(8,128)(2,1)S(1)}, bf16[128,4096]{1,0:T(8,128)(2,1)}, u32[]{:S(2)}) copy-start(bf16[128,4096]{1,0:T(8,128)(2,1)} %refs_6_.1) | copy-start | bytes 3145732
  104.3 4.0 %collective-permute-start.13 = (f32[8,128]{1,0:T(8,128)}, f32[8,128]{1,0:T(8,128)S(1)}, u32[]{:S(2)}, u32[]{:S(2)}) collective-permute-start(f32[8,128]{1,0:T(8,128)} %get-tuple-element.62), channel_id=1, source_target_pairs={{0,12},{1,13},{2,14},{3,15},{4,0},{5,1},{6,2},{7,3},{8,4},{9,5},{1... | collective-permute-start | bytes 12296 | tf_op jit(solution)/shard_map/ppermute | solution.py:19
  106.1 5.3 %collective-permute-start.14 = (f32[8,128]{1,0:T(8,128)}, f32[8,128]{1,0:T(8,128)S(1)}, u32[]{:S(2)}, u32[]{:S(2)}) collective-permute-start(f32[8,128]{1,0:T(8,128)} %get-tuple-element.62), channel_id=1, source_target_pairs={{0,8},{1,9},{2,10},{3,11},{4,12},{5,13},{6,14},{7,15},{8,0},{9,1},... | collective-permute-start | bytes 12296 | tf_op jit(solution)/shard_map/ppermute | solution.py:19
  106.2 5.2 %collective-permute-start.15 = (f32[8,128]{1,0:T(8,128)}, f32[8,128]{1,0:T(8,128)S(1)}, u32[]{:S(2)}, u32[]{:S(2)}) collective-permute-start(f32[8,128]{1,0:T(8,128)} %get-tuple-element.62), channel_id=1, source_target_pairs={{0,4},{1,5},{2,6},{3,7},{4,8},{5,9},{6,10},{7,11},{8,12},{9,13},{1... | collective-permute-start | bytes 12296 | tf_op jit(solution)/shard_map/ppermute | solution.py:19
  112.1 1.8 collective-permute-start.16
  112.3 14.4 %collective-permute-start.19 = (bf16[64,4096]{1,0:T(8,128)(2,1)S(1)}, bf16[64,4096]{1,0:T(8,128)(2,1)S(1)}, u32[]{:S(2)}, u32[]{:S(2)}) collective-permute-start(bf16[64,4096]{1,0:T(8,128)(2,1)S(1)} %slice.61), channel_id=1, source_target_pairs={{0,64},{16,80},{32,96},{48,112},{64,0},{80,16},{96,32},{112,48},{1... | collective-permute-start | bytes 1572872 | tf_op jit(solution)/shard_map/ppermute | solution.py:31
  113.9 8.6 %copy-start.15 = (f32[8,128]{1,0:T(8,128)}, f32[8,128]{1,0:T(8,128)S(1)}, u32[]{:S(2)}) copy-start(f32[8,128]{1,0:T(8,128)S(1)} %concatenate.45.about_a.about) | copy-start | bytes 12292
  113.9 12.8 %collective-permute-start.18 = (f32[8,128]{1,0:T(8,128)S(1)}, f32[8,128]{1,0:T(8,128)S(1)}, u32[]{:S(2)}, u32[]{:S(2)}) collective-permute-start(f32[8,128]{1,0:T(8,128)S(1)} %concatenate.45.about_a.about), channel_id=1, source_target_pairs={{0,64},{16,80},{32,96},{48,112},{64,0},{80,16},{96,32},{112,48},{1... | collective-permute-start | bytes 12296 | tf_op jit(solution)/shard_map/ppermute | solution.py:31
  126.7 10.3 %copy-start.9 = (bf16[64,4096]{1,0:T(8,128)(2,1)}, bf16[64,4096]{1,0:T(8,128)(2,1)S(1)}, u32[]{:S(2)}) copy-start(bf16[64,4096]{1,0:T(8,128)(2,1)S(1)} %collective-permute-done.19.rest_1_.rest_2_) | copy-start | bytes 1572868
  126.8 10.3 %copy-start.18 = (f32[8,128]{1,0:T(8,128)}, f32[8,128]{1,0:T(8,128)S(1)}, u32[]{:S(2)}) copy-start(f32[8,128]{1,0:T(8,128)S(1)} %collective-permute-done.18.about_b) | copy-start | bytes 12292
  126.8 48.9 %collective-permute-start.23 = (bf16[256,4096]{1,0:T(8,128)(2,1)}, bf16[256,4096]{1,0:T(8,128)(2,1)S(1)}, u32[]{:S(2)}, u32[]{:S(2)}) collective-permute-start(bf16[256,4096]{1,0:T(8,128)(2,1)} %pool_part.2), channel_id=1, source_target_pairs={{0,2},{1,3},{2,0},{3,1},{4,6},{5,7},{6,4},{7,5},{8,10},{9,11},{10,... | collective-permute-start | bytes 6291464 | tf_op jit(solution)/shard_map/ppermute | solution.py:23
  137.1 49.4 %collective-permute-start.20 = (bf16[128,4096]{1,0:T(8,128)(2,1)}, bf16[128,4096]{1,0:T(8,128)(2,1)S(1)}, u32[]{:S(2)}, u32[]{:S(2)}) collective-permute-start(bf16[128,4096]{1,0:T(8,128)(2,1)} %get-tuple-element.72), channel_id=1, source_target_pairs={{0,4},{1,5},{2,6},{3,7},{4,8},{5,9},{6,10},{7,11},{8,12},{9,13},{1... | collective-permute-start | bytes 3145736 | tf_op jit(solution)/shard_map/ppermute | solution.py:19
  137.5 52.2 %collective-permute-start.21 = (bf16[128,4096]{1,0:T(8,128)(2,1)}, bf16[128,4096]{1,0:T(8,128)(2,1)}, u32[]{:S(2)}, u32[]{:S(2)}) collective-permute-start(bf16[128,4096]{1,0:T(8,128)(2,1)} %get-tuple-element.73), channel_id=1, source_target_pairs={{0,8},{1,9},{2,10},{3,11},{4,12},{5,13},{6,14},{7,15},{8,0},{9,1},... | collective-permute-start | bytes 3145736 | tf_op jit(solution)/shard_map/ppermute | solution.py:19
  140.2 49.6 %collective-permute-start.22 = (bf16[128,4096]{1,0:T(8,128)(2,1)}, bf16[128,4096]{1,0:T(8,128)(2,1)}, u32[]{:S(2)}, u32[]{:S(2)}) collective-permute-start(bf16[128,4096]{1,0:T(8,128)(2,1)} %get-tuple-element.74), channel_id=1, source_target_pairs={{0,12},{1,13},{2,14},{3,15},{4,0},{5,1},{6,2},{7,3},{8,4},{9,5},{1... | collective-permute-start | bytes 3145736 | tf_op jit(solution)/shard_map/ppermute | solution.py:19
  152.0 7.3 %copy-start.22 = (bf16[64,4096]{1,0:T(8,128)(2,1)S(1)}, bf16[64,4096]{1,0:T(8,128)(2,1)}, u32[]{:S(2)}) copy-start(bf16[64,4096]{1,0:T(8,128)(2,1)} %get-tuple-element.86) | copy-start | bytes 1572868
  159.3 36.2 %collective-permute-start.24 = (bf16[64,4096]{1,0:T(8,128)(2,1)S(1)}, bf16[64,4096]{1,0:T(8,128)(2,1)S(1)}, u32[]{:S(2)}, u32[]{:S(2)}) collective-permute-start(bf16[64,4096]{1,0:T(8,128)(2,1)S(1)} %copy-done.22), channel_id=1, source_target_pairs={{0,16},{16,32},{32,48},{48,0},{64,80},{80,96},{96,112},{112,64},{1... | collective-permute-start | bytes 1572872 | tf_op jit(solution)/shard_map/ppermute | solution.py:35
  164.8 18.6 %copy-start.21 = (bf16[64,4096]{1,0:T(8,128)(2,1)S(1)}, bf16[64,4096]{1,0:T(8,128)(2,1)}, u32[]{:S(2)}) copy-start(bf16[64,4096]{1,0:T(8,128)(2,1)} %get-tuple-element.87) | copy-start | bytes 1572868
  164.8 21.8 %copy-start.20 = (bf16[64,4096]{1,0:T(8,128)(2,1)S(1)}, bf16[64,4096]{1,0:T(8,128)(2,1)}, u32[]{:S(2)}) copy-start(bf16[64,4096]{1,0:T(8,128)(2,1)} %get-tuple-element.88) | copy-start | bytes 1572868
  175.7 1.3 copy-start.7
  183.4 14.2 %collective-permute-start.25 = (bf16[64,4096]{1,0:T(8,128)(2,1)S(1)}, bf16[64,4096]{1,0:T(8,128)(2,1)S(1)}, u32[]{:S(2)}, u32[]{:S(2)}) collective-permute-start(bf16[64,4096]{1,0:T(8,128)(2,1)S(1)} %copy-done.21), channel_id=1, source_target_pairs={{0,32},{16,48},{32,0},{48,16},{64,96},{80,112},{96,64},{112,80},{1... | collective-permute-start | bytes 1572872 | tf_op jit(solution)/shard_map/ppermute | solution.py:35
  186.5 3.9 %copy-start.11 = (bf16[128,4096]{1,0:T(8,128)(2,1)}, bf16[128,4096]{1,0:T(8,128)(2,1)S(1)}, u32[]{:S(2)}) copy-start(bf16[128,4096]{1,0:T(8,128)(2,1)S(1)} %collective-permute-done.20.refs_1_) | copy-start | bytes 3145732
  186.5 22.6 %collective-permute-start.26 = (bf16[64,4096]{1,0:T(8,128)(2,1)S(1)}, bf16[64,4096]{1,0:T(8,128)(2,1)S(1)}, u32[]{:S(2)}, u32[]{:S(2)}) collective-permute-start(bf16[64,4096]{1,0:T(8,128)(2,1)S(1)} %copy-done.20), channel_id=1, source_target_pairs={{0,48},{16,0},{32,16},{48,32},{64,112},{80,64},{96,80},{112,96},{1... | collective-permute-start | bytes 1572872 | tf_op jit(solution)/shard_map/ppermute | solution.py:35
  195.5 13.7 %copy-start.12 = (bf16[64,4096]{1,0:T(8,128)(2,1)}, bf16[64,4096]{1,0:T(8,128)(2,1)S(1)}, u32[]{:S(2)}) copy-start(bf16[64,4096]{1,0:T(8,128)(2,1)S(1)} %collective-permute-done.24.refs_1_) | copy-start | bytes 1572868
  197.5 11.6 %copy-start.13 = (bf16[64,4096]{1,0:T(8,128)(2,1)}, bf16[64,4096]{1,0:T(8,128)(2,1)S(1)}, u32[]{:S(2)}) copy-start(bf16[64,4096]{1,0:T(8,128)(2,1)S(1)} %collective-permute-done.25.refs_2_) | copy-start | bytes 1572868
  209.2 0.8 copy-start.14
Sparse Core Ops, SparseCore 0:
  22.2 50.9 all-gather.1

commit v4 on v1

--- a/solution.py
+++ b/solution.py
@@ -103,7 +103,8 @@
     ]
 
 
-def hard_kernel(bases, infos, before, *rest):
+def hard_kernel(bases, before, *rest):
+    infos, rest = rest[:8], rest[8:]
     q_refs = rest[:10]
     n1, n2, e1, e2, row_sum, s1, s2, codes, acc1, acc2, sq1, sq2 = rest[10:]
     k = pl.program_id(0)
@@ -121,7 +122,7 @@
     @pl.when(k == pl.num_programs(0) - 1)
     def _():
         for slot in range(8):
-            info = infos[slot].astype(f32)
+            info = infos[slot][...].astype(f32)
             code = info[0:8, 0:128] * 256.0 + info[8:16, 0:128]
             q_scale = info[0:1, 128:256] + info[1:2, 128:256] + info[2:3, 128:256]
             codes[slot] = jnp.concatenate([code[0:7], q_scale], axis=0)
@@ -143,8 +144,9 @@
             row_sum[slot : slot + 1, :] = sums[slot]
 
 
-def hard_scores(bases, infos, before, q_refs, n1, n2, chunk=1024):
+def hard_scores(bases, before, q_refs, n1, n2, chunk=1024):
     rows, width = n1.shape
+    tails = [q for q in q_refs if q.shape[0] % 64 == 16]
     outs = (
         shape_of((rows, 1024), f32),
         shape_of((rows, 1024), f32),
@@ -156,7 +158,8 @@
     return pl.pallas_call(
         hard_kernel,
         grid=(width // chunk,),
-        in_specs=[smem_spec(), whole_spec(infos), whole_spec(before)]
+        in_specs=[smem_spec(), whole_spec(before)]
+        + [pl.BlockSpec((16, 256), lambda k, at=x.shape[0] // 16 - 1: (at, 0)) for x in tails]
         + q_specs(q_refs, chunk)
         + [cols_spec(x, chunk) for x in (n1, *n2)],
         out_specs=[whole_spec(o) for o in outs],
@@ -165,7 +168,7 @@
         compiler_params=params(),
         cost_estimate=cost(4 * rows * 1024 * width, n1, *n2, *q_refs, *outs[:2]),
         name="hard_scores",
-    )(bases, infos, before, *q_refs, n1, *n2)
+    )(bases, before, *tails, *q_refs, n1, *n2)
 
 
 def passage_rows(refs):
@@ -452,9 +455,6 @@
     side2a, side2b = hop_core(q2a), hop_core(q2b)
     q_refs = (message, q1, q2a, q2b, q3, side0, side1, side2a, side2b, side3)
     p_refs = (pc, p1, p2, p2x, p3)
-    tails = (message[128:], q1[128:], q2b[64:], q3[128:], side0[128:], side1[128:], side2b[64:], side3[128:])
-    infos = jnp.stack([x[:, :256] for x in tails])
-
     bases = jnp.stack([grp * n_pool, (grp ^ 2) * n_pool]).astype(f32)
     steps = jnp.arange(4, dtype=jnp.int32)
     y_places = (yi + steps) % 4
@@ -465,7 +465,7 @@
     about_first = jnp.concatenate([q_scale[None], pos[None], jnp.tile(zero_row, (6, 1))], axis=0)
 
     e_batch, stats, p_scales = batch_scores(places, about_first, p_refs, (queries,))
-    e1, e2, part, s1, s2, codes = hard_scores(bases, infos, stats, q_refs, pool, pool_x)
+    e1, e2, part, s1, s2, codes = hard_scores(bases, stats, q_refs, pool, pool_x)
     q_late, about_late = after((queries, about_first), pool_x[0])
     q_xa = hop_xl(q_late[:64])
     about_first_x = hop_xl(about_late)
@@ -501,17 +501,19 @@
     q_x = after((q_xa, q_xb), u_home)
     e_batch_x, _, _ = batch_scores(places, about_first_x, p_refs, q_x)
     d_home, d1, d2, d3 = passage_part(places, about, about_x, e_batch, e_batch_x, queries, q_x)
-    d_parts = (d_home, hop_y(d1, 1), hop_y(d2, 2), hop_y(d3, -1))
-
-    (e1_late, e_late) = after((e1, e_batch), d_home)
+    (e1_late,) = after((e1,), d_home)
     dn_home = pool_part(e1_late, fac, q_refs, f32)
+    (e_late,) = after((e_batch,), dn_home)
     dq_batch = query_part(places, about, e_late, p_scales, p_refs)
-    grad_passage = last_step(d_parts, passages)
+    (d2,) = after((d2,), dn_home)
+    (d3,) = after((d3,), dq_batch)
+    d_one, d_two, d_three = hop_y(d1, 1), hop_y(d2, 2), hop_y(d3, -1)
     fac_rows = jnp.broadcast_to(own_fac[:, None], (n_query, 128))
-    (dn_x,) = after((dn_x,), grad_passage)
     grad_pool = last_step((dn_home, dn_x), pool)
     (dq_batch,) = after((dq_batch,), grad_pool)
     grad_query = last_step(u_parts, queries, fac_rows, dq_batch)
+    (d_one, d_two, d_three), _ = lax.optimization_barrier(((d_one, d_two, d_three), grad_query))
+    grad_passage = last_step((d_home, d_one, d_two, d_three), passages)
     return (loss, grad_query, grad_passage, grad_pool)
 
 

time: 218 us -> 206 us (0.945)
  waiting for transfers between devices: 94.6 us -> 78.4 us
  starting transfers between devices: 29.7 us -> 39.9 us
  local copies, waits for them, and re-layouts: 11.5 us -> 7.36 us
    ppermute x10, waiting for transfers between devices: 50.7 us -> 30.4 us  [hop_z(): return lax.ppermute(x, 'grp', [(g, (g + 4 * by) % 16) for g in range(16)])]
    ppermute x2, waiting for transfers between devices: 0.01 us -> 15 us  [hop_xh(): return lax.ppermute(x, 'grp', [(g, g ^ 2) for g in range(16)])]
    ppermute x7, waiting for transfers between devices: 36.4 us -> 25.3 us  [hop_y(): lax.ppermute(x, 'loop', [(l, (l & 4) + (l + by) % 4) for l in range(8)])]
    ppermute x10, starting transfers between devices: 13.2 us -> 17.7 us  [hop_z(): return lax.ppermute(x, 'grp', [(g, (g + 4 * by) % 16) for g in range(16)])]
    ppermute x2, starting transfers between devices: 3.61 us -> 6.09 us  [hop_xh(): return lax.ppermute(x, 'grp', [(g, g ^ 2) for g in range(16)])]
    unnamed x61 -> x63, local copies, waits for them, and re-layouts: 6.47 us -> 4 us
  transfers between devices with their start and end apart: 31 -> 31, of which waited for: 12 -> 12; matrix products, arithmetic and copies ran while one was open for 7% -> 5% of each run, Pallas kernels for 27% -> 30%
where the time goes in v4:
time: 206 us
  waiting for transfers between devices  78.4 us (38%)
  Pallas kernels  70.5 us (34%)
  starting transfers between devices  39.9 us (19%)
  other arithmetic  7.48 us (4%)
  local copies, waits for them, and re-layouts  7.36 us (4%)
    ppermute x10, waiting for transfers between devices, hop_z(): return lax.ppermute(x, 'grp', [(g, (g + 4 * by) % 16) for g in range(16)])  30.4 us
    ppermute x7, waiting for transfers between devices, hop_y(): lax.ppermute(x, 'loop', [(l, (l & 4) + (l + by) % 4) for l in range(8)])  25.3 us
    ppermute x10, starting transfers between devices, hop_z(): return lax.ppermute(x, 'grp', [(g, (g + 4 * by) % 16) for g in range(16)])  17.7 us
    ppermute x2, waiting for transfers between devices, hop_xh(): return lax.ppermute(x, 'grp', [(g, g ^ 2) for g in range(16)])  15 us
    pallas_call x3, Pallas kernels, last_step(): pl.pallas_call(functools.partial(last_kernel, len(parts), fac is not None...  14.7 us
    pallas_call x2, Pallas kernels, pool_part(): pl.pallas_call(pool_kernel, grid=(width // 2048,), in_specs=[whole_spec(e...  14.1 us
    pallas_call x2, Pallas kernels, hard_back(): pl.pallas_call(functools.partial(back_kernel, first), grid=(width // 2048...  13.5 us
    pallas_call x1, Pallas kernels, hard_scores(): pl.pallas_call(hard_kernel, grid=(width // chunk,), in_specs=[smem_spec()...  11.9 us
  transfers between devices with their start and end apart: 31, of which 12 were waited for; matrix products, arithmetic and copies ran while one was open for 5% of the time, Pallas kernels for 30%

profile of v4, /device:TPU:0, one launch (start us, length us, event | category | flops | bytes accessed | tf_op | source)
XLA Modules:
  0.0 205.5 jit_solution(11285941386151751791)
XLA Ops:
  0.7 1.7 collective-permute-start
  3.0 1.5 multiply_reduce_fusion
  4.5 0.7 fusion.20
  5.2 0.7 fusion.19
  5.9 1.3 pad_maximum_fusion.rest_0_.rest_8_
  7.2 4.1 %collective-permute-start.5 = (bf16[144,4096]{1,0:T(8,128)(2,1)S(1)}, bf16[144,4096]{1,0:T(8,128)(2,1)}, u32[]{:S(2)}, u32[]{:S(2)}) collective-permute-start(bf16[144,4096]{1,0:T(8,128)(2,1)S(1)} %pad_maximum_fusion.rest_0_.rest_8_), channel_id=1, source_target_pairs={{0,12},{1,13},{2,14},{3,15},{4,0},{5,1},{6,2},{7,3},{8,4},{9,5},{1... | collective-permute-start | bytes 3538952 | tf_op jit(solution)/shard_map/ppermute | solution.py:19
  11.4 3.1 %collective-permute-done = bf16[64,4096]{1,0:T(8,128)(2,1)S(1)} collective-permute-done((bf16[64,4096]{1,0:T(8,128)(2,1)}, bf16[64,4096]{1,0:T(8,128)(2,1)S(1)}, u32[]{:S(2)}, u32[]{:S(2)}) %collective-permute-start) | collective-permute-done | bytes 524320 | tf_op jit(solution)/shard_map/ppermute | solution.py:31
  14.4 3.3 %collective-permute-start.14 = (bf16[256,4096]{1,0:T(8,128)(2,1)S(1)}, bf16[256,4096]{1,0:T(8,128)(2,1)S(1)}, u32[]{:S(2)}, u32[]{:S(2)}) collective-permute-start(bf16[256,4096]{1,0:T(8,128)(2,1)S(1)} %copy-done.2), channel_id=1, source_target_pairs={{0,2},{1,3},{2,0},{3,1},{4,6},{5,7},{6,4},{7,5},{8,10},{9,11},{10,... | collective-permute-start | bytes 6291464 | tf_op jit(solution)/shard_map/ppermute | solution.py:23
  17.8 3.1 %collective-permute-start.1 = (bf16[128,4096]{1,0:T(8,128)(2,1)S(1)}, bf16[128,4096]{1,0:T(8,128)(2,1)S(1)}, u32[]{:S(2)}, u32[]{:S(2)}) collective-permute-start(bf16[128,4096]{1,0:T(8,128)(2,1)S(1)} %constant_dynamic-update-slice_fusion.rest_0_), channel_id=1, source_target_pairs={{0,48},{16,0},{32,16},{48,32},{64,112},{80,64},{96,80},{112,96},{1... | collective-permute-start | bytes 3145736 | tf_op jit(solution)/shard_map/ppermute | solution.py:35
  20.9 15.4 %collective-permute-done.5.rest_1_.rest_9_ = bf16[144,4096]{1,0:T(8,128)(2,1)} collective-permute-done((bf16[144,4096]{1,0:T(8,128)(2,1)S(1)}, bf16[144,4096]{1,0:T(8,128)(2,1)}, u32[]{:S(2)}, u32[]{:S(2)}) %collective-permute-start.5) | collective-permute-done | bytes 1179680 | tf_op jit(solution)/shard_map/ppermute | solution.py:19
  36.3 1.6 collective-permute-start.3
  37.9 1.9 collective-permute-done.6.rest_3_.rest_12_.rest_4_
  39.8 1.1 slice.56
  41.0 1.1 slice.57
  42.1 0.2 collective-permute-done.1.rest_1_
  42.3 4.0 %collective-permute-start.9 = (bf16[64,4096]{1,0:T(8,128)(2,1)S(1)}, bf16[64,4096]{1,0:T(8,128)(2,1)}, u32[]{:S(2)}, u32[]{:S(2)}) collective-permute-start(bf16[64,4096]{1,0:T(8,128)(2,1)S(1)} %slice.57), channel_id=1, source_target_pairs={{0,12},{1,13},{2,14},{3,15},{4,0},{5,1},{6,2},{7,3},{8,4},{9,5},{1... | collective-permute-start | bytes 1572872 | tf_op jit(solution)/shard_map/ppermute | solution.py:19
  46.4 14.9 %collective-permute-done.3.rest_4_ = bf16[128,4096]{1,0:T(8,128)(2,1)S(1)} collective-permute-done((bf16[128,4096]{1,0:T(8,128)(2,1)S(1)}, bf16[128,4096]{1,0:T(8,128)(2,1)S(1)}, u32[]{:S(2)}, u32[]{:S(2)}) %collective-permute-start.3) | collective-permute-done | bytes 1048608 | tf_op jit(solution)/shard_map/ppermute | solution.py:35
  61.3 1.7 collective-permute-start.2
  63.1 0.4 collective-permute-start.4
  63.5 0.5 collective-permute-start.12
  64.0 8.8 %collective-permute-done.2.rest_2_ = bf16[64,4096]{1,0:T(8,128)(2,1)S(1)} collective-permute-done((bf16[64,4096]{1,0:T(8,128)(2,1)S(1)}, bf16[64,4096]{1,0:T(8,128)(2,1)S(1)}, u32[]{:S(2)}, u32[]{:S(2)}) %collective-permute-start.2) | collective-permute-done | bytes 524320 | tf_op jit(solution)/shard_map/ppermute | solution.py:35
  72.9 0.5 collective-permute-start.11
  73.5 0.7 copy-done.4
  74.3 1.4 collective-permute-done.4.rest_3_
  75.6 1.1 collective-permute-start.18
  76.8 0.7 fusion.25.places
  77.5 0.9 collective-permute-start.19
  78.4 0.7 add_convert_fusion.bases
  79.1 4.3 %batch_scores.2 = (f32[512,128]{1,0:T(8,128)}, f32[8,128]{1,0:T(8,128)}, f32[512,128]{1,0:T(8,128)}) custom-call(f32[8]{0:T(128)} %fusion.25.places, f32[8,128]{1,0:T(8,128)} %copy-done.24, bf16[128,4096]{1,0:T(8,128)(2,1)} %copy-done.8, bf16[128,4096]{1,0:T(8,128)(2,1)} %copy-done.6, bf16[64,4096]{1,0:T(8,128)(2,1)} %copy-done.10, ...), custom_call_target="tpu_custom_call" | custom-call | flops 1 | bytes 1 | tf_op jit(solution)/shard_map/batch_scores/pallas_call | solution.py:220
  83.4 0.8 copy-done.9
  84.2 11.9 %hard_scores.1 = (f32[256,1024]{1,0:T(8,128)}, f32[256,1024]{1,0:T(8,128)}, f32[8,128]{1,0:T(8,128)}, f32[256,128]{1,0:T(8,128)}, f32[256,128]{1,0:T(8,128)}, /*index=5*/f32[8,8,128]{2,1,0:T(8,128)}) custom-call(f32[2]{0:T(128)} %add_convert_fusion.bases, f32[8,128]{1,0:T(8,128)} %get-tuple-element.49.before, bf16[144,4096]{1,0:T(8,128)(2,1)} %copy-done.3, ...), custom_call_target="tpu_custom_call" | custom-call | flops 1 | bytes 1 | tf_op jit(solution)/shard_map/hard_scores/pallas_call | solution.py:158
  96.2 6.3 %hard_back.2 = bf16[512,4096]{1,0:T(8,128)(2,1)} custom-call(f32[256,1024]{1,0:T(8,128)} %get-tuple-element.80.e1.e, f32[256,1024]{1,0:T(8,128)} %get-tuple-element.61.e2.e, f32[256,128]{1,0:T(8,128)} %get-tuple-element.62.s1, f32[256,128]{1,0:T(8,128)} %get-tuple-element.63.s2, bf16[256,4096]{1,0:T(8,128)(2,1)} %refs_2_.1, bf16[256,4096]{1,0:T(8,128)(2,1)} %copy-done.4), custom_call_target="tpu_custom_call" | custom-call | flops 1 | bytes 1 | tf_op jit(solution)/shard_map/hard_back/pallas_call | solution.py:263
  102.5 0.1 collective-permute-start.21
  102.6 3.9 %collective-permute-start.15 = (f32[8,128]{1,0:T(8,128)S(1)}, f32[8,128]{1,0:T(8,128)S(1)}, u32[]{:S(2)}, u32[]{:S(2)}) collective-permute-start(f32[8,128]{1,0:T(8,128)S(1)} %copy-done.27), channel_id=1, source_target_pairs={{0,12},{1,13},{2,14},{3,15},{4,0},{5,1},{6,2},{7,3},{8,4},{9,5},{1... | collective-permute-start | bytes 12296 | tf_op jit(solution)/shard_map/ppermute | solution.py:19
  106.5 0.9 collective-permute-start.17
  107.4 0.4 collective-permute-done.15
  107.8 3.8 %collective-permute-done.16 = f32[8,128]{1,0:T(8,128)S(1)} collective-permute-done((f32[8,128]{1,0:T(8,128)S(1)}, f32[8,128]{1,0:T(8,128)S(1)}, u32[]{:S(2)}, u32[]{:S(2)}) %collective-permute-start.16) | collective-permute-done | bytes 4128 | tf_op jit(solution)/shard_map/ppermute | solution.py:19
  111.8 1.2 collective-permute-start.23
  113.1 1.1 collective-permute-start.22
  114.2 0.6 fusion.16.fac
  114.8 6.9 %pool_part.2 = bf16[256,4096]{1,0:T(8,128)(2,1)} custom-call(f32[256,1024]{1,0:T(8,128)} %get-tuple-element.61.e2.e, f32[8,128]{1,0:T(8,128)} %fusion.16.fac, bf16[144,4096]{1,0:T(8,128)(2,1)} %copy-done.3, bf16[144,4096]{1,0:T(8,128)(2,1)} %collective-permute-done.5.rest_1_.rest_9_, bf16[64,4096]{1,0:T(8,128)(2,1)} %collective-permute-done.9.rest_10_.rest_2_, ...), custom_call_target="tpu_custom_call" | custom-call | flops 1 | bytes 1 | tf_op jit(solution)/shard_map/pool_part/pallas_call | solution.py:294
  121.7 4.6 %collective-permute-done.22.about_b = f32[8,128]{1,0:T(8,128)S(1)} collective-permute-done((f32[8,128]{1,0:T(8,128)S(1)}, f32[8,128]{1,0:T(8,128)S(1)}, u32[]{:S(2)}, u32[]{:S(2)}) %collective-permute-start.22) | collective-permute-done | bytes 4128 | tf_op jit(solution)/shard_map/ppermute | solution.py:31
  126.3 2.8 %collective-permute-start.27 = (bf16[256,4096]{1,0:T(8,128)(2,1)}, bf16[256,4096]{1,0:T(8,128)(2,1)S(1)}, u32[]{:S(2)}, u32[]{:S(2)}) collective-permute-start(bf16[256,4096]{1,0:T(8,128)(2,1)} %pool_part.2), channel_id=1, source_target_pairs={{0,2},{1,3},{2,0},{3,1},{4,6},{5,7},{6,4},{7,5},{8,10},{9,11},{10,... | collective-permute-start | bytes 6291464 | tf_op jit(solution)/shard_map/ppermute | solution.py:23
  129.1 7.2 %hard_back.3 = (f32[128,4096]{1,0:T(8,128)}, bf16[128,4096]{1,0:T(8,128)(2,1)}, bf16[128,4096]{1,0:T(8,128)(2,1)}, bf16[128,4096]{1,0:T(8,128)(2,1)}) custom-call(f32[256,1024]{1,0:T(8,128)} %get-tuple-element.80.e1.e, f32[256,1024]{1,0:T(8,128)} %get-tuple-element.61.e2.e, f32[256,128]{1,0:T(8,128)} %get-tuple-element.62.s1, ...), custom_call_target="tpu_custom_call" | custom-call | flops 1 | bytes 1 | tf_op jit(solution)/shard_map/hard_back/pallas_call | solution.py:263
  136.4 2.1 %collective-permute-start.25 = (bf16[128,4096]{1,0:T(8,128)(2,1)}, bf16[128,4096]{1,0:T(8,128)(2,1)S(1)}, u32[]{:S(2)}, u32[]{:S(2)}) collective-permute-start(bf16[128,4096]{1,0:T(8,128)(2,1)} %get-tuple-element.73), channel_id=1, source_target_pairs={{0,8},{1,9},{2,10},{3,11},{4,12},{5,13},{6,14},{7,15},{8,0},{9,1},... | collective-permute-start | bytes 3145736 | tf_op jit(solution)/shard_map/ppermute | solution.py:19
  138.5 2.5 %collective-permute-start.26 = (bf16[128,4096]{1,0:T(8,128)(2,1)}, bf16[128,4096]{1,0:T(8,128)(2,1)S(1)}, u32[]{:S(2)}, u32[]{:S(2)}) collective-permute-start(bf16[128,4096]{1,0:T(8,128)(2,1)} %get-tuple-element.74), channel_id=1, source_target_pairs={{0,12},{1,13},{2,14},{3,15},{4,0},{5,1},{6,2},{7,3},{8,4},{9,5},{1... | collective-permute-start | bytes 3145736 | tf_op jit(solution)/shard_map/ppermute | solution.py:19
  141.1 4.4 %batch_scores.3 = (f32[512,128]{1,0:T(8,128)}, f32[8,128]{1,0:T(8,128)}, f32[512,128]{1,0:T(8,128)}) custom-call(f32[8]{0:T(128)} %fusion.25.places, f32[8,128]{1,0:T(8,128)} %copy-done.25, bf16[128,4096]{1,0:T(8,128)(2,1)} %copy-done.8, bf16[128,4096]{1,0:T(8,128)(2,1)} %copy-done.6, bf16[64,4096]{1,0:T(8,128)(2,1)} %copy-done.10, ...), custom_call_target="tpu_custom_call" | custom-call | flops 1 | bytes 1 | tf_op jit(solution)/shard_map/batch_scores/pallas_call | solution.py:220
  145.5 3.4 %passage_part.1 = (f32[64,4096]{1,0:T(8,128)}, bf16[64,4096]{1,0:T(8,128)(2,1)}, bf16[64,4096]{1,0:T(8,128)(2,1)}, bf16[64,4096]{1,0:T(8,128)(2,1)}) custom-call(f32[8]{0:T(128)} %fusion.25.places, f32[8,128]{1,0:T(8,128)} %copy-done.22, f32[8,128]{1,0:T(8,128)} %copy-done.26, f32[512,128]{1,0:T(8,128)} %get-tuple-element.81.e_a.e, ...), custom_call_target="tpu_custom_call" | custom-call | flops 1 | bytes 1 | tf_op jit(solution)/shard_map/passage_part/pallas_call | solution.py:359
  148.9 7.2 %pool_part.3.refs_0_ = f32[256,4096]{1,0:T(8,128)} custom-call(f32[256,1024]{1,0:T(8,128)} %get-tuple-element.80.e1.e, f32[8,128]{1,0:T(8,128)} %fusion.16.fac, bf16[144,4096]{1,0:T(8,128)(2,1)} %copy-done.3, bf16[144,4096]{1,0:T(8,128)(2,1)} %collective-permute-done.5.rest_1_.rest_9_, bf16[64,4096]{1,0:T(8,128)(2,1)} %collective-permute-done.9.rest_10_.rest_2_, ...), custom_call_target="tpu_custom_call" | custom-call | flops 1 | bytes 1 | tf_op jit(solution)/shard_map/pool_part/pallas_call | solution.py:294
  156.2 4.2 %query_part.1.refs_5_ = f32[128,4096]{1,0:T(8,128)} custom-call(f32[8]{0:T(128)} %fusion.25.places, f32[8,128]{1,0:T(8,128)} %copy-done.22, f32[512,128]{1,0:T(8,128)} %get-tuple-element.81.e_a.e, f32[512,128]{1,0:T(8,128)} %get-tuple-element.82.scales, bf16[128,4096]{1,0:T(8,128)(2,1)} %copy-done.8, bf16[128,4096]{1,0:T(8,128)(2,1)} %copy-done.6, ...), custom_call_target="tpu_custom_call" | custom-call | flops 1 | bytes 1 | tf_op jit(solution)/shard_map/query_part/pallas_call | solution.py:325
  160.4 15.0 %collective-permute-done.27.refs_1_ = bf16[256,4096]{1,0:T(8,128)(2,1)S(1)} collective-permute-done((bf16[256,4096]{1,0:T(8,128)(2,1)}, bf16[256,4096]{1,0:T(8,128)(2,1)S(1)}, u32[]{:S(2)}, u32[]{:S(2)}) %collective-permute-start.27) | collective-permute-done | bytes 2097184 | tf_op jit(solution)/shard_map/ppermute | solution.py:23
  175.3 0.6 collective-permute-start.29
  175.9 8.9 %collective-permute-done.24.refs_1_ = bf16[128,4096]{1,0:T(8,128)(2,1)S(1)} collective-permute-done((bf16[128,4096]{1,0:T(8,128)(2,1)}, bf16[128,4096]{1,0:T(8,128)(2,1)S(1)}, u32[]{:S(2)}, u32[]{:S(2)}) %collective-permute-start.24) | collective-permute-done | bytes 1048608 | tf_op jit(solution)/shard_map/ppermute | solution.py:19
  184.8 1.6 collective-permute-start.30
  186.4 1.2 fusion.21
  187.6 6.3 %last_step.3 = f32[256,4096]{1,0:T(8,128)} custom-call(f32[256,4096]{1,0:T(8,128)} %pool_part.3.refs_0_, bf16[256,4096]{1,0:T(8,128)(2,1)} %copy-done.14, bf16[256,4096]{1,0:T(8,128)(2,1)} %refs_2_.1), custom_call_target="tpu_custom_call" | custom-call | flops 1 | bytes 1 | tf_op jit(solution)/shard_map/last_step/pallas_call | solution.py:405
  193.9 0.8 broadcast_in_dim.19.refs_4_
  194.8 0.2 copy-done.17
  194.9 0.4 copy-done.18
  195.3 5.0 %last_step.4 = f32[128,4096]{1,0:T(8,128)} custom-call(f32[128,4096]{1,0:T(8,128)} %get-tuple-element.71.refs_0_, bf16[128,4096]{1,0:T(8,128)(2,1)} %copy-done.16, bf16[128,4096]{1,0:T(8,128)(2,1)} %copy-done.17, bf16[128,4096]{1,0:T(8,128)(2,1)} %copy-done.18, f32[128,128]{1,0:T(8,128)} %broadcast_in_dim.19.refs_4_, f32[128,4096]{1,0:T(8,128)} %query_part.1.refs_5_, ...), custom_call_target="tpu_custom_call" | custom-call | flops 1 | bytes 1 | tf_op jit(solution)/shard_map/last_step/pallas_call | solution.py:405
  200.4 0.8 copy-done.19
  201.1 0.2 copy-done.20
  201.3 0.8 copy-done.21
  202.1 3.4 %last_step.5 = f32[64,4096]{1,0:T(8,128)} custom-call(f32[64,4096]{1,0:T(8,128)} %get-tuple-element.79.refs_0_, bf16[64,4096]{1,0:T(8,128)(2,1)} %copy-done.19, bf16[64,4096]{1,0:T(8,128)(2,1)} %copy-done.20, bf16[64,4096]{1,0:T(8,128)(2,1)} %copy-done.21, bf16[64,4096]{1,0:T(8,128)(2,1)} %refs_4_.1), custom_call_target="tpu_custom_call" | custom-call | flops 1 | bytes 1 | tf_op jit(solution)/shard_map/last_step/pallas_call | solution.py:405
  (111 shorter events, 1.0 us)
Async XLA Ops:
  0.6 17.1 %copy-start.15 = (bf16[64,4096]{1,0:T(8,128)(2,1)S(1)}, bf16[64,4096]{1,0:T(8,128)(2,1)}, u32[]{:S(2)}) copy-start(bf16[64,4096]{1,0:T(8,128)(2,1)} %refs_4_.1) | copy-start | bytes 1572868
  0.6 13.8 %copy-start.2 = (bf16[256,4096]{1,0:T(8,128)(2,1)S(1)}, bf16[256,4096]{1,0:T(8,128)(2,1)}, u32[]{:S(2)}) copy-start(bf16[256,4096]{1,0:T(8,128)(2,1)} %refs_2_.1) | copy-start | bytes 6291460
  0.7 13.8 %collective-permute-start = (bf16[64,4096]{1,0:T(8,128)(2,1)}, bf16[64,4096]{1,0:T(8,128)(2,1)S(1)}, u32[]{:S(2)}, u32[]{:S(2)}) collective-permute-start(bf16[64,4096]{1,0:T(8,128)(2,1)} %refs_4_.1), channel_id=1, source_target_pairs={{0,64},{16,80},{32,96},{48,112},{64,0},{80,16},{96,32},{112,48},{1... | collective-permute-start | bytes 1572872 | tf_op jit(solution)/shard_map/ppermute | solution.py:31
  7.2 34.9 %copy-start.3 = (bf16[144,4096]{1,0:T(8,128)(2,1)}, bf16[144,4096]{1,0:T(8,128)(2,1)S(1)}, u32[]{:S(2)}) copy-start(bf16[144,4096]{1,0:T(8,128)(2,1)S(1)} %pad_maximum_fusion.rest_0_.rest_8_) | copy-start | bytes 3538948
  7.2 29.1 %collective-permute-start.5 = (bf16[144,4096]{1,0:T(8,128)(2,1)S(1)}, bf16[144,4096]{1,0:T(8,128)(2,1)}, u32[]{:S(2)}, u32[]{:S(2)}) collective-permute-start(bf16[144,4096]{1,0:T(8,128)(2,1)S(1)} %pad_maximum_fusion.rest_0_.rest_8_), channel_id=1, source_target_pairs={{0,12},{1,13},{2,14},{3,15},{4,0},{5,1},{6,2},{7,3},{8,4},{9,5},{1... | collective-permute-start | bytes 3538952 | tf_op jit(solution)/shard_map/ppermute | solution.py:19
  11.4 28.5 %collective-permute-start.6 = (bf16[144,4096]{1,0:T(8,128)(2,1)S(1)}, bf16[144,4096]{1,0:T(8,128)(2,1)}, u32[]{:S(2)}, u32[]{:S(2)}) collective-permute-start(bf16[144,4096]{1,0:T(8,128)(2,1)S(1)} %pad_maximum_fusion.rest_0_.rest_8_), channel_id=1, source_target_pairs={{0,4},{1,5},{2,6},{3,7},{4,8},{5,9},{6,10},{7,11},{8,12},{9,13},{1... | collective-permute-start | bytes 3538952 | tf_op jit(solution)/shard_map/ppermute | solution.py:19
  14.4 58.5 %collective-permute-start.14 = (bf16[256,4096]{1,0:T(8,128)(2,1)S(1)}, bf16[256,4096]{1,0:T(8,128)(2,1)S(1)}, u32[]{:S(2)}, u32[]{:S(2)}) collective-permute-start(bf16[256,4096]{1,0:T(8,128)(2,1)S(1)} %copy-done.2), channel_id=1, source_target_pairs={{0,2},{1,3},{2,0},{3,1},{4,6},{5,7},{6,4},{7,5},{8,10},{9,11},{10,... | collective-permute-start | bytes 6291464 | tf_op jit(solution)/shard_map/ppermute | solution.py:23
  17.8 45.3 %copy-start.8 = (bf16[128,4096]{1,0:T(8,128)(2,1)}, bf16[128,4096]{1,0:T(8,128)(2,1)S(1)}, u32[]{:S(2)}) copy-start(bf16[128,4096]{1,0:T(8,128)(2,1)S(1)} %constant_dynamic-update-slice_fusion.rest_0_) | copy-start | bytes 3145732
  17.8 46.2 %copy-start.30 = (s32[128]{0:T(128)S(1)}, s32[128]{0:T(128)}, u32[]{:S(2)}) copy-start(s32[128]{0:T(128)} %param.11) | copy-start | bytes 1540
  17.8 55.7 %copy-start = (bf16[128,4096]{1,0:T(8,128)(2,1)S(1)}, bf16[128,4096]{1,0:T(8,128)(2,1)}, u32[]{:S(2)}) copy-start(bf16[128,4096]{1,0:T(8,128)(2,1)} %refs_6_.1) | copy-start | bytes 3145732
  17.8 24.5 %collective-permute-start.1 = (bf16[128,4096]{1,0:T(8,128)(2,1)S(1)}, bf16[128,4096]{1,0:T(8,128)(2,1)S(1)}, u32[]{:S(2)}, u32[]{:S(2)}) collective-permute-start(bf16[128,4096]{1,0:T(8,128)(2,1)S(1)} %constant_dynamic-update-slice_fusion.rest_0_), channel_id=1, source_target_pairs={{0,48},{16,0},{32,16},{48,32},{64,112},{80,64},{96,80},{112,96},{1... | collective-permute-start | bytes 3145736 | tf_op jit(solution)/shard_map/ppermute | solution.py:35
  20.9 42.5 %collective-permute-start.8 = (bf16[144,4096]{1,0:T(8,128)(2,1)S(1)}, bf16[144,4096]{1,0:T(8,128)(2,1)S(1)}, u32[]{:S(2)}, u32[]{:S(2)}) collective-permute-start(bf16[144,4096]{1,0:T(8,128)(2,1)S(1)} %pad_maximum_fusion.rest_0_.rest_8_), channel_id=1, source_target_pairs={{0,1},{1,0},{2,3},{3,2},{4,5},{5,4},{6,7},{7,6},{8,9},{9,8},{10,11... | collective-permute-start | bytes 3538952 | tf_op jit(solution)/shard_map/ppermute | solution.py:27
  36.3 25.0 %collective-permute-start.3 = (bf16[128,4096]{1,0:T(8,128)(2,1)S(1)}, bf16[128,4096]{1,0:T(8,128)(2,1)S(1)}, u32[]{:S(2)}, u32[]{:S(2)}) collective-permute-start(bf16[128,4096]{1,0:T(8,128)(2,1)S(1)} %constant_dynamic-update-slice_fusion.rest_0_), channel_id=1, source_target_pairs={{0,16},{16,32},{32,48},{48,0},{64,80},{80,96},{96,112},{112,64},{1... | collective-permute-start | bytes 3145736 | tf_op jit(solution)/shard_map/ppermute | solution.py:35
  41.0 22.5 %collective-permute-start.7 = (bf16[80,4096]{1,0:T(8,128)(2,1)S(1)}, bf16[80,4096]{1,0:T(8,128)(2,1)}, u32[]{:S(2)}, u32[]{:S(2)}) collective-permute-start(bf16[80,4096]{1,0:T(8,128)(2,1)S(1)} %slice.56), channel_id=1, source_target_pairs={{0,4},{1,5},{2,6},{3,7},{4,8},{5,9},{6,10},{7,11},{8,12},{9,13},{1... | collective-permute-start | bytes 1966088 | tf_op jit(solution)/shard_map/ppermute | solution.py:19
  42.3 34.5 %copy-start.6 = (bf16[128,4096]{1,0:T(8,128)(2,1)}, bf16[128,4096]{1,0:T(8,128)(2,1)S(1)}, u32[]{:S(2)}) copy-start(bf16[128,4096]{1,0:T(8,128)(2,1)S(1)} %collective-permute-done.1.rest_1_) | copy-start | bytes 3145732
  42.3 20.8 %collective-permute-start.9 = (bf16[64,4096]{1,0:T(8,128)(2,1)S(1)}, bf16[64,4096]{1,0:T(8,128)(2,1)}, u32[]{:S(2)}, u32[]{:S(2)}) collective-permute-start(bf16[64,4096]{1,0:T(8,128)(2,1)S(1)} %slice.57), channel_id=1, source_target_pairs={{0,12},{1,13},{2,14},{3,15},{4,0},{5,1},{6,2},{7,3},{8,4},{9,5},{1... | collective-permute-start | bytes 1572872 | tf_op jit(solution)/shard_map/ppermute | solution.py:19
  61.3 15.5 %copy-start.7 = (bf16[128,4096]{1,0:T(8,128)(2,1)}, bf16[128,4096]{1,0:T(8,128)(2,1)S(1)}, u32[]{:S(2)}) copy-start(bf16[128,4096]{1,0:T(8,128)(2,1)S(1)} %collective-permute-done.3.rest_4_) | copy-start | bytes 3145732
  61.3 11.6 %collective-permute-start.2 = (bf16[64,4096]{1,0:T(8,128)(2,1)S(1)}, bf16[64,4096]{1,0:T(8,128)(2,1)S(1)}, u32[]{:S(2)}, u32[]{:S(2)}) collective-permute-start(bf16[64,4096]{1,0:T(8,128)(2,1)S(1)} %slice.70), channel_id=1, source_target_pairs={{0,48},{16,0},{32,16},{48,32},{64,112},{80,64},{96,80},{112,96},{1... | collective-permute-start | bytes 1572872 | tf_op jit(solution)/shard_map/ppermute | solution.py:35
  63.1 12.6 %collective-permute-start.4 = (bf16[64,4096]{1,0:T(8,128)(2,1)S(1)}, bf16[64,4096]{1,0:T(8,128)(2,1)S(1)}, u32[]{:S(2)}, u32[]{:S(2)}) collective-permute-start(bf16[64,4096]{1,0:T(8,128)(2,1)S(1)} %slice.71), channel_id=1, source_target_pairs={{0,16},{16,32},{32,48},{48,0},{64,80},{80,96},{96,112},{112,64},{1... | collective-permute-start | bytes 1572872 | tf_op jit(solution)/shard_map/ppermute | solution.py:35
  63.4 19.9 %collective-permute-start.10 = (bf16[144,4096]{1,0:T(8,128)(2,1)}, bf16[144,4096]{1,0:T(8,128)(2,1)}, u32[]{:S(2)}, u32[]{:S(2)}) collective-permute-start(bf16[144,4096]{1,0:T(8,128)(2,1)} %collective-permute-done.5.rest_1_.rest_9_), channel_id=1, source_target_pairs={{0,1},{1,0},{2,3},{3,2},{4,5},{5,4},{6,7},{7,6},{8,9},{9,8},{10,11... | collective-permute-start | bytes 3538952 | tf_op jit(solution)/shard_map/ppermute | solution.py:27
  63.5 12.2 %copy-start.5 = (bf16[144,4096]{1,0:T(8,128)(2,1)}, bf16[144,4096]{1,0:T(8,128)(2,1)S(1)}, u32[]{:S(2)}) copy-start(bf16[144,4096]{1,0:T(8,128)(2,1)S(1)} %collective-permute-done.8.rest_4_.rest_13_.rest_5_) | copy-start | bytes 3538948
  63.5 19.9 %collective-permute-start.12 = (bf16[144,4096]{1,0:T(8,128)(2,1)}, bf16[144,4096]{1,0:T(8,128)(2,1)}, u32[]{:S(2)}, u32[]{:S(2)}) collective-permute-start(bf16[144,4096]{1,0:T(8,128)(2,1)} %collective-permute-done.6.rest_3_.rest_12_.rest_4_), channel_id=1, source_target_pairs={{0,1},{1,0},{2,3},{3,2},{4,5},{5,4},{6,7},{7,6},{8,9},{9,8},{10,11... | collective-permute-start | bytes 3538952 | tf_op jit(solution)/shard_map/ppermute | solution.py:27
  72.9 3.9 %copy-start.10 = (bf16[64,4096]{1,0:T(8,128)(2,1)}, bf16[64,4096]{1,0:T(8,128)(2,1)S(1)}, u32[]{:S(2)}) copy-start(bf16[64,4096]{1,0:T(8,128)(2,1)S(1)} %collective-permute-done.2.rest_2_) | copy-start | bytes 1572868
  72.9 4.6 %collective-permute-start.13 = (bf16[64,4096]{1,0:T(8,128)(2,1)}, bf16[64,4096]{1,0:T(8,128)(2,1)}, u32[]{:S(2)}, u32[]{:S(2)}) collective-permute-start(bf16[64,4096]{1,0:T(8,128)(2,1)} %collective-permute-done.9.rest_10_.rest_2_), channel_id=1, source_target_pairs={{0,1},{1,0},{2,3},{3,2},{4,5},{5,4},{6,7},{7,6},{8,9},{9,8},{10,11... | collective-permute-start | bytes 1572872 | tf_op jit(solution)/shard_map/ppermute | solution.py:27
  72.9 1.3 copy-start.4
  72.9 10.4 %collective-permute-start.11 = (bf16[80,4096]{1,0:T(8,128)(2,1)}, bf16[80,4096]{1,0:T(8,128)(2,1)S(1)}, u32[]{:S(2)}, u32[]{:S(2)}) collective-permute-start(bf16[80,4096]{1,0:T(8,128)(2,1)} %collective-permute-done.7.rest_2_.rest_11_.rest_3_), channel_id=1, source_target_pairs={{0,1},{1,0},{2,3},{3,2},{4,5},{5,4},{6,7},{7,6},{8,9},{9,8},{10,11... | collective-permute-start | bytes 1966088 | tf_op jit(solution)/shard_map/ppermute | solution.py:27
  73.5 5.6 %copy-start.24 = (f32[8,128]{1,0:T(8,128)}, f32[8,128]{1,0:T(8,128)S(1)}, u32[]{:S(2)}) copy-start(f32[8,128]{1,0:T(8,128)S(1)} %maximum_maximum_fusion.about) | copy-start | bytes 12292
  75.6 1.2 copy-start.11
  75.6 20.5 %collective-permute-start.18 = (bf16[64,4096]{1,0:T(8,128)(2,1)S(1)}, bf16[64,4096]{1,0:T(8,128)(2,1)S(1)}, u32[]{:S(2)}, u32[]{:S(2)}) collective-permute-start(bf16[64,4096]{1,0:T(8,128)(2,1)S(1)} %slice.58), channel_id=1, source_target_pairs={{0,64},{16,80},{32,96},{48,112},{64,0},{80,16},{96,32},{112,48},{1... | collective-permute-start | bytes 1572872 | tf_op jit(solution)/shard_map/ppermute | solution.py:31
  77.5 18.6 %collective-permute-start.19 = (f32[8,128]{1,0:T(8,128)S(1)}, f32[8,128]{1,0:T(8,128)S(1)}, u32[]{:S(2)}, u32[]{:S(2)}) collective-permute-start(f32[8,128]{1,0:T(8,128)S(1)} %maximum_maximum_fusion.about), channel_id=1, source_target_pairs={{0,64},{16,80},{32,96},{48,112},{64,0},{80,16},{96,32},{112,48},{1... | collective-permute-start | bytes 12296 | tf_op jit(solution)/shard_map/ppermute | solution.py:31
  83.3 0.9 copy-start.9
  96.1 6.4 %copy-start.25 = (f32[8,128]{1,0:T(8,128)}, f32[8,128]{1,0:T(8,128)S(1)}, u32[]{:S(2)}) copy-start(f32[8,128]{1,0:T(8,128)S(1)} %collective-permute-done.19.about) | copy-start | bytes 12292
  96.2 6.4 %copy-start.12 = (bf16[64,4096]{1,0:T(8,128)(2,1)}, bf16[64,4096]{1,0:T(8,128)(2,1)S(1)}, u32[]{:S(2)}) copy-start(bf16[64,4096]{1,0:T(8,128)(2,1)S(1)} %collective-permute-done.18.rest_5_.q_b) | copy-start | bytes 1572868
  96.2 6.5 %copy-start.27 = (f32[8,128]{1,0:T(8,128)S(1)}, f32[8,128]{1,0:T(8,128)}, u32[]{:S(2)}) copy-start(f32[8,128]{1,0:T(8,128)} %get-tuple-element.55) | copy-start | bytes 12292
  96.2 15.6 %copy-start.23 = (f32[8,8,128]{2,1,0:T(8,128)S(1)}, f32[8,8,128]{2,1,0:T(8,128)}, u32[]{:S(2)}) copy-start(f32[8,8,128]{2,1,0:T(8,128)} %get-tuple-element.67) | copy-start | bytes 98308
  96.2 15.6 %copy-start.1 = (bf16[128,4096]{1,0:T(8,128)(2,1)S(1)}, bf16[128,4096]{1,0:T(8,128)(2,1)}, u32[]{:S(2)}) copy-start(bf16[128,4096]{1,0:T(8,128)(2,1)} %refs_6_.1) | copy-start | bytes 3145732
  102.5 26.6 %collective-permute-start.21 = (bf16[512,4096]{1,0:T(8,128)(2,1)}, bf16[512,4096]{1,0:T(8,128)(2,1)}, u32[]{:S(2)}, u32[]{:S(2)}) collective-permute-start(bf16[512,4096]{1,0:T(8,128)(2,1)} %hard_back.2), channel_id=1, source_target_pairs={{0,1},{1,0},{2,3},{3,2},{4,5},{5,4},{6,7},{7,6},{8,9},{9,8},{10,11... | collective-permute-start | bytes 12582920 | tf_op jit(solution)/shard_map/ppermute | solution.py:27
  102.6 5.2 %collective-permute-start.15 = (f32[8,128]{1,0:T(8,128)S(1)}, f32[8,128]{1,0:T(8,128)S(1)}, u32[]{:S(2)}, u32[]{:S(2)}) collective-permute-start(f32[8,128]{1,0:T(8,128)S(1)} %copy-done.27), channel_id=1, source_target_pairs={{0,12},{1,13},{2,14},{3,15},{4,0},{5,1},{6,2},{7,3},{8,4},{9,5},{1... | collective-permute-start | bytes 12296 | tf_op jit(solution)/shard_map/ppermute | solution.py:19
  106.5 5.1 %collective-permute-start.16 = (f32[8,128]{1,0:T(8,128)S(1)}, f32[8,128]{1,0:T(8,128)S(1)}, u32[]{:S(2)}, u32[]{:S(2)}) collective-permute-start(f32[8,128]{1,0:T(8,128)S(1)} %copy-done.27), channel_id=1, source_target_pairs={{0,8},{1,9},{2,10},{3,11},{4,12},{5,13},{6,14},{7,15},{8,0},{9,1},... | collective-permute-start | bytes 12296 | tf_op jit(solution)/shard_map/ppermute | solution.py:19
  106.5 5.1 %collective-permute-start.17 = (f32[8,128]{1,0:T(8,128)S(1)}, f32[8,128]{1,0:T(8,128)S(1)}, u32[]{:S(2)}, u32[]{:S(2)}) collective-permute-start(f32[8,128]{1,0:T(8,128)S(1)} %copy-done.27), channel_id=1, source_target_pairs={{0,4},{1,5},{2,6},{3,7},{4,8},{5,9},{6,10},{7,11},{8,12},{9,13},{1... | collective-permute-start | bytes 12296 | tf_op jit(solution)/shard_map/ppermute | solution.py:19
  111.7 1.4 collective-permute-start.20
  111.8 14.5 %collective-permute-start.23 = (bf16[64,4096]{1,0:T(8,128)(2,1)S(1)}, bf16[64,4096]{1,0:T(8,128)(2,1)S(1)}, u32[]{:S(2)}, u32[]{:S(2)}) collective-permute-start(bf16[64,4096]{1,0:T(8,128)(2,1)S(1)} %slice.69), channel_id=1, source_target_pairs={{0,64},{16,80},{32,96},{48,112},{64,0},{80,16},{96,32},{112,48},{1... | collective-permute-start | bytes 1572872 | tf_op jit(solution)/shard_map/ppermute | solution.py:31
  113.1 8.6 %copy-start.22 = (f32[8,128]{1,0:T(8,128)}, f32[8,128]{1,0:T(8,128)S(1)}, u32[]{:S(2)}) copy-start(f32[8,128]{1,0:T(8,128)S(1)} %concatenate.49.about_a.about) | copy-start | bytes 12292
  113.1 13.2 %collective-permute-start.22 = (f32[8,128]{1,0:T(8,128)S(1)}, f32[8,128]{1,0:T(8,128)S(1)}, u32[]{:S(2)}, u32[]{:S(2)}) collective-permute-start(f32[8,128]{1,0:T(8,128)S(1)} %concatenate.49.about_a.about), channel_id=1, source_target_pairs={{0,64},{16,80},{32,96},{48,112},{64,0},{80,16},{96,32},{112,48},{1... | collective-permute-start | bytes 12296 | tf_op jit(solution)/shard_map/ppermute | solution.py:31
  126.3 10.0 %copy-start.26 = (f32[8,128]{1,0:T(8,128)}, f32[8,128]{1,0:T(8,128)S(1)}, u32[]{:S(2)}) copy-start(f32[8,128]{1,0:T(8,128)S(1)} %collective-permute-done.22.about_b) | copy-start | bytes 12292
  126.3 10.0 %copy-start.13 = (bf16[64,4096]{1,0:T(8,128)(2,1)}, bf16[64,4096]{1,0:T(8,128)(2,1)S(1)}, u32[]{:S(2)}) copy-start(bf16[64,4096]{1,0:T(8,128)(2,1)S(1)} %collective-permute-done.23.rest_6_.q_c) | copy-start | bytes 1572868
  126.3 49.0 %collective-permute-start.27 = (bf16[256,4096]{1,0:T(8,128)(2,1)}, bf16[256,4096]{1,0:T(8,128)(2,1)S(1)}, u32[]{:S(2)}, u32[]{:S(2)}) collective-permute-start(bf16[256,4096]{1,0:T(8,128)(2,1)} %pool_part.2), channel_id=1, source_target_pairs={{0,2},{1,3},{2,0},{3,1},{4,6},{5,7},{6,4},{7,5},{8,10},{9,11},{10,... | collective-permute-start | bytes 6291464 | tf_op jit(solution)/shard_map/ppermute | solution.py:23
  136.4 48.4 %collective-permute-start.24 = (bf16[128,4096]{1,0:T(8,128)(2,1)}, bf16[128,4096]{1,0:T(8,128)(2,1)S(1)}, u32[]{:S(2)}, u32[]{:S(2)}) collective-permute-start(bf16[128,4096]{1,0:T(8,128)(2,1)} %get-tuple-element.72), channel_id=1, source_target_pairs={{0,4},{1,5},{2,6},{3,7},{4,8},{5,9},{6,10},{7,11},{8,12},{9,13},{1... | collective-permute-start | bytes 3145736 | tf_op jit(solution)/shard_map/ppermute | solution.py:19
  136.4 57.5 %collective-permute-start.25 = (bf16[128,4096]{1,0:T(8,128)(2,1)}, bf16[128,4096]{1,0:T(8,128)(2,1)S(1)}, u32[]{:S(2)}, u32[]{:S(2)}) collective-permute-start(bf16[128,4096]{1,0:T(8,128)(2,1)} %get-tuple-element.73), channel_id=1, source_target_pairs={{0,8},{1,9},{2,10},{3,11},{4,12},{5,13},{6,14},{7,15},{8,0},{9,1},... | collective-permute-start | bytes 3145736 | tf_op jit(solution)/shard_map/ppermute | solution.py:19
  138.5 55.4 %collective-permute-start.26 = (bf16[128,4096]{1,0:T(8,128)(2,1)}, bf16[128,4096]{1,0:T(8,128)(2,1)S(1)}, u32[]{:S(2)}, u32[]{:S(2)}) collective-permute-start(bf16[128,4096]{1,0:T(8,128)(2,1)} %get-tuple-element.74), channel_id=1, source_target_pairs={{0,12},{1,13},{2,14},{3,15},{4,0},{5,1},{6,2},{7,3},{8,4},{9,5},{1... | collective-permute-start | bytes 3145736 | tf_op jit(solution)/shard_map/ppermute | solution.py:19
  156.1 44.2 %collective-permute-start.28 = (bf16[64,4096]{1,0:T(8,128)(2,1)}, bf16[64,4096]{1,0:T(8,128)(2,1)S(1)}, u32[]{:S(2)}, u32[]{:S(2)}) collective-permute-start(bf16[64,4096]{1,0:T(8,128)(2,1)} %get-tuple-element.84), channel_id=1, source_target_pairs={{0,16},{16,32},{32,48},{48,0},{64,80},{80,96},{96,112},{112,64},{1... | collective-permute-start | bytes 1572872 | tf_op jit(solution)/shard_map/ppermute | solution.py:35
  156.2 19.2 %copy-start.29 = (bf16[64,4096]{1,0:T(8,128)(2,1)S(1)}, bf16[64,4096]{1,0:T(8,128)(2,1)}, u32[]{:S(2)}) copy-start(bf16[64,4096]{1,0:T(8,128)(2,1)} %get-tuple-element.86) | copy-start | bytes 1572868
  156.2 28.6 %copy-start.28 = (bf16[64,4096]{1,0:T(8,128)(2,1)S(1)}, bf16[64,4096]{1,0:T(8,128)(2,1)}, u32[]{:S(2)}) copy-start(bf16[64,4096]{1,0:T(8,128)(2,1)} %get-tuple-element.88) | copy-start | bytes 1572868
  175.3 12.2 %copy-start.14 = (bf16[256,4096]{1,0:T(8,128)(2,1)}, bf16[256,4096]{1,0:T(8,128)(2,1)S(1)}, u32[]{:S(2)}) copy-start(bf16[256,4096]{1,0:T(8,128)(2,1)S(1)} %collective-permute-done.27.refs_1_) | copy-start | bytes 6291460
  175.3 25.0 %collective-permute-start.29 = (bf16[64,4096]{1,0:T(8,128)(2,1)S(1)}, bf16[64,4096]{1,0:T(8,128)(2,1)S(1)}, u32[]{:S(2)}, u32[]{:S(2)}) collective-permute-start(bf16[64,4096]{1,0:T(8,128)(2,1)S(1)} %copy-done.29), channel_id=1, source_target_pairs={{0,32},{16,48},{32,0},{48,16},{64,96},{80,112},{96,64},{112,80},{1... | collective-permute-start | bytes 1572872 | tf_op jit(solution)/shard_map/ppermute | solution.py:35
  184.8 9.1 %copy-start.16 = (bf16[128,4096]{1,0:T(8,128)(2,1)}, bf16[128,4096]{1,0:T(8,128)(2,1)S(1)}, u32[]{:S(2)}) copy-start(bf16[128,4096]{1,0:T(8,128)(2,1)S(1)} %collective-permute-done.24.refs_1_) | copy-start | bytes 3145732
  184.8 15.6 %collective-permute-start.30 = (bf16[64,4096]{1,0:T(8,128)(2,1)S(1)}, bf16[64,4096]{1,0:T(8,128)(2,1)S(1)}, u32[]{:S(2)}, u32[]{:S(2)}) collective-permute-start(bf16[64,4096]{1,0:T(8,128)(2,1)S(1)} %copy-done.28), channel_id=1, source_target_pairs={{0,48},{16,0},{32,16},{48,32},{64,112},{80,64},{96,80},{112,96},{1... | collective-permute-start | bytes 1572872 | tf_op jit(solution)/shard_map/ppermute | solution.py:35
  193.9 1.0 copy-start.17
  193.9 1.4 copy-start.18
  200.3 0.8 copy-start.19
  200.3 1.0 copy-start.20
  201.3 0.8 copy-start.21
